TPU v7x, 512 devices: a whole 4x8x8 slice. The times are simulated.
512 devices in a mesh: lat: 16 (over y_hi, x), lon: 32 (over z, y_lo, core).
Axes of the slice: x: 4, y: 8 (y_hi: 4, y_lo: 2; y = y_hi * 2 + y_lo), z: 8, core: 2. Of those that a mesh axis runs over, the one named last changes fastest.
Arguments:
- tokens: bfloat16 [128, 1024, 1024], P('lat', 'lon'), may hold values from -40 to 40
- ln_gain: float32 [1024], replicated, may hold values from 0.1 to 1.9
- w_qkv: bfloat16 [1024, 1536], replicated, may hold values from -0.34375 to 0.34375
- bias_table: float32 [8, 225], replicated, may hold values from -4 to 4
- bias_index: int32 [64, 64], replicated, may hold values from 0 to 224
- cap_group: int32 [2, 256, 4, 1], P(None, 'lon'), may hold values from 0 to 31; in each aligned block of 32 rows (0 to 31, 32 to 63, ..., all dimensions but the last counted through in order) at most 2 rows name the same one
Outputs:
- mixed: bfloat16 [128, 1024, 512], P('lat', 'lon')
Inputs may be any that keep to these rules, and one draw needn't show every extreme that they name: `cap_group`: within one pole, the 32 tiles of one longitude sector name any one group at most 2 times, and some sector names some group exactly 2 times.
All inputs are finite; a program needn't handle non-finite values.
Results may differ from a plain program's by a relative error of at most 0.0079.
Values may be sent and summed in bfloat16 or wider, within the bound.
No kernel may reach another device: no remote copies, remote signals or barrier semaphores. Data moves between devices by JAX's collectives and lax.ppermute only.
A program may use at most 128 MiB of HBM per device.

v0:
```python
import jax
import jax.numpy as jnp
from jax import lax
from jax.sharding import PartitionSpec as P

D = 1024
HEADS = 8
HD = 64
WIN = 8
TW = 4
CAP = 4
RH = 8
RW = 32
HW = 512
HALF = 4
BIAS_ROWS = 225
TILES_DEV = 32


epsilon = 1e-05
masked_score = -1e30


def with_halo(block, sides, width, periodic):
    for axis, dim in sides:
        count = lax.axis_size(axis)
        forward = [(i, i + 1) for i in range(count - 1)]
        if periodic:
            forward.append((count - 1, 0))
        backward = [(target, source) for source, target in forward]
        low = lax.ppermute(
            lax.slice_in_dim(block, block.shape[dim] - width, None, axis=dim), axis, forward
        )
        high = lax.ppermute(lax.slice_in_dim(block, 0, width, axis=dim), axis, backward)
        block = jnp.concatenate([low, block, high], axis=dim)
    return block


def layer_norm(row_tokens, ln_gain):
    values = row_tokens.astype(jnp.float32)
    center = jnp.mean(values, axis=-1, keepdims=True)
    spread = jnp.mean(jnp.square(values - center), axis=-1, keepdims=True)
    return ((values - center) * lax.rsqrt(spread + epsilon) * ln_gain).astype(jnp.bfloat16)


def softmax_bf16(scores):
    highest = jnp.max(scores, axis=-1, keepdims=True)
    raised = jnp.exp(scores - highest)
    return (raised / jnp.sum(raised, axis=-1, keepdims=True)).astype(jnp.bfloat16)


def local(tokens, ln_gain, w_qkv, bias_table, bias_index, cap_group):
    lat_index = lax.axis_index("lat")
    lat_count = lax.axis_size("lat")
    lon_count = lax.axis_size("lon")
    att_scale = HD ** (-0.5)
    normed = layer_norm(tokens, ln_gain)
    projected = jnp.dot(
        normed.reshape(RH * RW, D), w_qkv, preferred_element_type=jnp.float32
    ).astype(jnp.bfloat16)
    grid_proj = projected.reshape(RH, RW, 3 * HW)
    queries = grid_proj[:, :, :HW]
    keys_values = grid_proj[:, :, HW:]
    wider = with_halo(keys_values, (("lon", 1),), HALF, True)
    extended = with_halo(wider, (("lat", 0),), HALF, False)
    is_north = lat_index == 0
    is_polar = is_north | (lat_index == lat_count - 1)
    cap_start = jnp.where(is_north, 0, RH - CAP).astype(jnp.int32)
    tile_cols = RW // TW
    group_ids = jnp.where(is_north, cap_group[0], cap_group[1]).reshape(TILES_DEV)
    most_slots = 2 * TILES_DEV // lon_count
    slot_total = lon_count * most_slots
    group_hot = (group_ids[:, None] == jnp.arange(lon_count, dtype=jnp.int32)[None, :]).astype(
        jnp.int32
    )
    earlier = jnp.cumsum(group_hot, axis=0) - group_hot
    slot_rank = jnp.sum(earlier * group_hot, axis=1)
    slot_of = group_ids * most_slots + slot_rank
    dispatch = (jnp.arange(slot_total, dtype=jnp.int32)[:, None] == slot_of[None, :]).astype(
        jnp.bfloat16
    )
    slot_valid = jnp.sum(dispatch, axis=1).reshape(lon_count, most_slots)
    channels = grid_proj.shape[-1]
    cap_rows = lax.dynamic_slice_in_dim(grid_proj, cap_start, CAP, 0)
    cap_rows = cap_rows.reshape(CAP, tile_cols, TW, channels).transpose(1, 0, 2, 3)
    packed = jnp.dot(
        dispatch, cap_rows.reshape(TILES_DEV, TW * channels), preferred_element_type=jnp.float32
    ).astype(jnp.bfloat16)
    arrived, arrived_valid = (
        lax.all_to_all(
            packed.reshape(lon_count, most_slots, TW, 3 * HW),
            "lon",
            split_axis=0,
            concat_axis=0,
            tiled=True,
        ),
        lax.all_to_all(slot_valid, "lon", split_axis=0, concat_axis=0, tiled=True),
    )
    slot_proj = arrived.reshape(-1, 3 * HW)
    token_valid = jnp.broadcast_to(arrived_valid.reshape(-1, 1), (slot_total, TW)).reshape(-1) > 0.5
    cap_q = slot_proj[:, :HW].reshape(-1, HEADS, HD)
    cap_k = slot_proj[:, HW : 2 * HW].reshape(-1, HEADS, HD)
    cap_v = slot_proj[:, 2 * HW :].reshape(-1, HEADS, HD)
    cap_scores = (
        jnp.einsum("qhd,khd->hqk", cap_q, cap_k, preferred_element_type=jnp.float32) * att_scale
    )
    cap_scores = jnp.where(token_valid[None, None, :], cap_scores, masked_score)
    cap_weights = softmax_bf16(cap_scores)
    cap_result = jnp.einsum(
        "hqk,khd->qhd", cap_weights, cap_v, preferred_element_type=jnp.float32
    ).astype(jnp.bfloat16)
    returned = lax.all_to_all(
        cap_result.reshape(lon_count, most_slots, TW, HW),
        "lon",
        split_axis=0,
        concat_axis=0,
        tiled=True,
    )
    position_hot = (
        bias_index[:, :, None] == jnp.arange(BIAS_ROWS, dtype=jnp.int32)[None, None, :]
    ).astype(jnp.float32)
    position_bias = jnp.einsum(
        "pqt,ht->hpq", position_hot, bias_table, precision=lax.Precision.HIGHEST
    )
    ext_rows = RH + WIN
    ext_cols = RW + WIN
    win_rows = ext_rows // WIN
    win_cols = ext_cols // WIN
    padded_q = jnp.pad(queries, ((HALF, HALF), (HALF, HALF), (0, 0)))
    grid_q = padded_q.reshape(win_rows, WIN, win_cols, WIN, HEADS, HD)
    grid_k = extended[:, :, :HW].reshape(win_rows, WIN, win_cols, WIN, HEADS, HD)
    grid_v = extended[:, :, HW:].reshape(win_rows, WIN, win_cols, WIN, HEADS, HD)
    global_row = lat_index * RH - HALF + jnp.arange(ext_rows, dtype=jnp.int32)
    row_valid = (global_row >= 0) & (global_row < RH * lat_count)
    key_valid = jnp.broadcast_to(row_valid.reshape(win_rows, WIN, 1), (win_rows, WIN, WIN)).reshape(
        win_rows, 1, 1, 1, WIN * WIN
    )
    scores = jnp.einsum(
        "aibjhd,akblhd->abhijkl", grid_q, grid_k, preferred_element_type=jnp.float32
    )
    scores = (
        scores.reshape(win_rows, win_cols, HEADS, WIN * WIN, WIN * WIN) * att_scale
        + position_bias[None, None]
    )
    scores = jnp.where(key_valid, scores, masked_score)
    weights = softmax_bf16(scores).reshape(win_rows, win_cols, HEADS, WIN, WIN, WIN, WIN)
    win_out = jnp.einsum(
        "abhijkl,akblhd->aibjhd", weights, grid_v, preferred_element_type=jnp.float32
    )
    win_grid = win_out.reshape(ext_rows, ext_cols, HW)[HALF : HALF + RH, HALF : HALF + RW]
    tile_out = jnp.dot(
        dispatch.T, returned.reshape(slot_total, TW * HW), preferred_element_type=jnp.float32
    )
    cap_rows = tile_out.reshape(tile_cols, CAP, TW, HW).transpose(1, 0, 2, 3).reshape(CAP, RW, HW)
    cap_rows = jnp.where(is_polar, cap_rows, 0.0)
    cap_grid = lax.dynamic_update_slice_in_dim(
        jnp.zeros((RH, RW, HW), jnp.float32), cap_rows, cap_start, 0
    )
    return (win_grid + cap_grid).astype(jnp.bfloat16)


def solution(mesh):
    placed = (P("lat", "lon", None), P(), P(), P(), P(), P(None, "lon", None, None))
    return jax.shard_map(
        local, mesh=mesh, in_specs=placed, out_specs=P("lat", "lon", None), check_vma=False
    )
```

profile of v0, /device:TPU:41, one launch (start us, length us, event | category | flops | bytes accessed | tf_op | source)
XLA Modules:
  0.0 162.2 jit_solution(6435841221841551102)
XLA Ops:
  2.7 12.2 %all-to-all-start.1 = ((bf16[32,1,2]{2,1,0:T(2,128)(2,1)}), bf16[32,1,2]{2,1,0:T(2,128)(2,1)S(1)}, u32[]{:S(2)}, u32[]{:S(2)}) async-start(bf16[32,1,2]{2,1,0:T(2,128)(2,1)} %all_to_all.16), calls=%async_computation.1 | async-start | bytes 32768 | tf_op jit(solution)/shard_map/all_to_all | solution.py:97
  20.6 3.4 %collective-permute-start = (bf16[8,4,1024]{2,1,0:T(4,128)(2,1)}, bf16[8,4,1024]{2,1,0:T(4,128)(2,1)S(1)}, u32[]{:S(2)}, u32[]{:S(2)}) collective-permute-start(bf16[8,4,1024]{2,1,0:T(4,128)(2,1)} %get-tuple-element.10), channel_id=1, source_target_pairs={{0,1},{1,2},{2,3},{3,4},{4,5},{5,6},{6,7},{7,8},{8,9},{9,10},{10,1... | collective-permute-start | bytes 196616 | tf_op jit(solution)/shard_map/ppermute | solution.py:31
  24.0 1.9 %collective-permute-start.1 = (bf16[8,4,1024]{2,1,0:T(4,128)(2,1)}, bf16[8,4,1024]{2,1,0:T(4,128)(2,1)S(1)}, u32[]{:S(2)}, u32[]{:S(2)}) collective-permute-start(bf16[8,4,1024]{2,1,0:T(4,128)(2,1)} %get-tuple-element.11), channel_id=1, source_target_pairs={{1,0},{2,1},{3,2},{4,3},{5,4},{6,5},{7,6},{8,7},{9,8},{10,9},{11,1... | collective-permute-start | bytes 196616 | tf_op jit(solution)/shard_map/ppermute | solution.py:34
  29.8 3.0 %reshape.188 = bf16[32,2,4,1536]{3,2,1,0:T(4,128)(2,1)} reshape(bf16[64,6144]{1,0:T(8,128)(2,1)} %convolution_convert_fusion) | data formatting | bytes 1572864 | tf_op jit(solution)/shard_map/reshape | solution.py:91
  32.8 4.2 %fusion.16 = f32[8,64,64]{2,0,1:T(8,128)} fusion(s32[64,64]{1,0:T(8,128)} %param.10, f32[8,225]{1,0:T(8,128)} %param.9), kind=kOutput, calls=%fused_computation.30 | convolution fusion | flops 89395200 | bytes 154656 | tf_op jit(solution)/shard_map/pqt,ht->hpq/dot_general | solution.py:122
  39.7 3.1 %collective-permute-start.2 = (bf16[4,40,1024]{2,1,0:T(8,128)(2,1)}, bf16[4,40,1024]{2,1,0:T(8,128)(2,1)}, u32[]{:S(2)}, u32[]{:S(2)}) collective-permute-start(bf16[4,40,1024]{2,1,0:T(8,128)(2,1)} %get-tuple-element.12), channel_id=1, source_target_pairs={{0,32},{32,64},{64,96},{96,128},{128,160},{160,192},{192,224},{224... | collective-permute-start | bytes 983048 | tf_op jit(solution)/shard_map/ppermute | solution.py:31
  42.8 6.4 %collective-permute-start.3 = (bf16[4,40,1024]{2,1,0:T(8,128)(2,1)}, bf16[4,40,1024]{2,1,0:T(8,128)(2,1)}, u32[]{:S(2)}, u32[]{:S(2)}) collective-permute-start(bf16[4,40,1024]{2,1,0:T(8,128)(2,1)} %get-tuple-element.13), channel_id=1, source_target_pairs={{32,0},{64,32},{96,64},{128,96},{160,128},{192,160},{224,192},{256... | collective-permute-start | bytes 983048 | tf_op jit(solution)/shard_map/ppermute | solution.py:34
  50.8 2.6 %reshape.183 = bf16[2,8,5,8,8,64]{5,4,3,2,1,0:T(8,128)(2,1)} reshape(bf16[16,40,512]{2,1,0:T(8,128)(2,1)} %pad.4) | data formatting | bytes 1310720 | tf_op jit(solution)/shard_map/reshape | solution.py:130
  53.4 2.8 %add.58 = f32[8,8,8,8,8]{4,3,0,2,1:T(8,128)} reshape(f32[8,64,64]{2,0,1:T(8,128)} %fusion.16) | data formatting | bytes 262144 | tf_op jit(solution)/shard_map/add | solution.py:142
  56.2 3.2 %copy.69 = f32[8,8,8,8,8]{2,4,3,1,0:T(8,128)} copy(f32[8,8,8,8,8]{4,3,0,2,1:T(8,128)} %add.58) | data formatting | bytes 262144 | tf_op jit(solution)/shard_map/add | solution.py:142
  59.5 10.4 %all-to-all-start = ((bf16[32,2,4,1536]{3,2,1,0:T(4,128)(2,1)}), bf16[32,2,4,1536]{3,2,1,0:T(4,128)(2,1)}, u32[]{:S(2)}, u32[]{:S(2)}) async-start(bf16[32,2,4,1536]{3,2,1,0:T(4,128)(2,1)} %reshape.188), calls=%async_computation | async-start | bytes 1572864 | tf_op jit(solution)/shard_map/all_to_all | solution.py:90
  70.2 1.5 pad_maximum_fusion
  72.9 2.6 %reshape.182 = bf16[2,8,5,8,8,64]{5,4,3,2,1,0:T(8,128)(2,1)} reshape(bf16[16,40,512]{2,1,0:T(8,128)(2,1)} %get-tuple-element.5) | data formatting | bytes 1310720 | tf_op jit(solution)/shard_map/reshape | solution.py:132
  75.5 2.6 %reshape.184 = bf16[2,8,5,8,8,64]{5,4,3,2,1,0:T(8,128)(2,1)} reshape(bf16[16,40,512]{2,1,0:T(8,128)(2,1)} %get-tuple-element.6) | data formatting | bytes 1310720 | tf_op jit(solution)/shard_map/reshape | solution.py:131
  78.2 20.6 %fusion.2 = (f32[2,5,8,8,8]{4,3,2,1,0:T(8,128)S(1)}, f32[2,5,8,8,8,8,8]{4,6,5,3,2,1,0:T(8,128)}) fusion(f32[8,8,8,8,8]{2,4,3,1,0:T(8,128)} %copy.69, pred[2,8]{1,0:T(4,128)(4,1)S(1)} %copy-done.4, bf16[2,8,5,8,8,64,1]{5,4,3,2,1,0,6:T(8,128)(2,1)} %bitcast.63, bf16[2,8,5,8,8,64,1]{5,4,3,2,1,0,6:T(8,128)(2,1)} %bitcast.62), kind=kOutput, calls=%fused_computation.5 | convolution fusion | flops 43248640 | bytes 2773008 | tf_op jit(solution)/shard_map/aibjhd,akblhd->abhijkl/dot_general | solution.py:138
  98.8 11.8 %fusion.1 = f32[2,5,8,8,8]{4,3,2,1,0:T(8,128)} fusion(f32[2,5,8,8,8,8,8]{4,6,5,3,2,1,0:T(8,128)} %get-tuple-element.15, f32[2,5,8,8,8]{4,3,2,1,0:T(8,128)S(1)} %get-tuple-element.14, f32[8,8,8,8,8]{2,4,3,1,0:T(8,128)S(1)} %copy-done.1, pred[2,8]{1,0:T(4,128)(4,1)S(1)} %copy-done.4), kind=kLoop, calls=%fused_computation.4 | loop fusion | flops 1633280 | bytes 1482768 | tf_op jit(solution)/shard_map/reduce_sum | solution.py:49
  110.6 2.3 %reshape.189 = bf16[256,1536]{1,0:T(8,128)(2,1)} reshape(bf16[32,2,4,1536]{3,2,1,0:T(4,128)(2,1)} %all-to-all-done) | data formatting | bytes 1572864 | tf_op jit(solution)/shard_map/reshape | solution.py:99
  112.9 2.0 %fusion.38 = (bf16[256,512]{1,0:T(8,128)(2,1)}, bf16[256,512]{1,0:T(8,128)(2,1)}, bf16[256,512]{1,0:T(8,128)(2,1)}) fusion(bf16[256,1536]{1,0:T(8,128)(2,1)} %reshape.189), kind=kLoop, calls=%fused_computation.65 | loop fusion | bytes 1572864 | tf_op jit(solution)/shard_map/slice | solution.py:102
  114.9 1.8 %copy.104 = bf16[256,512]{0,1:T(8,128)(2,1)} copy(bf16[256,512]{1,0:T(8,128)(2,1)} %get-tuple-element.7) | data formatting | bytes 524288
  116.7 1.8 %copy.103 = bf16[256,512]{0,1:T(8,128)(2,1)} copy(bf16[256,512]{1,0:T(8,128)(2,1)} %get-tuple-element.8) | data formatting | bytes 524288
  118.5 1.8 %copy.102 = bf16[256,512]{0,1:T(8,128)(2,1)} copy(bf16[256,512]{1,0:T(8,128)(2,1)} %get-tuple-element.9) | data formatting | bytes 524288
  120.3 3.2 %fusion.41 = (f32[8,256]{1,0:T(8,128)S(1)}, f32[8,256,256]{1,2,0:T(8,128)}) fusion(pred[256]{0:T(512)(128)(4,1)S(1)} %gt.20, bf16[256,8,64]{0,2,1:T(8,128)(2,1)} %bitcast.75, bf16[256,8,64]{0,2,1:T(8,128)(2,1)} %bitcast.74), kind=kOutput, calls=%fused_computation.68 | convolution fusion | flops 69206272 | bytes 2629888 | tf_op jit(solution)/shard_map/sub | solution.py:48
  123.5 2.7 %fusion.15 = bf16[256,8,64]{0,2,1:T(8,128)(2,1)} fusion(bf16[256,8,64]{0,2,1:T(8,128)(2,1)} %bitcast.76, f32[8,256,256]{1,2,0:T(8,128)} %get-tuple-element.17, f32[8,256]{1,0:T(8,128)S(1)} %get-tuple-element.16), kind=kOutput, calls=%fused_computation.29 | convolution fusion | flops 68288512 | bytes 2629632 | tf_op jit(solution)/shard_map/hqk,khd->qhd/dot_general | solution.py:109
  126.2 2.0 %copy.81 = bf16[256,8,64]{2,1,0:T(8,128)(2,1)} copy(bf16[256,8,64]{0,2,1:T(8,128)(2,1)} %fusion.15) | data formatting | bytes 524288 | tf_op jit(solution)/shard_map/convert_element_type | solution.py:111
  128.3 2.1 %reshape.193 = bf16[32,2,4,512]{3,2,1,0:T(4,128)(2,1)} reshape(bf16[256,8,64]{2,1,0:T(8,128)(2,1)} %copy.81) | data formatting | bytes 524288 | tf_op jit(solution)/shard_map/reshape | solution.py:113
  130.3 8.3 %all-to-all-start.2 = ((bf16[32,2,4,512]{3,2,1,0:T(4,128)(2,1)}), bf16[32,2,4,512]{3,2,1,0:T(4,128)(2,1)}, u32[]{:S(2)}, u32[]{:S(2)}) async-start(bf16[32,2,4,512]{3,2,1,0:T(4,128)(2,1)} %reshape.193), calls=%async_computation.2 | async-start | bytes 524288 | tf_op jit(solution)/shard_map/all_to_all | solution.py:112
  138.7 10.8 %fusion.7 = f32[2,8,5,8,8,64]{5,3,1,4,2,0:T(8,128)S(1)} fusion(f32[2,5,8,8,8,8,8]{4,6,5,3,2,1,0:T(8,128)} %get-tuple-element.15, f32[2,5,8,8,8]{4,3,2,1,0:T(8,128)} %fusion.1, f32[2,5,8,8,8]{4,3,2,1,0:T(8,128)S(1)} %get-tuple-element.14, f32[8,8,8,8,8]{2,4,3,1,0:T(8,128)} %copy.69, pred[2,8]{1,0:T(4,128)(4,1)S(1)} %copy-done.4, ...), kind=kOutput, calls=%fused_computation.16 | convolution fusion | flops 43909120 | bytes 3448848 | tf_op jit(solution)/shard_map/abhijkl,akblhd->aibjhd/dot_general | solution.py:147
  149.5 3.0 %copy.72 = f32[2,8,5,8,8,64]{5,4,3,2,1,0:T(8,128)} copy(f32[2,8,5,8,8,64]{5,3,1,4,2,0:T(8,128)S(1)} %fusion.7) | data formatting | bytes 2621440 | tf_op jit(solution)/shard_map/abhijkl,akblhd->aibjhd/transpose | solution.py:147
  152.5 2.9 %reshape.185 = f32[16,40,512]{2,1,0:T(8,128)} reshape(f32[2,8,5,8,8,64]{5,4,3,2,1,0:T(8,128)} %copy.72) | data formatting | bytes 2621440 | tf_op jit(solution)/shard_map/reshape | solution.py:150
  155.4 1.9 %slice.69 = f32[8,32,512]{2,1,0:T(8,128)} slice(f32[16,40,512]{2,1,0:T(8,128)} %reshape.185), slice={[4:12], [4:36], [0:512]} | slice | bytes 1048576 | tf_op jit(solution)/shard_map/slice | solution.py:150
  158.7 1.8 %fusion.24 = f32[8,32,512]{2,1,0:T(8,128)} fusion(f32[8,32,512]{2,1,0:T(8,128)} %slice.69, s32[]{:T(128)S(6)} %select_n.54, f32[4,32,512]{2,0,1:T(4,128)S(1)} %bitcast.72), kind=kLoop, calls=%fused_computation.41 | loop fusion | flops 65536 | bytes 786436 | tf_op jit(solution)/shard_map/add | solution.py:159
  160.4 1.8 %convert_element_type.49 = bf16[8,32,512]{2,1,0:T(8,128)(2,1)} convert(f32[8,32,512]{2,1,0:T(8,128)} %fusion.24) | non-fusion elementwise | flops 131072 | bytes 786432 | tf_op jit(solution)/shard_map/convert_element_type | solution.py:159
  (58 shorter events, 19.3 us)
Async XLA Ops:
  0.0 18.8 %copy-start = (bf16[1024,1536]{1,0:T(8,128)(2,1)S(1)}, bf16[1024,1536]{1,0:T(8,128)(2,1)}, u32[]{:S(2)}) copy-start(bf16[1024,1536]{1,0:T(8,128)(2,1)} %param.8) | copy-start | bytes 9437188
  1.3 0.5 copy-start.5
  2.7 56.7 %all-to-all-start.1 = ((bf16[32,1,2]{2,1,0:T(2,128)(2,1)}), bf16[32,1,2]{2,1,0:T(2,128)(2,1)S(1)}, u32[]{:S(2)}, u32[]{:S(2)}) async-start(bf16[32,1,2]{2,1,0:T(2,128)(2,1)} %all_to_all.16), calls=%async_computation.1 | async-start | bytes 32768 | tf_op jit(solution)/shard_map/all_to_all | solution.py:97
  19.8 6.1 %copy-start.2 = (bf16[256,1536]{1,0:T(8,128)(2,1)}, bf16[256,1536]{1,0:T(8,128)(2,1)S(1)}, u32[]{:S(2)}) copy-start(bf16[256,1536]{1,0:T(8,128)(2,1)S(1)} %convolution_convert_fusion.1) | copy-start | bytes 2359300
  20.6 16.9 %collective-permute-start = (bf16[8,4,1024]{2,1,0:T(4,128)(2,1)}, bf16[8,4,1024]{2,1,0:T(4,128)(2,1)S(1)}, u32[]{:S(2)}, u32[]{:S(2)}) collective-permute-start(bf16[8,4,1024]{2,1,0:T(4,128)(2,1)} %get-tuple-element.10), channel_id=1, source_target_pairs={{0,1},{1,2},{2,3},{3,4},{4,5},{5,6},{6,7},{7,8},{8,9},{9,10},{10,1... | collective-permute-start | bytes 196616 | tf_op jit(solution)/shard_map/ppermute | solution.py:31
  24.0 13.6 %collective-permute-start.1 = (bf16[8,4,1024]{2,1,0:T(4,128)(2,1)}, bf16[8,4,1024]{2,1,0:T(4,128)(2,1)S(1)}, u32[]{:S(2)}, u32[]{:S(2)}) collective-permute-start(bf16[8,4,1024]{2,1,0:T(4,128)(2,1)} %get-tuple-element.11), channel_id=1, source_target_pairs={{1,0},{2,1},{3,2},{4,3},{5,4},{6,5},{7,6},{8,7},{9,8},{10,9},{11,1... | collective-permute-start | bytes 196616 | tf_op jit(solution)/shard_map/ppermute | solution.py:34
  26.8 1.6 copy-start.6
  32.8 16.4 %copy-start.7 = (s32[32]{0:T(128)S(1)}, s32[32]{0:T(128)}, u32[]{:S(2)}) copy-start(s32[32]{0:T(128)} %copy-done.5) | copy-start | bytes 388
  39.7 30.5 %collective-permute-start.2 = (bf16[4,40,1024]{2,1,0:T(8,128)(2,1)}, bf16[4,40,1024]{2,1,0:T(8,128)(2,1)}, u32[]{:S(2)}, u32[]{:S(2)}) collective-permute-start(bf16[4,40,1024]{2,1,0:T(8,128)(2,1)} %get-tuple-element.12), channel_id=1, source_target_pairs={{0,32},{32,64},{64,96},{96,128},{128,160},{160,192},{192,224},{224... | collective-permute-start | bytes 983048 | tf_op jit(solution)/shard_map/ppermute | solution.py:31
  42.8 27.4 %collective-permute-start.3 = (bf16[4,40,1024]{2,1,0:T(8,128)(2,1)}, bf16[4,40,1024]{2,1,0:T(8,128)(2,1)}, u32[]{:S(2)}, u32[]{:S(2)}) collective-permute-start(bf16[4,40,1024]{2,1,0:T(8,128)(2,1)} %get-tuple-element.13), channel_id=1, source_target_pairs={{32,0},{64,32},{96,64},{128,96},{160,128},{192,160},{224,192},{256... | collective-permute-start | bytes 983048 | tf_op jit(solution)/shard_map/ppermute | solution.py:34
  59.5 51.2 %all-to-all-start = ((bf16[32,2,4,1536]{3,2,1,0:T(4,128)(2,1)}), bf16[32,2,4,1536]{3,2,1,0:T(4,128)(2,1)}, u32[]{:S(2)}, u32[]{:S(2)}) async-start(bf16[32,2,4,1536]{3,2,1,0:T(4,128)(2,1)} %reshape.188), calls=%async_computation | async-start | bytes 1572864 | tf_op jit(solution)/shard_map/all_to_all | solution.py:90
  72.9 5.3 %copy-start.4 = (pred[2,8]{1,0:T(4,128)(4,1)S(1)}, pred[2,8]{1,0:T(4,128)(4,1)}, u32[]{:S(2)}) copy-start(pred[2,8]{1,0:T(4,128)(4,1)} %compare_and_fusion) | copy-start | bytes 52
  78.2 20.6 %copy-start.1 = (f32[8,8,8,8,8]{2,4,3,1,0:T(8,128)S(1)}, f32[8,8,8,8,8]{2,4,3,1,0:T(8,128)}, u32[]{:S(2)}) copy-start(f32[8,8,8,8,8]{2,4,3,1,0:T(8,128)} %copy.69) | copy-start | bytes 393220
  130.3 27.0 %all-to-all-start.2 = ((bf16[32,2,4,512]{3,2,1,0:T(4,128)(2,1)}), bf16[32,2,4,512]{3,2,1,0:T(4,128)(2,1)}, u32[]{:S(2)}, u32[]{:S(2)}) async-start(bf16[32,2,4,512]{3,2,1,0:T(4,128)(2,1)} %reshape.193), calls=%async_computation.2 | async-start | bytes 524288 | tf_op jit(solution)/shard_map/all_to_all | solution.py:112
  152.5 4.8 %copy-start.3 = (pred[32,64]{1,0:T(8,128)(4,1)S(1)}, pred[32,64]{1,0:T(8,128)(4,1)}, u32[]{:S(2)}) copy-start(pred[32,64]{1,0:T(8,128)(4,1)} %iota_compare_fusion.7) | copy-start | bytes 6148
where the time goes:
time: 164 us; the launch traced here: 162 us
  local copies, waits for them, and re-layouts  46.7 us (28%)
  starting transfers between devices  45.7 us (28%)
  matrix products  45 us (27%)
  other arithmetic  24.5 us (15%)
    dot_general x1, matrix products, local(): jnp.einsum('aibjhd,akblhd->abhijkl', grid_q, grid_k, preferred_element_ty...  20.6 us
    all_to_all x1, starting transfers between devices, local(): lax.all_to_all(slot_valid, 'lon', split_axis=0, concat_axis=0, tiled=True)  12.2 us
    reduce_sum x1, other arithmetic, softmax_bf16(): jnp.sum(raised, axis=-1, keepdims=True)  11.8 us
    dot_general x1, matrix products, local(): jnp.einsum('abhijkl,akblhd->aibjhd', weights, grid_v, preferred_element_t...  10.8 us
    all_to_all x1, starting transfers between devices, local(): lax.all_to_all(packed.reshape(lon_count, most_slots, TW, 3 * HW), 'lon',...  10.4 us
    all_to_all x1, starting transfers between devices, local(): lax.all_to_all(cap_result.reshape(lon_count, most_slots, TW, HW), 'lon',...  8.34 us
    ppermute x2, starting transfers between devices, with_halo(): lax.ppermute(lax.slice_in_dim(block, 0, width, axis=dim), axis, backward)  8.29 us
    ppermute x2, starting transfers between devices, with_halo(): lax.ppermute(lax.slice_in_dim(block, block.shape[dim] - width, None, axis...  6.48 us
  transfers between devices with their start and end apart: 7, of which 0 were waited for; matrix products, arithmetic and copies ran while one was open for 55% of the time, Pallas kernels for 0%

commit v1 on v0

v1 whole, which is shorter than its diff:
```python
import functools

import jax
import jax.numpy as jnp
from jax import lax
from jax.experimental import pallas as pl
from jax.experimental.pallas import tpu as pltpu
from jax.sharding import PartitionSpec as P

D = 1024
HEADS = 8
HD = 64
WIN = 8
TW = 4
CAP = 4
RH = 8
RW = 32
HW = 512
HALF = 4
BIAS_ROWS = 225
TILES_DEV = 32
GROUPS = 32
MOST = 2
SLOT_TOKENS = GROUPS * MOST * TW
CAP_TOKENS = CAP * RW
N_WIN = 10
WIN_B = 5
WTOK = WIN * WIN
QROWS = HALF * WIN

epsilon = 1e-05
masked_score = -1e30
EMPTY = 128.0
EMPTY_ABOVE = 64.0

VMEM = pltpu.VMEM
SMEM = pltpu.SMEM


def vspec():
    return pl.BlockSpec(memory_space=VMEM)


def sspec():
    return pl.BlockSpec(memory_space=SMEM)


def aspec():
    return pl.BlockSpec(memory_space=pl.ANY)


def norm_rows(values, gain):
    center = jnp.mean(values, axis=-1, keepdims=True)
    shifted = values - center
    spread = jnp.mean(jnp.square(shifted), axis=-1, keepdims=True)
    return shifted * lax.rsqrt(spread + epsilon) * gain


def slot_rows(group_ref, pole, lane):
    row = lane // RW
    col = lane % RW
    tile = (col // TW) * CAP + row
    group = jnp.zeros_like(lane)
    for t in range(TILES_DEV):
        group = jnp.where(tile == t, group_ref[pole, t], group)
    rank = jnp.zeros_like(lane)
    for t in range(TILES_DEV):
        same = (group == group_ref[pole, t]) & (tile > t)
        rank = rank + same.astype(jnp.int32)
    return (group * MOST + rank) * TW + col % TW


def pack_kernel(group_ref, tokens_ref, send_ref, rows, sem):
    north = lax.axis_index("lat") == 0
    pole = jnp.where(north, 0, 1)
    start = jnp.where(north, 0, RH - CAP)
    copy = pltpu.make_async_copy(tokens_ref.at[pl.ds(start, CAP)], rows, sem)
    copy.start()
    lane = lax.broadcasted_iota(jnp.int32, (8, CAP_TOKENS), 1)
    slot = slot_rows(group_ref, pole, lane)[0:1]
    copy.wait()
    x = rows[...].reshape(CAP_TOKENS, D)
    step = 64
    for i in range(0, SLOT_TOKENS, step):
        hit = lax.broadcasted_iota(jnp.int32, (step, CAP_TOKENS), 0) + i == slot
        hot = hit.astype(jnp.float32)
        filled = jnp.max(hot, axis=1, keepdims=True) > 0.5
        moved = jnp.dot(hot.astype(jnp.bfloat16), x, preferred_element_type=jnp.float32)
        send_ref[i : i + step, :] = jnp.where(filled, moved, EMPTY).astype(jnp.bfloat16)


def edge_kernel(group_ref, own_ref, north_ref, south_ref, left_ref, right_ref, undo_ref):
    lower = lax.broadcasted_iota(jnp.int32, (8, D), 0) < HALF

    def two(ref, i, base):
        first = [ref[i, 0:8].astype(jnp.float32), ref[i + 1, 0:8].astype(jnp.float32)]
        last = [ref[i, 24:32].astype(jnp.float32), ref[i + 1, 24:32].astype(jnp.float32)]
        head = jnp.where(lower, first[0], pltpu.roll(first[1], HALF, 0))
        tail = jnp.where(lower, pltpu.roll(last[0], HALF, 0), last[1])
        return head, tail

    pairs = [(north_ref, 0), (north_ref, 2)]
    pairs += [(own_ref, i) for i in range(0, RH, 2)]
    pairs += [(south_ref, 0), (south_ref, 2)]
    for n in range(0, len(pairs), 2):
        heads, tails = zip(*[two(ref, i, 0) for ref, i in pairs[n : n + 2]])
        left_ref[n * 8 : n * 8 + 16] = jnp.concatenate(heads, 0).astype(jnp.bfloat16)
        right_ref[n * 8 : n * 8 + 16] = jnp.concatenate(tails, 0).astype(jnp.bfloat16)

    lat = lax.axis_index("lat")
    north = lat == 0
    polar = north | (lat == lax.axis_size("lat") - 1)
    pole = jnp.where(north, 0, 1)
    token = lax.broadcasted_iota(jnp.int32, (CAP_TOKENS, 128), 0)
    slot = slot_rows(group_ref, pole, token)
    slot = jnp.where(polar, slot, -1)
    for i in range(0, SLOT_TOKENS, 128):
        hit = lax.broadcasted_iota(jnp.int32, (CAP_TOKENS, 128), 1) + i == slot
        undo_ref[:, i : i + 128] = hit.astype(jnp.float32).astype(jnp.bfloat16)


def cap_kernel(x_ref, gain_ref, w_ref, out_ref, normed, qkv, w, sem):
    n = SLOT_TOKENS
    copy = pltpu.make_async_copy(w_ref, w, sem)
    copy.start()
    gain = gain_ref[...]
    for i in range(0, n, 32):
        normed[i : i + 32] = norm_rows(x_ref[i : i + 32].astype(jnp.float32), gain).astype(jnp.bfloat16)
    pick = (lax.broadcasted_iota(jnp.int32, (8, 128), 1) == 0).astype(jnp.bfloat16)
    first = lax.dot_general(
        pick, x_ref[:, 0:128], (((1,), (1,)), ((), ())), preferred_element_type=jnp.float32
    )
    empty = jnp.where(first[0:1] > EMPTY_ABOVE, masked_score, 0.0)
    copy.wait()
    for j in range(0, 3 * HW, 256):
        part = jnp.dot(normed[...], w[:, j : j + 256], preferred_element_type=jnp.float32)
        qkv[:, j : j + 256] = part.astype(jnp.bfloat16)
    low = lax.broadcasted_iota(jnp.int32, (n, 128), 1) < HD
    for pair in range(HEADS // 2):
        at = pair * 128
        q = qkv[:, at : at + 128] * jnp.bfloat16(HD ** (-0.5))
        k = qkv[:, HW + at : HW + at + 128]
        v = qkv[:, 2 * HW + at : 2 * HW + at + 128]
        mixed = []
        for half in range(2):
            mine = low if half == 0 else jnp.logical_not(low)
            qh = jnp.where(mine, q, jnp.zeros_like(q))
            s = lax.dot_general(qh, k, (((1,), (1,)), ((), ())), preferred_element_type=jnp.float32)
            s = s + empty
            raised = jnp.exp(s - jnp.max(s, axis=-1, keepdims=True))
            weights = (raised * (1.0 / jnp.sum(raised, axis=-1, keepdims=True))).astype(jnp.bfloat16)
            mixed.append(jnp.dot(weights, v, preferred_element_type=jnp.float32))
        out_ref[:, at : at + 128] = jnp.where(low, mixed[0], mixed[1]).astype(jnp.bfloat16)


def window_kernel(
    own_ref, north_ref, south_ref, left_ref, right_ref, gain_ref, table_ref, index_ref, w_ref,
    out_ref, xs, xq, kv, qs, bias, scores, weights, wout, edges, w, sem,
):
    copy = pltpu.make_async_copy(w_ref, w, sem)
    copy.start()
    lat = lax.axis_index("lat")
    gain = gain_ref[...]

    lane = lax.broadcasted_iota(jnp.int32, (8, 128), 1)
    first = lane < WTOK
    key_row = (lane % WTOK) // WIN
    off_north = (lat == 0) & (key_row < HALF)
    off_south = (lat == lax.axis_size("lat") - 1) & (key_row >= HALF)
    tables = []
    for h in range(HEADS):
        tables.append([jnp.broadcast_to(table_ref[h : h + 1, c : c + 128], (8, 128)) for c in (0, 128)])
    for a in range(2):
        off = off_north if a == 0 else off_south
        for i in range(0, QROWS, 8):
            at = (QROWS if a == 0 else 0) + i
            idx = index_ref[at : at + 8, :]
            inner = idx & 127
            high = idx >= 128
            for h4 in range(4):
                found = []
                for h in (h4, h4 + 4):
                    lo = jnp.take_along_axis(tables[h][0], inner, axis=1)
                    hi = jnp.take_along_axis(tables[h][1], inner, axis=1)
                    found.append(jnp.where(high, hi, lo))
                value = jnp.where(first, found[0], found[1])
                to = a * 128 + h4 * QROWS + i
                bias[to : to + 8, :] = jnp.where(off, masked_score, value)

    for side, ref in enumerate((left_ref, right_ref)):
        for i in range(0, 64, 32):
            edges[side, i : i + 32] = norm_rows(ref[i : i + 32].astype(jnp.float32), gain)
    lower = lax.broadcasted_iota(jnp.int32, (8, D), 0) < HALF
    rows = [(north_ref, i) for i in range(HALF)] + [(own_ref, i) for i in range(RH)]
    rows += [(south_ref, i) for i in range(HALF)]
    for r in range(0, RH + WIN, 2):
        blocks = [[], []]
        for k in range(2):
            ref, i = rows[r + k]
            normed = norm_rows(ref[i].astype(jnp.float32), gain)
            turned = [pltpu.roll(normed[j * 8 : j * 8 + 8], HALF, 0) for j in range(4)]
            lo = edges[0, r * 4 : r * 4 + 8]
            hi = edges[1, r * 4 : r * 4 + 8]
            if k == 0:
                hi = pltpu.roll(hi, HALF, 0)
            else:
                lo = pltpu.roll(lo, HALF, 0)
            seq = [lo] + turned + [hi]
            blocks[k] = [jnp.where(lower, seq[b], seq[b + 1]) for b in range(WIN_B)]
        a, wr = r // WIN, r % WIN
        for b in range(WIN_B):
            both = jnp.concatenate([blocks[0][b], blocks[1][b]], 0).astype(jnp.bfloat16)
            to = (a * WIN_B + b) * WTOK + wr * WIN
            xs[to : to + 16] = both
            if (wr >= HALF) == (a == 0):
                to = (a * WIN_B + b) * QROWS + (wr % HALF) * WIN
                xq[to : to + 16] = both
    copy.wait()

    for j in range(0, HW, 256):
        part = jnp.dot(xq[...], w[:, j : j + 256], preferred_element_type=jnp.float32)
        qs[:, j : j + 256] = part.astype(jnp.bfloat16)
    for j in range(0, 2 * HW, 256):
        part = jnp.dot(xs[...], w[:, HW + j : HW + j + 256], preferred_element_type=jnp.float32)
        kv[:, j : j + 256] = part.astype(jnp.bfloat16)

    head = lax.broadcasted_iota(jnp.int32, (QROWS, HW), 1) // HD % 4
    blank = jnp.zeros((WTOK, HW // 2), jnp.bfloat16)

    def two_groups(x):
        top = jnp.concatenate([x[:, : HW // 2], blank], 1)
        low = jnp.concatenate([blank, x[:, HW // 2 :]], 1)
        return jnp.concatenate([top, low], 0)

    for n in range(N_WIN):
        q = qs[n * QROWS : n * QROWS + QROWS] * jnp.bfloat16(HD ** (-0.5))
        spread = jnp.concatenate([jnp.where(head == h, q, jnp.zeros_like(q)) for h in range(4)], 0)
        k = two_groups(kv[n * WTOK : n * WTOK + WTOK, 0:HW])
        s = lax.dot_general(spread, k, (((1,), (1,)), ((), ())), preferred_element_type=jnp.float32)
        a = n // WIN_B
        scores[n * 128 : n * 128 + 128] = s + bias[a * 128 : a * 128 + 128]
    left = lax.broadcasted_iota(jnp.int32, (128, 128), 1) < WTOK
    for n in range(N_WIN):
        s = scores[n * 128 : n * 128 + 128]
        top0 = jnp.max(jnp.where(left, s, -jnp.inf), axis=-1, keepdims=True)
        top1 = jnp.max(jnp.where(left, -jnp.inf, s), axis=-1, keepdims=True)
        raised = jnp.exp(s - jnp.where(left, top0, top1))
        sum0 = jnp.sum(jnp.where(left, raised, 0.0), axis=-1, keepdims=True)
        sum1 = jnp.sum(jnp.where(left, 0.0, raised), axis=-1, keepdims=True)
        share = jnp.where(left, 1.0 / sum0, 1.0 / sum1)
        weights[n * 128 : n * 128 + 128] = (raised * share).astype(jnp.bfloat16)
    for n in range(N_WIN):
        v = two_groups(kv[n * WTOK : n * WTOK + WTOK, HW : 2 * HW])
        o = jnp.dot(weights[n * 128 : n * 128 + 128], v, preferred_element_type=jnp.float32)
        total = o[0:QROWS]
        for h in range(1, 4):
            total = jnp.where(head == h, o[h * QROWS : h * QROWS + QROWS], total)
        wout[n] = total
    lower = lax.broadcasted_iota(jnp.int32, (8, HW), 0) < HALF
    for r in range(RH):
        a, wr = r // HALF, r % HALF
        turned = [
            pltpu.roll(wout[a * WIN_B + b, wr * WIN : wr * WIN + WIN], HALF, 0) for b in range(WIN_B)
        ]
        for j in range(4):
            to = r * RW + j * 8
            out_ref[to : to + 8] = jnp.where(lower, turned[j], turned[j + 1])


def join_kernel(win_ref, back_ref, undo_ref, out_ref):
    north = lax.axis_index("lat") == 0
    cap = jnp.dot(undo_ref[...], back_ref[...], preferred_element_type=jnp.float32)
    top = win_ref[0:CAP_TOKENS] + jnp.where(north, cap, 0.0)
    low = win_ref[CAP_TOKENS:] + jnp.where(north, 0.0, cap)
    out_ref[0:CAP_TOKENS] = top.astype(jnp.bfloat16)
    out_ref[CAP_TOKENS:] = low.astype(jnp.bfloat16)


def sds(shape, dtype):
    return jax.ShapeDtypeStruct(shape, dtype)


def call(kernel, name, outs, ins, out_specs, scratch, mib, flops, nbytes, trans=0):
    return pl.pallas_call(
        kernel,
        name=name,
        out_shape=outs,
        in_specs=ins,
        out_specs=out_specs,
        scratch_shapes=scratch,
        compiler_params=pltpu.CompilerParams(vmem_limit_bytes=mib << 20),
        cost_estimate=pl.CostEstimate(flops=flops, bytes_accessed=nbytes, transcendentals=trans),
    )


def exchange(block):
    return lax.all_to_all(block, "lon", split_axis=0, concat_axis=0, tiled=True)


def local(tokens, ln_gain, w_qkv, bias_table, bias_index, cap_group):
    lat_count = lax.axis_size("lat")
    lon_count = lax.axis_size("lon")
    bf16, f32 = jnp.bfloat16, jnp.float32
    gain = ln_gain.reshape(1, D)
    groups = cap_group.reshape(2, TILES_DEV)

    packed = call(
        pack_kernel, "pack", sds((SLOT_TOKENS, D), bf16),
        [sspec(), aspec()], vspec(),
        [VMEM((CAP, RW, D), bf16), pltpu.SemaphoreType.DMA],
        8, 2 * SLOT_TOKENS * CAP_TOKENS * D, 1 << 20,
    )(groups, tokens)
    arrived = exchange(packed.reshape(lon_count, MOST * TW, D)).reshape(SLOT_TOKENS, D)

    down = [(i, i + 1) for i in range(lat_count - 1)]
    up = [(i + 1, i) for i in range(lat_count - 1)]
    east = [(i, (i + 1) % lon_count) for i in range(lon_count)]
    west = [((i + 1) % lon_count, i) for i in range(lon_count)]
    tied, _ = lax.optimization_barrier((tokens, packed))
    north = lax.ppermute(tied[RH - HALF :], "lat", down)
    south = lax.ppermute(tied[:HALF], "lat", up)
    head, tail, undo = call(
        edge_kernel, "edges",
        (sds((64, D), bf16), sds((64, D), bf16), sds((CAP_TOKENS, SLOT_TOKENS), bf16)),
        [sspec(), vspec(), vspec(), vspec()], (vspec(), vspec(), vspec()), [],
        8, 1 << 20, 3 << 19,
    )(groups, tokens, north, south)
    left = lax.ppermute(tail, "lon", east)
    right = lax.ppermute(head, "lon", west)

    cap_result = call(
        cap_kernel, "caps", sds((SLOT_TOKENS, HW), bf16),
        [vspec(), vspec(), aspec()], vspec(),
        [VMEM((SLOT_TOKENS, D), bf16), VMEM((SLOT_TOKENS, 3 * HW), bf16), VMEM((D, 3 * HW), bf16), pltpu.SemaphoreType.DMA],
        20, 1100 << 20, 4 << 20, 1 << 19,
    )(arrived, gain, w_qkv)
    returned = exchange(cap_result.reshape(lon_count, MOST * TW, HW)).reshape(SLOT_TOKENS, HW)

    table = jnp.pad(bias_table, ((0, 0), (0, 256 - BIAS_ROWS)))
    index = jnp.concatenate([bias_index, bias_index], axis=1)
    own, _ = lax.optimization_barrier((tokens, cap_result))
    win_out = call(
        window_kernel, "windows", sds((RH * RW, HW), f32),
        [vspec()] * 8 + [aspec()], vspec(),
        [
            VMEM((N_WIN * WTOK, D), bf16),
            VMEM((N_WIN * QROWS, D), bf16),
            VMEM((N_WIN * WTOK, 2 * HW), bf16),
            VMEM((N_WIN * QROWS, HW), bf16),
            VMEM((2 * 128, 128), f32),
            VMEM((N_WIN * 128, 128), f32),
            VMEM((N_WIN * 128, 128), bf16),
            VMEM((N_WIN, QROWS, HW), f32),
            VMEM((2, 64, D), f32),
            VMEM((D, 3 * HW), bf16),
            pltpu.SemaphoreType.DMA,
        ],
        28, 2300 << 20, 6 << 20, 1 << 18,
    )(own, north, south, left, right, gain, table, index, w_qkv)
    mixed = call(
        join_kernel, "join", sds((RH * RW, HW), bf16),
        [vspec()] * 3, vspec(), [],
        8, 2 * CAP_TOKENS * SLOT_TOKENS * HW, 1 << 20,
    )(win_out, returned, undo)
    return mixed.reshape(RH, RW, HW)


def solution(mesh):
    placed = (P("lat", "lon", None), P(), P(), P(), P(), P(None, "lon", None, None))
    return jax.shard_map(
        local, mesh=mesh, in_specs=placed, out_specs=P("lat", "lon", None), check_vma=False
    )
```

time: 164 us -> 62.8 us (0.38)
  the two profiles are of different devices: /device:TPU:41 before, /device:TPU:1 now
where the time goes in v1:
time: 62.8 us; the launch traced here: 62.2 us
  starting transfers between devices  28.6 us (46%)
  waiting for transfers between devices  14.6 us (23%)
  Pallas kernels  11.9 us (19%)
  local copies, waits for them, and re-layouts  6.84 us (11%)
    all_to_all x2, starting transfers between devices, exchange(): return lax.all_to_all(block, 'lon', split_axis=0, concat_axis=0, tiled=True)  17.9 us
    all_to_all x2, waiting for transfers between devices, exchange(): return lax.all_to_all(block, 'lon', split_axis=0, concat_axis=0, tiled=True)  10 us
    unnamed x15, local copies, waits for them, and re-layouts  5.63 us
    pallas_call x1, Pallas kernels, local(): call(window_kernel, 'windows', sds((RH * RW, HW), f32), [vspec()] * 8 + [...  4.83 us
    ppermute x1, waiting for transfers between devices, local(): right = lax.ppermute(head, 'lon', west)  4.54 us
    ppermute x1, starting transfers between devices, local(): north = lax.ppermute(tied[RH - HALF:], 'lat', down)  4 us
    ppermute x1, starting transfers between devices, local(): left = lax.ppermute(tail, 'lon', east)  3.55 us
    pallas_call x1, Pallas kernels, local(): call(cap_kernel, 'caps', sds((SLOT_TOKENS, HW), bf16), [vspec(), vspec(),...  3.28 us
  transfers between devices with their start and end apart: 6, of which 2 were waited for; matrix products, arithmetic and copies ran while one was open for 2% of the time, Pallas kernels for 15%

profile of v1, /device:TPU:1, one launch (start us, length us, event | category | flops | bytes accessed | tf_op | source)
XLA Modules:
  0.0 62.2 jit_solution(1439618385596085970)
XLA Ops:
  0.0 0.0 copy-start.4
  0.0 0.8 %copy.8 = s32[2,8,4,1]{2,1,0,3:T(8,128)S(1)} copy(s32[2,8,4,1]{1,3,2,0:T(1,128)} %param.11) | data formatting | bytes 512 | tf_op args[5]
  0.8 0.1 reshape.21.group_ref
  0.9 1.0 %copy-done = bf16[8,32,1024]{2,1,0:T(8,128)(2,1)S(1)} copy-done((bf16[8,32,1024]{2,1,0:T(8,128)(2,1)S(1)}, bf16[8,32,1024]{2,1,0:T(8,128)(2,1)}, u32[]{:S(2)}) %copy-start) | copy-done | bytes 524312
  1.9 1.7 %pack.1 = bf16[256,1024]{1,0:T(8,128)(2,1)} custom-call(s32[2,32]{1,0:T(2,128)S(1)} %reshape.21.group_ref, bf16[8,32,1024]{2,1,0:T(8,128)(2,1)S(1)} %copy-done), custom_call_target="tpu_custom_call" | custom-call | flops 67108864 | bytes 1048576 | tf_op jit(solution)/shard_map/pack/pallas_call | solution.py:307
  3.7 13.0 %all-to-all-start = ((bf16[32,8,1024]{2,1,0:T(8,128)(2,1)}), bf16[32,8,1024]{2,1,0:T(8,128)(2,1)S(1)}, u32[]{:S(2)}, u32[]{:S(2)}) async-start(bf16[32,8,1024]{2,1,0:T(8,128)(2,1)} %bitcast), calls=%async_computation | async-start | bytes 1048576 | tf_op jit(solution)/shard_map/all_to_all | solution.py:297
  16.7 0.0 copy-start.1
  16.7 0.0 copy-start.6
  16.7 0.0 copy-start.5
  16.7 1.1 %fusion = (bf16[4,32,1024]{2,1,0:T(8,128)(2,1)S(1)}, bf16[4,32,1024]{2,1,0:T(8,128)(2,1)S(1)}) fusion(bf16[8,32,1024]{2,1,0:T(8,128)(2,1)} %own_ref.2), kind=kLoop, calls=%fused_computation.1 | loop fusion | bytes 1048576 | tf_op jit(solution)/shard_map/slice | solution.py:321
  17.8 1.3 %collective-permute-start.1 = (bf16[4,32,1024]{2,1,0:T(8,128)(2,1)S(1)}, bf16[4,32,1024]{2,1,0:T(8,128)(2,1)S(1)}, u32[]{:S(2)}, u32[]{:S(2)}) collective-permute-start(bf16[4,32,1024]{2,1,0:T(8,128)(2,1)S(1)} %get-tuple-element.15), channel_id=1, source_target_pairs={{32,0},{64,32},{96,64},{128,96},{160,128},{192,160},{224,192},{256... | collective-permute-start | bytes 786440 | tf_op jit(solution)/shard_map/ppermute | solution.py:321
  19.1 4.0 %collective-permute-start = (bf16[4,32,1024]{2,1,0:T(8,128)(2,1)S(1)}, bf16[4,32,1024]{2,1,0:T(8,128)(2,1)S(1)}, u32[]{:S(2)}, u32[]{:S(2)}) collective-permute-start(bf16[4,32,1024]{2,1,0:T(8,128)(2,1)S(1)} %get-tuple-element.16), channel_id=1, source_target_pairs={{0,32},{32,64},{64,96},{96,128},{128,160},{160,192},{192,224},{224... | collective-permute-start | bytes 786440 | tf_op jit(solution)/shard_map/ppermute | solution.py:320
  23.1 10.0 %all-to-all-done = bf16[32,8,1024]{2,1,0:T(8,128)(2,1)S(1)} async-done(((bf16[32,8,1024]{2,1,0:T(8,128)(2,1)}), bf16[32,8,1024]{2,1,0:T(8,128)(2,1)S(1)}, u32[]{:S(2)}, u32[]{:S(2)}) %all-to-all-start) | async-done | bytes 524320 | tf_op jit(solution)/shard_map/all_to_all | solution.py:297
  33.2 0.0 copy-done.4
  33.2 1.9 %copy-done.2 = bf16[1024,1536]{1,0:T(8,128)(2,1)S(1)} copy-done((bf16[1024,1536]{1,0:T(8,128)(2,1)S(1)}, bf16[1024,1536]{1,0:T(8,128)(2,1)}, u32[]{:S(2)}) %copy-start.2) | copy-done | bytes 3145752
  35.1 3.3 %caps.1 = bf16[256,512]{1,0:T(8,128)(2,1)} custom-call(bf16[256,1024]{1,0:T(8,128)(2,1)S(1)} %bitcast.11, f32[1,1024]{1,0:T(1,128)S(1)} %bitcast.12, bf16[1024,1536]{1,0:T(8,128)(2,1)S(1)} %copy-done.2), custom_call_target="tpu_custom_call" | custom-call | flops 1153433600 | bytes 4194304 | tf_op jit(solution)/shard_map/caps/pallas_call | solution.py:331
  38.4 4.9 %all-to-all-start.1 = ((bf16[32,8,512]{2,1,0:T(8,128)(2,1)}), bf16[32,8,512]{2,1,0:T(8,128)(2,1)S(1)}, u32[]{:S(2)}, u32[]{:S(2)}) async-start(bf16[32,8,512]{2,1,0:T(8,128)(2,1)} %bitcast.3), calls=%async_computation.1 | async-start | bytes 524288 | tf_op jit(solution)/shard_map/all_to_all | solution.py:297
  43.3 0.0 collective-permute-done.1.south_ref
  43.3 0.0 collective-permute-done.north_ref
  43.3 0.0 copy-done.1
  43.3 1.2 %edges.1 = (bf16[64,1024]{1,0:T(8,128)(2,1)S(1)}, bf16[64,1024]{1,0:T(8,128)(2,1)S(1)}, bf16[128,256]{1,0:T(8,128)(2,1)S(1)}) custom-call(s32[2,32]{1,0:T(2,128)S(1)} %reshape.21.group_ref, bf16[8,32,1024]{2,1,0:T(8,128)(2,1)S(1)} %copy-done.1, bf16[4,32,1024]{2,1,0:T(8,128)(2,1)S(1)} %collective-permute-done.north_ref, ...), custom_call_target="tpu_custom_call" | custom-call | flops 1048576 | bytes 1572864 | tf_op jit(solution)/shard_map/edges/pallas_call | solution.py:322
  44.5 3.5 %collective-permute-start.2 = (bf16[64,1024]{1,0:T(8,128)(2,1)S(1)}, bf16[64,1024]{1,0:T(8,128)(2,1)S(1)}, u32[]{:S(2)}, u32[]{:S(2)}) collective-permute-start(bf16[64,1024]{1,0:T(8,128)(2,1)S(1)} %get-tuple-element.12), channel_id=1, source_target_pairs={{0,1},{1,2},{2,3},{3,4},{4,5},{5,6},{6,7},{7,8},{8,9},{9,10},{10,1... | collective-permute-start | bytes 393224 | tf_op jit(solution)/shard_map/ppermute | solution.py:328
  48.0 1.9 %collective-permute-start.3 = (bf16[64,1024]{1,0:T(8,128)(2,1)S(1)}, bf16[64,1024]{1,0:T(8,128)(2,1)S(1)}, u32[]{:S(2)}, u32[]{:S(2)}) collective-permute-start(bf16[64,1024]{1,0:T(8,128)(2,1)S(1)} %get-tuple-element.13), channel_id=1, source_target_pairs={{1,0},{2,1},{3,2},{4,3},{5,4},{6,5},{7,6},{8,7},{9,8},{10,9},{11,1... | collective-permute-start | bytes 393224 | tf_op jit(solution)/shard_map/ppermute | solution.py:329
  49.9 0.0 copy-done.6
  50.0 0.0 copy-done.5
  50.0 0.1 pad_add_fusion.index_ref
  50.1 0.0 collective-permute-done.2.left_ref
  50.1 4.5 %collective-permute-done.3.right_ref = bf16[64,1024]{1,0:T(8,128)(2,1)S(1)} collective-permute-done((bf16[64,1024]{1,0:T(8,128)(2,1)S(1)}, bf16[64,1024]{1,0:T(8,128)(2,1)S(1)}, u32[]{:S(2)}, u32[]{:S(2)}) %collective-permute-start.3) | collective-permute-done | bytes 131104 | tf_op jit(solution)/shard_map/ppermute | solution.py:329
  54.6 1.9 %copy-done.3 = bf16[1024,1536]{1,0:T(8,128)(2,1)S(1)} copy-done((bf16[1024,1536]{1,0:T(8,128)(2,1)S(1)}, bf16[1024,1536]{1,0:T(8,128)(2,1)}, u32[]{:S(2)}) %copy-start.3) | copy-done | bytes 3145752
  56.5 4.8 %windows.1.win_ref = f32[256,512]{1,0:T(8,128)S(1)} custom-call(bf16[8,32,1024]{2,1,0:T(8,128)(2,1)S(1)} %copy-done.1, bf16[4,32,1024]{2,1,0:T(8,128)(2,1)S(1)} %collective-permute-done.north_ref, bf16[4,32,1024]{2,1,0:T(8,128)(2,1)S(1)} %collective-permute-done.1.south_ref, bf16[64,1024]{1,0:T(8,128)(2,1)S(1)} %collective-permute-done.2.left_ref, ...), custom_call_target="tpu_custom_call" | custom-call | flops 2411724800 | bytes 6291456 | tf_op jit(solution)/shard_map/windows/pallas_call | solution.py:342
  61.3 0.0 all-to-all-done.1
  61.3 0.9 %join.1 = bf16[256,512]{1,0:T(8,128)(2,1)} custom-call(f32[256,512]{1,0:T(8,128)S(1)} %windows.1.win_ref, bf16[256,512]{1,0:T(8,128)(2,1)S(1)} %bitcast.10, bf16[128,256]{1,0:T(8,128)(2,1)S(1)} %get-tuple-element.14.undo_ref), custom_call_target="tpu_custom_call" | custom-call | flops 33554432 | bytes 1048576 | tf_op jit(solution)/shard_map/join/pallas_call | solution.py:360
  (4 shorter events, 0.0 us)
Async XLA Ops:
  0.0 33.2 %copy-start.4 = (f32[1024]{0:T(1024)S(1)}, f32[1024]{0:T(1024)}, u32[]{:S(2)}) copy-start(f32[1024]{0:T(1024)} %param.7) | copy-start | bytes 12292
  0.9 1.0 %copy-start = (bf16[8,32,1024]{2,1,0:T(8,128)(2,1)S(1)}, bf16[8,32,1024]{2,1,0:T(8,128)(2,1)}, u32[]{:S(2)}) copy-start(bf16[8,32,1024]{2,1,0:T(8,128)(2,1)} %own_ref.2) | copy-start | bytes 1572868
  3.7 29.5 %all-to-all-start = ((bf16[32,8,1024]{2,1,0:T(8,128)(2,1)}), bf16[32,8,1024]{2,1,0:T(8,128)(2,1)S(1)}, u32[]{:S(2)}, u32[]{:S(2)}) async-start(bf16[32,8,1024]{2,1,0:T(8,128)(2,1)} %bitcast), calls=%async_computation | async-start | bytes 1048576 | tf_op jit(solution)/shard_map/all_to_all | solution.py:297
  16.7 26.6 %copy-start.1 = (bf16[8,32,1024]{2,1,0:T(8,128)(2,1)S(1)}, bf16[8,32,1024]{2,1,0:T(8,128)(2,1)}, u32[]{:S(2)}) copy-start(bf16[8,32,1024]{2,1,0:T(8,128)(2,1)} %own_ref.2) | copy-start | bytes 1572868
  16.7 33.3 %copy-start.6 = (f32[8,225]{1,0:T(8,128)S(1)}, f32[8,225]{1,0:T(8,128)}, u32[]{:S(2)}) copy-start(f32[8,225]{1,0:T(8,128)} %param.9) | copy-start | bytes 21604
  16.7 33.3 %copy-start.5 = (s32[64,64]{1,0:T(8,128)S(1)}, s32[64,64]{1,0:T(8,128)}, u32[]{:S(2)}) copy-start(s32[64,64]{1,0:T(8,128)} %param.10) | copy-start | bytes 49156
  17.8 25.4 %collective-permute-start.1 = (bf16[4,32,1024]{2,1,0:T(8,128)(2,1)S(1)}, bf16[4,32,1024]{2,1,0:T(8,128)(2,1)S(1)}, u32[]{:S(2)}, u32[]{:S(2)}) collective-permute-start(bf16[4,32,1024]{2,1,0:T(8,128)(2,1)S(1)} %get-tuple-element.15), channel_id=1, source_target_pairs={{32,0},{64,32},{96,64},{128,96},{160,128},{192,160},{224,192},{256... | collective-permute-start | bytes 786440 | tf_op jit(solution)/shard_map/ppermute | solution.py:321
  19.1 24.2 %collective-permute-start = (bf16[4,32,1024]{2,1,0:T(8,128)(2,1)S(1)}, bf16[4,32,1024]{2,1,0:T(8,128)(2,1)S(1)}, u32[]{:S(2)}, u32[]{:S(2)}) collective-permute-start(bf16[4,32,1024]{2,1,0:T(8,128)(2,1)S(1)} %get-tuple-element.16), channel_id=1, source_target_pairs={{0,32},{32,64},{64,96},{96,128},{128,160},{160,192},{192,224},{224... | collective-permute-start | bytes 786440 | tf_op jit(solution)/shard_map/ppermute | solution.py:320
  33.2 1.9 %copy-start.2 = (bf16[1024,1536]{1,0:T(8,128)(2,1)S(1)}, bf16[1024,1536]{1,0:T(8,128)(2,1)}, u32[]{:S(2)}) copy-start(bf16[1024,1536]{1,0:T(8,128)(2,1)} %w_ref.3) | copy-start | bytes 9437188
  38.4 23.0 %all-to-all-start.1 = ((bf16[32,8,512]{2,1,0:T(8,128)(2,1)}), bf16[32,8,512]{2,1,0:T(8,128)(2,1)S(1)}, u32[]{:S(2)}, u32[]{:S(2)}) async-start(bf16[32,8,512]{2,1,0:T(8,128)(2,1)} %bitcast.3), calls=%async_computation.1 | async-start | bytes 524288 | tf_op jit(solution)/shard_map/all_to_all | solution.py:297
  44.5 5.6 %collective-permute-start.2 = (bf16[64,1024]{1,0:T(8,128)(2,1)S(1)}, bf16[64,1024]{1,0:T(8,128)(2,1)S(1)}, u32[]{:S(2)}, u32[]{:S(2)}) collective-permute-start(bf16[64,1024]{1,0:T(8,128)(2,1)S(1)} %get-tuple-element.12), channel_id=1, source_target_pairs={{0,1},{1,2},{2,3},{3,4},{4,5},{5,6},{6,7},{7,8},{8,9},{9,10},{10,1... | collective-permute-start | bytes 393224 | tf_op jit(solution)/shard_map/ppermute | solution.py:328
  48.0 6.6 %collective-permute-start.3 = (bf16[64,1024]{1,0:T(8,128)(2,1)S(1)}, bf16[64,1024]{1,0:T(8,128)(2,1)S(1)}, u32[]{:S(2)}, u32[]{:S(2)}) collective-permute-start(bf16[64,1024]{1,0:T(8,128)(2,1)S(1)} %get-tuple-element.13), channel_id=1, source_target_pairs={{1,0},{2,1},{3,2},{4,3},{5,4},{6,5},{7,6},{8,7},{9,8},{10,9},{11,1... | collective-permute-start | bytes 393224 | tf_op jit(solution)/shard_map/ppermute | solution.py:329
  54.6 1.9 %copy-start.3 = (bf16[1024,1536]{1,0:T(8,128)(2,1)S(1)}, bf16[1024,1536]{1,0:T(8,128)(2,1)}, u32[]{:S(2)}) copy-start(bf16[1024,1536]{1,0:T(8,128)(2,1)} %w_ref.3) | copy-start | bytes 9437188

commit v2 on v1

v2 whole, which is shorter than its diff:
```python
import jax
import jax.numpy as jnp
from jax import lax
from jax.experimental import pallas as pl
from jax.experimental.pallas import tpu as pltpu
from jax.sharding import PartitionSpec as P


D = 1024
HEADS = 8
HD = 64
WIN = 8
TW = 4
CAP = 4
RH = 8
RW = 32
HW = 512
HALF = 4
BIAS_ROWS = 225
TILES_DEV = 32
TILE_COLS = RW // TW
GROUPS = 32
MOST = 2
SLOT_TOKENS = GROUPS * MOST * TW
CAP_TOKENS = CAP * RW
N_WIN = 10
WIN_B = 5
WTOK = WIN * WIN
QROWS = HALF * WIN

epsilon = 1e-05
masked_score = -1e30
EMPTY = 128.0
EMPTY_ABOVE = 64.0

ALL_VMEM = 67043328
SOME_VMEM = 24 << 20

VMEM = pltpu.VMEM
SMEM = pltpu.SMEM


def vspec():
    return pl.BlockSpec(memory_space=VMEM)


def aspec():
    return pl.BlockSpec(memory_space=pl.ANY)


def hspec():
    return pl.BlockSpec(memory_space=pltpu.HBM)


def norm_rows(values, gain):
    center = jnp.mean(values, axis=-1, keepdims=True)
    shifted = values - center
    spread = jnp.mean(jnp.square(shifted), axis=-1, keepdims=True)
    return shifted * lax.rsqrt(spread + epsilon) * gain


def slot_rows(group_ref, pole, lane):
    tile = lane // TW
    names = [group_ref[pole, t // TILE_COLS, 0, t % TILE_COLS] for t in range(TILES_DEV)]
    group = jnp.zeros_like(lane)
    for t in range(TILES_DEV):
        group = jnp.where(tile == t, names[t], group)
    rank = jnp.zeros_like(lane)
    for t in range(TILES_DEV):
        same = (group == names[t]) & (tile > t)
        rank = rank + same.astype(jnp.int32)
    return (group * MOST + rank) * TW + lane % TW


PACK_STEP = 64


def pack_kernel(names_ref, tokens_ref, send_ref, group_ref, rows, out, name_sem, sem, out_sem):
    north = lax.axis_index("lat") == 0
    pole = jnp.where(north, 0, 1)
    start = jnp.where(north, 0, RH - CAP)
    names = pltpu.make_async_copy(names_ref, group_ref, name_sem)
    names.start()
    copy = pltpu.make_async_copy(tokens_ref.at[pl.ds(start, CAP)], rows, sem)
    copy.start()
    names.wait()
    lane = lax.broadcasted_iota(jnp.int32, (8, CAP_TOKENS), 1)
    slot = slot_rows(group_ref, pole, lane)[0:1]
    copy.wait()
    x = rows[...].reshape(CAP_TOKENS, D)
    sends = []
    for n in range(SLOT_TOKENS // PACK_STEP):
        at = pl.ds(n * PACK_STEP, PACK_STEP)
        hit = lax.broadcasted_iota(jnp.int32, (PACK_STEP, CAP_TOKENS), 0) + n * PACK_STEP == slot
        hot = hit.astype(jnp.float32)
        filled = jnp.max(hot, axis=1, keepdims=True) > 0.5
        moved = jnp.dot(hot.astype(jnp.bfloat16), x, preferred_element_type=jnp.float32)
        out[at, :] = jnp.where(filled, moved, EMPTY).astype(jnp.bfloat16)
        sends.append(pltpu.make_async_copy(out.at[at], send_ref.at[at], out_sem.at[n]))
        sends[n].start()
    for send in sends:
        send.wait()


def edge_kernel(own_ref, head_ref, tail_ref):
    lower = lax.broadcasted_iota(jnp.int32, (8, D), 0) < HALF
    for r in range(0, RH, 4):
        heads, tails = [], []
        for i in (r, r + 2):
            first = [own_ref[i + k, 0:8].astype(jnp.float32) for k in range(2)]
            last = [own_ref[i + k, 24:32].astype(jnp.float32) for k in range(2)]
            heads.append(jnp.where(lower, first[0], pltpu.roll(first[1], HALF, 0)))
            tails.append(jnp.where(lower, pltpu.roll(last[0], HALF, 0), last[1]))
        head_ref[r * 4 : r * 4 + 16] = jnp.concatenate(heads, 0).astype(jnp.bfloat16)
        tail_ref[r * 4 : r * 4 + 16] = jnp.concatenate(tails, 0).astype(jnp.bfloat16)


def undo_kernel(names_ref, undo_ref, group_ref, name_sem):
    names = pltpu.make_async_copy(names_ref, group_ref, name_sem)
    names.start()
    lat = lax.axis_index("lat")
    north = lat == 0
    polar = north | (lat == lax.axis_size("lat") - 1)
    pole = jnp.where(north, 0, 1)
    token = lax.broadcasted_iota(jnp.int32, (CAP_TOKENS, 128), 0)
    names.wait()
    slot = slot_rows(group_ref, pole, token)
    slot = jnp.where(polar, slot, -1)
    for i in range(0, SLOT_TOKENS, 128):
        hit = lax.broadcasted_iota(jnp.int32, (CAP_TOKENS, 128), 1) + i == slot
        undo_ref[:, i : i + 128] = hit.astype(jnp.float32).astype(jnp.bfloat16)


RIM_SIDE = HALF * HALF
RIM = HALF * RW + 2 * RIM_SIDE


def rim_kernel(own_ref, left_ref, right_ref, up_ref, down_ref, sem):
    copies = []
    for n, (out, first) in enumerate(((up_ref, 0), (down_ref, RH - HALF))):
        for r in range(HALF):
            at = pl.ds(r * RW, RW)
            copies.append(pltpu.make_async_copy(own_ref.at[first + r], out.at[at], sem.at[n * 6 + r]))
        for k, side in enumerate((left_ref, right_ref)):
            at = pl.ds(HALF * RW + k * RIM_SIDE, RIM_SIDE)
            part = side.at[pl.ds(first * HALF, RIM_SIDE)]
            copies.append(pltpu.make_async_copy(part, out.at[at], sem.at[n * 6 + 4 + k]))
    for copy in copies:
        copy.start()
    for copy in copies:
        copy.wait()


W_STEP = 256


def cap_norm_kernel(x_ref, gain_ref, normed, empty_ref):
    gain = gain_ref[...]
    for i in range(0, SLOT_TOKENS, 32):
        normed[i : i + 32] = norm_rows(x_ref[i : i + 32].astype(jnp.float32), gain).astype(jnp.bfloat16)
    pick = (lax.broadcasted_iota(jnp.int32, (8, 128), 1) == 0).astype(jnp.bfloat16)
    first = lax.dot_general(
        pick, x_ref[:, 0:128], (((1,), (1,)), ((), ())), preferred_element_type=jnp.float32
    )
    empty_ref[...] = jnp.where(first > EMPTY_ABOVE, masked_score, 0.0)


def cap_kernel(normed, empty_ref, w_ref, out_ref, qkv):
    n = SLOT_TOKENS
    empty = empty_ref[0:1]
    for j in range(0, 3 * HW, W_STEP):
        w = w_ref[:, j : j + W_STEP]
        part = jnp.dot(normed[...], w, preferred_element_type=jnp.float32)
        qkv[:, j : j + W_STEP] = part.astype(jnp.bfloat16)
    low = lax.broadcasted_iota(jnp.int32, (n, 128), 1) < HD
    for pair in range(HEADS // 2):
        at = pair * 128
        q = qkv[:, at : at + 128] * jnp.bfloat16(HD ** (-0.5))
        k = qkv[:, HW + at : HW + at + 128]
        v = qkv[:, 2 * HW + at : 2 * HW + at + 128]
        mixed = []
        for half in range(2):
            mine = low if half == 0 else jnp.logical_not(low)
            qh = jnp.where(mine, q, jnp.zeros_like(q))
            s = lax.dot_general(qh, k, (((1,), (1,)), ((), ())), preferred_element_type=jnp.float32)
            s = s + empty
            raised = jnp.exp(s - jnp.max(s, axis=-1, keepdims=True))
            weights = (raised * (1.0 / jnp.sum(raised, axis=-1, keepdims=True))).astype(jnp.bfloat16)
            mixed.append(jnp.dot(weights, v, preferred_element_type=jnp.float32))
        out_ref[:, at : at + 128] = jnp.where(low, mixed[0], mixed[1]).astype(jnp.bfloat16)


def bias_kernel(table_ref, index_ref, bias_ref):
    lat = lax.axis_index("lat")
    lane = lax.broadcasted_iota(jnp.int32, (8, 128), 1)
    first = lane < WTOK
    key_row = (lane % WTOK) // WIN
    off_north = (lat == 0) & (key_row < HALF)
    off_south = (lat == lax.axis_size("lat") - 1) & (key_row >= HALF)
    tables = []
    for h in range(HEADS):
        parts = [table_ref[h : h + 1, c : c + 128] for c in (0, BIAS_ROWS - 128)]
        tables.append([jnp.broadcast_to(part, (8, 128)) for part in parts])
    for a in range(2):
        off = off_north if a == 0 else off_south
        for i in range(0, QROWS, 8):
            at = (QROWS if a == 0 else 0) + i
            idx = index_ref[at : at + 8, :]
            idx = jnp.concatenate([idx, idx], axis=1)
            high = idx >= 128
            inner = jnp.where(high, idx - (BIAS_ROWS - 128), idx)
            for h4 in range(4):
                found = []
                for h in (h4, h4 + 4):
                    lo = jnp.take_along_axis(tables[h][0], inner, axis=1)
                    hi = jnp.take_along_axis(tables[h][1], inner, axis=1)
                    found.append(jnp.where(high, hi, lo))
                value = jnp.where(first, found[0], found[1])
                to = a * 128 + h4 * QROWS + i
                bias_ref[to : to + 8, :] = jnp.where(off, masked_score, value)


def window_kernel(
    own_ref, north_ref, south_ref, left_ref, right_ref, gain_ref, bias, w_ref,
    out_ref, xs, xq, kv, qs, scores, weights, wout, edges,
):
    gain = gain_ref[...]

    for side, ref in enumerate((left_ref, right_ref)):
        at = HALF * RW + side * RIM_SIDE
        for to, x in (
            (0, north_ref[at : at + RIM_SIDE]),
            (RIM_SIDE, ref[...]),
            (3 * RIM_SIDE, south_ref[at : at + RIM_SIDE]),
        ):
            edges[side, to : to + x.shape[0]] = norm_rows(x.astype(jnp.float32), gain)
    lower = lax.broadcasted_iota(jnp.int32, (8, D), 0) < HALF
    rows = [(north_ref, i) for i in range(HALF)] + [(own_ref, i) for i in range(RH)]
    rows += [(south_ref, i) for i in range(HALF)]
    for r in range(0, RH + WIN, 2):
        blocks = [[], []]
        for k in range(2):
            ref, i = rows[r + k]
            x = ref[i] if ref is own_ref else ref[i * RW : i * RW + RW]
            normed = norm_rows(x.astype(jnp.float32), gain)
            turned = [pltpu.roll(normed[j * 8 : j * 8 + 8], HALF, 0) for j in range(4)]
            lo = edges[0, r * 4 : r * 4 + 8]
            hi = edges[1, r * 4 : r * 4 + 8]
            if k == 0:
                hi = pltpu.roll(hi, HALF, 0)
            else:
                lo = pltpu.roll(lo, HALF, 0)
            seq = [lo] + turned + [hi]
            blocks[k] = [jnp.where(lower, seq[b], seq[b + 1]) for b in range(WIN_B)]
        a, wr = r // WIN, r % WIN
        for b in range(WIN_B):
            both = jnp.concatenate([blocks[0][b], blocks[1][b]], 0).astype(jnp.bfloat16)
            to = (a * WIN_B + b) * WTOK + wr * WIN
            xs[to : to + 16] = both
            if (wr >= HALF) == (a == 0):
                to = (a * WIN_B + b) * QROWS + (wr % HALF) * WIN
                xq[to : to + 16] = both

    for j in range(0, 3 * HW, W_STEP):
        w = w_ref[:, j : j + W_STEP]
        if j < HW:
            qs[:, j : j + W_STEP] = jnp.dot(xq[...], w, preferred_element_type=jnp.float32).astype(jnp.bfloat16)
        else:
            part = jnp.dot(xs[...], w, preferred_element_type=jnp.float32)
            kv[:, j - HW : j - HW + W_STEP] = part.astype(jnp.bfloat16)

    head = lax.broadcasted_iota(jnp.int32, (QROWS, HW), 1) // HD % 4
    blank = jnp.zeros((WTOK, HW // 2), jnp.bfloat16)

    def two_groups(x):
        top = jnp.concatenate([x[:, : HW // 2], blank], 1)
        low = jnp.concatenate([blank, x[:, HW // 2 :]], 1)
        return jnp.concatenate([top, low], 0)

    for n in range(N_WIN):
        q = qs[n * QROWS : n * QROWS + QROWS] * jnp.bfloat16(HD ** (-0.5))
        spread = jnp.concatenate([jnp.where(head == h, q, jnp.zeros_like(q)) for h in range(4)], 0)
        k = two_groups(kv[n * WTOK : n * WTOK + WTOK, 0:HW])
        s = lax.dot_general(spread, k, (((1,), (1,)), ((), ())), preferred_element_type=jnp.float32)
        a = n // WIN_B
        scores[n * 128 : n * 128 + 128] = s + bias[a * 128 : a * 128 + 128]
    left = lax.broadcasted_iota(jnp.int32, (128, 128), 1) < WTOK
    for n in range(N_WIN):
        s = scores[n * 128 : n * 128 + 128]
        top0 = jnp.max(jnp.where(left, s, -jnp.inf), axis=-1, keepdims=True)
        top1 = jnp.max(jnp.where(left, -jnp.inf, s), axis=-1, keepdims=True)
        raised = jnp.exp(s - jnp.where(left, top0, top1))
        sum0 = jnp.sum(jnp.where(left, raised, 0.0), axis=-1, keepdims=True)
        sum1 = jnp.sum(jnp.where(left, 0.0, raised), axis=-1, keepdims=True)
        share = jnp.where(left, 1.0 / sum0, 1.0 / sum1)
        weights[n * 128 : n * 128 + 128] = (raised * share).astype(jnp.bfloat16)
    for n in range(N_WIN):
        v = two_groups(kv[n * WTOK : n * WTOK + WTOK, HW : 2 * HW])
        o = jnp.dot(weights[n * 128 : n * 128 + 128], v, preferred_element_type=jnp.float32)
        total = o[0:QROWS]
        for h in range(1, 4):
            total = jnp.where(head == h, o[h * QROWS : h * QROWS + QROWS], total)
        wout[n] = total
    lower = lax.broadcasted_iota(jnp.int32, (8, HW), 0) < HALF
    for r in range(RH):
        a, wr = r // HALF, r % HALF
        turned = [
            pltpu.roll(wout[a * WIN_B + b, wr * WIN : wr * WIN + WIN], HALF, 0) for b in range(WIN_B)
        ]
        for j in range(4):
            to = r * RW + j * 8
            out_ref[to : to + 8] = jnp.where(lower, turned[j], turned[j + 1])


def join_kernel(win_ref, back_ref, undo_ref, out_ref):
    north = lax.axis_index("lat") == 0
    cap = jnp.dot(undo_ref[...], back_ref[...], preferred_element_type=jnp.float32)
    top = win_ref[0:CAP_TOKENS] + jnp.where(north, cap, 0.0)
    low = win_ref[CAP_TOKENS:] + jnp.where(north, 0.0, cap)
    out_ref[0:CAP_TOKENS] = top.astype(jnp.bfloat16)
    out_ref[CAP_TOKENS:] = low.astype(jnp.bfloat16)


def sds(shape, dtype):
    return jax.ShapeDtypeStruct(shape, dtype)


def call(kernel, outs, ins, out_specs, scratch, vmem, flops, nbytes, trans=0):
    return pl.pallas_call(
        kernel,
        out_shape=outs,
        in_specs=ins,
        out_specs=out_specs,
        scratch_shapes=scratch,
        compiler_params=pltpu.CompilerParams(vmem_limit_bytes=vmem),
        cost_estimate=pl.CostEstimate(flops=flops, bytes_accessed=nbytes, transcendentals=trans),
    )


def exchange(block):
    return lax.all_to_all(block, "lon", split_axis=0, concat_axis=0, tiled=True)


def layer(tokens, ln_gain, w_qkv, bias_table, bias_index, cap_group):
    lat_count = lax.axis_size("lat")
    lon_count = lax.axis_size("lon")
    bf16, f32 = jnp.bfloat16, jnp.float32
    gain = ln_gain.reshape(1, D)
    groups = cap_group.transpose(0, 2, 3, 1)

    packed = call(
        pack_kernel, sds((SLOT_TOKENS, D), bf16),
        [aspec(), hspec()], hspec(),
        [
            SMEM((2, CAP, 1, TILE_COLS), jnp.int32),
            VMEM((CAP, RW, D), bf16),
            VMEM((SLOT_TOKENS, D), bf16),
            pltpu.SemaphoreType.DMA,
            pltpu.SemaphoreType.DMA,
            pltpu.SemaphoreType.DMA((SLOT_TOKENS // PACK_STEP,)),
        ],
        ALL_VMEM, 2 * SLOT_TOKENS * CAP_TOKENS * D, 1 << 20,
    )(groups, tokens)
    arrived = exchange(packed.reshape(lon_count, MOST * TW, D)).reshape(SLOT_TOKENS, D)

    down = [(i, i + 1) for i in range(lat_count - 1)]
    up = [(i + 1, i) for i in range(lat_count - 1)]
    east = [(i, (i + 1) % lon_count) for i in range(lon_count)]
    west = [((i + 1) % lon_count, i) for i in range(lon_count)]
    side = sds((RH * HALF, D), bf16)
    head, tail = call(
        edge_kernel, (side, side), [vspec()], (vspec(), vspec()), [],
        SOME_VMEM, 1 << 18, 3 << 18,
    )(tokens)
    left = lax.ppermute(tail, "lon", east)
    right = lax.ppermute(head, "lon", west)
    undo = call(
        undo_kernel, sds((CAP_TOKENS, SLOT_TOKENS), bf16), [aspec()], vspec(),
        [SMEM((2, CAP, 1, TILE_COLS), jnp.int32), pltpu.SemaphoreType.DMA],
        SOME_VMEM, 1 << 18, 1 << 16,
    )(groups)
    rim = sds((RIM, D), bf16)
    to_north, to_south = call(
        rim_kernel, (rim, rim), [aspec(), aspec(), aspec()], (vspec(), vspec()),
        [pltpu.SemaphoreType.DMA((12,))],
        SOME_VMEM, 1 << 10, 3 << 19,
    )(tokens, left, right)
    north = lax.ppermute(to_south, "lat", down)
    south = lax.ppermute(to_north, "lat", up)

    bias = call(
        bias_kernel, sds((2 * 128, 128), f32),
        [vspec(), vspec()], vspec(), [],
        SOME_VMEM, 1 << 18, 1 << 18,
    )(bias_table, bias_index)

    normed, empty = call(
        cap_norm_kernel, (sds((SLOT_TOKENS, D), bf16), sds((8, SLOT_TOKENS), f32)),
        [vspec()] * 2, (vspec(), vspec()), [],
        SOME_VMEM, 8 << 20, 3 << 20,
    )(arrived, gain)
    cap_result = call(
        cap_kernel, sds((SLOT_TOKENS, HW), bf16),
        [vspec()] * 3, vspec(), [VMEM((SLOT_TOKENS, 3 * HW), bf16)],
        SOME_VMEM, 1100 << 20, 4 << 20, 1 << 19,
    )(normed, empty, w_qkv)
    returned = exchange(cap_result.reshape(lon_count, MOST * TW, HW)).reshape(SLOT_TOKENS, HW)

    win_out = call(
        window_kernel, sds((RH * RW, HW), f32),
        [vspec()] * 8, vspec(),
        [
            VMEM((N_WIN * WTOK, D), bf16),
            VMEM((N_WIN * QROWS, D), bf16),
            VMEM((N_WIN * WTOK, 2 * HW), bf16),
            VMEM((N_WIN * QROWS, HW), bf16),
            VMEM((N_WIN * 128, 128), f32),
            VMEM((N_WIN * 128, 128), bf16),
            VMEM((N_WIN, QROWS, HW), f32),
            VMEM((2, 64, D), f32),
        ],
        SOME_VMEM, 2300 << 20, 6 << 20, 1 << 18,
    )(tokens, north, south, left, right, gain, bias, w_qkv)
    mixed = call(
        join_kernel, sds((RH * RW, HW), bf16),
        [vspec()] * 3, vspec(), [],
        8 << 20, 2 * CAP_TOKENS * SLOT_TOKENS * HW, 1 << 20,
    )(win_out, returned, undo)
    return mixed.reshape(RH, RW, HW)


def solution(mesh):
    placed = (P("lat", "lon", None), P(), P(), P(), P(), P(None, "lon", None, None))
    return jax.shard_map(
        layer, mesh=mesh, in_specs=placed, out_specs=P("lat", "lon", None), check_vma=False
    )
```

time: 62.8 us -> 63.6 us (1.013)
  the two profiles are of different devices: /device:TPU:1 before, /device:TPU:41 now
where the time goes in v2:
time: 63.6 us; the launch traced here: 62.7 us
  starting transfers between devices  35.6 us (56%)
  Pallas kernels  12 us (19%)
  waiting for transfers between devices  9.37 us (15%)
  local copies, waits for them, and re-layouts  5.52 us (9%)
    all_to_all x2, starting transfers between devices, exchange(): return lax.all_to_all(block, 'lon', split_axis=0, concat_axis=0, tiled=True)  20.6 us
    ppermute x1, starting transfers between devices, layer(): south = lax.ppermute(to_north, 'lat', up)  6.38 us
    unnamed x18, local copies, waits for them, and re-layouts  5.52 us
    all_to_all x2, waiting for transfers between devices, exchange(): return lax.all_to_all(block, 'lon', split_axis=0, concat_axis=0, tiled=True)  4.51 us
    ppermute x1, waiting for transfers between devices, layer(): right = lax.ppermute(head, 'lon', west)  4.16 us
    pallas_call x1, Pallas kernels, layer(): call(window_kernel, sds((RH * RW, HW), f32), [vspec()] * 8, vspec(), [VME...  3.53 us
    ppermute x1, starting transfers between devices, layer(): left = lax.ppermute(tail, 'lon', east)  3.5 us
    ppermute x1, starting transfers between devices, layer(): north = lax.ppermute(to_south, 'lat', down)  3.12 us
  transfers between devices with their start and end apart: 6, of which 3 were waited for; matrix products, arithmetic and copies ran while one was open for 0% of the time, Pallas kernels for 14%

profile of v2, /device:TPU:41, one launch (start us, length us, event | category | flops | bytes accessed | tf_op | source)
XLA Modules:
  0.0 62.7 jit_solution(413115860609246464)
XLA Ops:
  0.0 2.0 %shard_map.68 = bf16[256,1024]{1,0:T(8,128)(2,1)} custom-call(s32[2,4,1,8]{3,2,1,0:T(1,128)} %bitcast.9, bf16[8,32,1024]{2,1,0:T(8,128)(2,1)} %tokens_ref.1), custom_call_target="tpu_custom_call" | custom-call | flops 67108864 | bytes 1048576 | tf_op jit(solution)/shard_map/pallas_call | solution.py:351
  2.0 12.2 %all-to-all-start = ((bf16[32,8,1024]{2,1,0:T(8,128)(2,1)}), bf16[32,8,1024]{2,1,0:T(8,128)(2,1)S(1)}, u32[]{:S(2)}, u32[]{:S(2)}) async-start(bf16[32,8,1024]{2,1,0:T(8,128)(2,1)} %bitcast.13), calls=%async_computation | async-start | bytes 1048576 | tf_op jit(solution)/shard_map/all_to_all | solution.py:341
  14.2 0.0 copy-start
  14.2 1.0 %copy-done = bf16[8,32,1024]{2,1,0:T(8,128)(2,1)S(1)} copy-done((bf16[8,32,1024]{2,1,0:T(8,128)(2,1)S(1)}, bf16[8,32,1024]{2,1,0:T(8,128)(2,1)}, u32[]{:S(2)}) %copy-start) | copy-done | bytes 524312
  15.3 0.0 copy-start.2
  15.3 0.0 copy-start.4
  15.4 0.0 copy-start.1
  15.4 0.0 copy-start.6
  15.4 3.5 %collective-permute-start = (bf16[32,1024]{1,0:T(8,128)(2,1)S(1)}, bf16[32,1024]{1,0:T(8,128)(2,1)S(1)}, u32[]{:S(2)}, u32[]{:S(2)}) collective-permute-start(bf16[32,1024]{1,0:T(8,128)(2,1)S(1)} %get-tuple-element.11), channel_id=1, source_target_pairs={{0,1},{1,2},{2,3},{3,4},{4,5},{5,6},{6,7},{7,8},{8,9},{9,10},{10,1... | collective-permute-start | bytes 196616 | tf_op jit(solution)/shard_map/ppermute | solution.py:375
  18.9 1.9 %collective-permute-start.1 = (bf16[32,1024]{1,0:T(8,128)(2,1)S(1)}, bf16[32,1024]{1,0:T(8,128)(2,1)S(1)}, u32[]{:S(2)}, u32[]{:S(2)}) collective-permute-start(bf16[32,1024]{1,0:T(8,128)(2,1)S(1)} %get-tuple-element.12), channel_id=1, source_target_pairs={{1,0},{2,1},{3,2},{4,3},{5,4},{6,5},{7,6},{8,7},{9,8},{10,9},{11,1... | collective-permute-start | bytes 196616 | tf_op jit(solution)/shard_map/ppermute | solution.py:376
  20.8 0.7 %collective-permute-done.left_ref = bf16[32,1024]{1,0:T(8,128)(2,1)S(1)} collective-permute-done((bf16[32,1024]{1,0:T(8,128)(2,1)S(1)}, bf16[32,1024]{1,0:T(8,128)(2,1)S(1)}, u32[]{:S(2)}, u32[]{:S(2)}) %collective-permute-start) | collective-permute-done | bytes 65568 | tf_op jit(solution)/shard_map/ppermute | solution.py:375
  21.5 4.2 %collective-permute-done.1.right_ref = bf16[32,1024]{1,0:T(8,128)(2,1)S(1)} collective-permute-done((bf16[32,1024]{1,0:T(8,128)(2,1)S(1)}, bf16[32,1024]{1,0:T(8,128)(2,1)S(1)}, u32[]{:S(2)}, u32[]{:S(2)}) %collective-permute-start.1) | collective-permute-done | bytes 65568 | tf_op jit(solution)/shard_map/ppermute | solution.py:376
  25.7 0.9 %shard_map.65 = (bf16[160,1024]{1,0:T(8,128)(2,1)S(1)}, bf16[160,1024]{1,0:T(8,128)(2,1)S(1)}) custom-call(bf16[8,32,1024]{2,1,0:T(8,128)(2,1)S(1)} %copy-done, bf16[32,1024]{1,0:T(8,128)(2,1)S(1)} %collective-permute-done.left_ref, bf16[32,1024]{1,0:T(8,128)(2,1)S(1)} %collective-permute-done.1.right_ref), custom_call_target="tpu_custom_call" | custom-call | flops 1024 | bytes 1572864 | tf_op jit(solution)/shard_map/pallas_call | solution.py:383
  26.6 3.1 %collective-permute-start.2 = (bf16[160,1024]{1,0:T(8,128)(2,1)S(1)}, bf16[160,1024]{1,0:T(8,128)(2,1)S(1)}, u32[]{:S(2)}, u32[]{:S(2)}) collective-permute-start(bf16[160,1024]{1,0:T(8,128)(2,1)S(1)} %get-tuple-element.13), channel_id=1, source_target_pairs={{0,32},{32,64},{64,96},{96,128},{128,160},{160,192},{192,224},{224... | collective-permute-start | bytes 983048 | tf_op jit(solution)/shard_map/ppermute | solution.py:388
  29.7 6.4 %collective-permute-start.3 = (bf16[160,1024]{1,0:T(8,128)(2,1)S(1)}, bf16[160,1024]{1,0:T(8,128)(2,1)S(1)}, u32[]{:S(2)}, u32[]{:S(2)}) collective-permute-start(bf16[160,1024]{1,0:T(8,128)(2,1)S(1)} %get-tuple-element.14), channel_id=1, source_target_pairs={{32,0},{64,32},{96,64},{128,96},{160,128},{192,160},{224,192},{256... | collective-permute-start | bytes 983048 | tf_op jit(solution)/shard_map/ppermute | solution.py:389
  36.1 0.0 all-to-all-done
  36.1 0.0 copy-start.5
  36.2 0.7 %copy-done.5 = f32[1024]{0:T(1024)S(1)} copy-done((f32[1024]{0:T(1024)S(1)}, f32[1024]{0:T(1024)}, u32[]{:S(2)}) %copy-start.5) | copy-done | bytes 4120
  36.8 0.4 shard_map.69
  37.2 0.0 copy-start.7
  37.2 1.9 %copy-done.7 = bf16[1024,1536]{1,0:T(8,128)(2,1)S(1)} copy-done((bf16[1024,1536]{1,0:T(8,128)(2,1)S(1)}, bf16[1024,1536]{1,0:T(8,128)(2,1)}, u32[]{:S(2)}) %copy-start.7) | copy-done | bytes 3145752
  39.1 2.9 %shard_map.70 = bf16[256,512]{1,0:T(8,128)(2,1)} custom-call(bf16[256,1024]{1,0:T(8,128)(2,1)S(1)} %get-tuple-element.15.normed, f32[8,256]{1,0:T(8,128)S(1)} %get-tuple-element.16.empty_ref, bf16[1024,1536]{1,0:T(8,128)(2,1)S(1)} %copy-done.7), custom_call_target="tpu_custom_call" | custom-call | flops 1153433600 | bytes 4194304 | tf_op jit(solution)/shard_map/pallas_call | solution.py:402
  42.0 8.4 %all-to-all-start.1 = ((bf16[32,8,512]{2,1,0:T(8,128)(2,1)}), bf16[32,8,512]{2,1,0:T(8,128)(2,1)S(1)}, u32[]{:S(2)}, u32[]{:S(2)}) async-start(bf16[32,8,512]{2,1,0:T(8,128)(2,1)} %bitcast.4), calls=%async_computation.1 | async-start | bytes 524288 | tf_op jit(solution)/shard_map/all_to_all | solution.py:341
  50.4 0.8 %shard_map.71.undo_ref = bf16[128,256]{1,0:T(8,128)(2,1)S(1)} custom-call(s32[2,4,1,8]{3,2,1,0:T(1,128)S(1)} %bitcast.10), custom_call_target="tpu_custom_call" | custom-call | flops 262144 | bytes 65536 | tf_op jit(solution)/shard_map/pallas_call | solution.py:377
  51.3 0.5 shard_map.66.bias
  51.8 0.0 collective-permute-done.2.north_ref
  51.8 0.0 collective-permute-done.3.south_ref
  51.8 0.0 copy-start.8
  51.8 1.9 %copy-done.8 = bf16[1024,1536]{1,0:T(8,128)(2,1)S(1)} copy-done((bf16[1024,1536]{1,0:T(8,128)(2,1)S(1)}, bf16[1024,1536]{1,0:T(8,128)(2,1)}, u32[]{:S(2)}) %copy-start.8) | copy-done | bytes 3145752
  53.7 3.5 %shard_map.67.win_ref = f32[256,512]{1,0:T(8,128)S(1)} custom-call(bf16[8,32,1024]{2,1,0:T(8,128)(2,1)S(1)} %copy-done.1, bf16[160,1024]{1,0:T(8,128)(2,1)S(1)} %collective-permute-done.2.north_ref, bf16[160,1024]{1,0:T(8,128)(2,1)S(1)} %collective-permute-done.3.south_ref, bf16[32,1024]{1,0:T(8,128)(2,1)S(1)} %collective-permute-done.left_ref, ...), custom_call_target="tpu_custom_call" | custom-call | flops 2411724800 | bytes 6291456 | tf_op jit(solution)/shard_map/pallas_call | solution.py:409
  57.2 4.5 %all-to-all-done.1 = bf16[32,8,512]{2,1,0:T(8,128)(2,1)S(1)} async-done(((bf16[32,8,512]{2,1,0:T(8,128)(2,1)}), bf16[32,8,512]{2,1,0:T(8,128)(2,1)S(1)}, u32[]{:S(2)}, u32[]{:S(2)}) %all-to-all-start.1) | async-done | bytes 262176 | tf_op jit(solution)/shard_map/all_to_all | solution.py:341
  61.8 0.9 %shard_map.72 = bf16[256,512]{1,0:T(8,128)(2,1)} custom-call(f32[256,512]{1,0:T(8,128)S(1)} %shard_map.67.win_ref, bf16[256,512]{1,0:T(8,128)(2,1)S(1)} %bitcast.8, bf16[128,256]{1,0:T(8,128)(2,1)S(1)} %shard_map.71.undo_ref), custom_call_target="tpu_custom_call" | custom-call | flops 33554432 | bytes 1048576 | tf_op jit(solution)/shard_map/pallas_call | solution.py:424
  (7 shorter events, 0.1 us)
Async XLA Ops:
  2.0 34.1 %all-to-all-start = ((bf16[32,8,1024]{2,1,0:T(8,128)(2,1)}), bf16[32,8,1024]{2,1,0:T(8,128)(2,1)S(1)}, u32[]{:S(2)}, u32[]{:S(2)}) async-start(bf16[32,8,1024]{2,1,0:T(8,128)(2,1)} %bitcast.13), calls=%async_computation | async-start | bytes 1048576 | tf_op jit(solution)/shard_map/all_to_all | solution.py:341
  14.2 1.0 %copy-start = (bf16[8,32,1024]{2,1,0:T(8,128)(2,1)S(1)}, bf16[8,32,1024]{2,1,0:T(8,128)(2,1)}, u32[]{:S(2)}) copy-start(bf16[8,32,1024]{2,1,0:T(8,128)(2,1)} %tokens_ref.1) | copy-start | bytes 1572868
  15.3 35.2 %copy-start.3 = (s32[2,8,4,1]{1,3,2,0:T(1,128)S(1)}, s32[2,8,4,1]{1,3,2,0:T(1,128)}, u32[]{:S(2)}) copy-start(s32[2,8,4,1]{1,3,2,0:T(1,128)} %param.11) | copy-start | bytes 772
  15.3 35.9 %copy-start.2 = (s32[64,64]{1,0:T(8,128)S(1)}, s32[64,64]{1,0:T(8,128)}, u32[]{:S(2)}) copy-start(s32[64,64]{1,0:T(8,128)} %index_ref.1) | copy-start | bytes 49156
  15.3 35.9 %copy-start.4 = (f32[8,225]{1,0:T(8,128)S(1)}, f32[8,225]{1,0:T(8,128)}, u32[]{:S(2)}) copy-start(f32[8,225]{1,0:T(8,128)} %table_ref.1) | copy-start | bytes 21604
  15.4 36.4 %copy-start.1 = (bf16[8,32,1024]{2,1,0:T(8,128)(2,1)S(1)}, bf16[8,32,1024]{2,1,0:T(8,128)(2,1)}, u32[]{:S(2)}) copy-start(bf16[8,32,1024]{2,1,0:T(8,128)(2,1)} %tokens_ref.1) | copy-start | bytes 1572868
  15.4 36.4 %copy-start.6 = (f32[1024]{0:T(1024)S(1)}, f32[1024]{0:T(1024)}, u32[]{:S(2)}) copy-start(f32[1024]{0:T(1024)} %param.7) | copy-start | bytes 12292
  15.4 6.1 %collective-permute-start = (bf16[32,1024]{1,0:T(8,128)(2,1)S(1)}, bf16[32,1024]{1,0:T(8,128)(2,1)S(1)}, u32[]{:S(2)}, u32[]{:S(2)}) collective-permute-start(bf16[32,1024]{1,0:T(8,128)(2,1)S(1)} %get-tuple-element.11), channel_id=1, source_target_pairs={{0,1},{1,2},{2,3},{3,4},{4,5},{5,6},{6,7},{7,8},{8,9},{9,10},{10,1... | collective-permute-start | bytes 196616 | tf_op jit(solution)/shard_map/ppermute | solution.py:375
  18.9 6.8 %collective-permute-start.1 = (bf16[32,1024]{1,0:T(8,128)(2,1)S(1)}, bf16[32,1024]{1,0:T(8,128)(2,1)S(1)}, u32[]{:S(2)}, u32[]{:S(2)}) collective-permute-start(bf16[32,1024]{1,0:T(8,128)(2,1)S(1)} %get-tuple-element.12), channel_id=1, source_target_pairs={{1,0},{2,1},{3,2},{4,3},{5,4},{6,5},{7,6},{8,7},{9,8},{10,9},{11,1... | collective-permute-start | bytes 196616 | tf_op jit(solution)/shard_map/ppermute | solution.py:376
  26.6 25.2 %collective-permute-start.2 = (bf16[160,1024]{1,0:T(8,128)(2,1)S(1)}, bf16[160,1024]{1,0:T(8,128)(2,1)S(1)}, u32[]{:S(2)}, u32[]{:S(2)}) collective-permute-start(bf16[160,1024]{1,0:T(8,128)(2,1)S(1)} %get-tuple-element.13), channel_id=1, source_target_pairs={{0,32},{32,64},{64,96},{96,128},{128,160},{160,192},{192,224},{224... | collective-permute-start | bytes 983048 | tf_op jit(solution)/shard_map/ppermute | solution.py:388
  29.7 22.0 %collective-permute-start.3 = (bf16[160,1024]{1,0:T(8,128)(2,1)S(1)}, bf16[160,1024]{1,0:T(8,128)(2,1)S(1)}, u32[]{:S(2)}, u32[]{:S(2)}) collective-permute-start(bf16[160,1024]{1,0:T(8,128)(2,1)S(1)} %get-tuple-element.14), channel_id=1, source_target_pairs={{32,0},{64,32},{96,64},{128,96},{160,128},{192,160},{224,192},{256... | collective-permute-start | bytes 983048 | tf_op jit(solution)/shard_map/ppermute | solution.py:389
  36.1 0.7 %copy-start.5 = (f32[1024]{0:T(1024)S(1)}, f32[1024]{0:T(1024)}, u32[]{:S(2)}) copy-start(f32[1024]{0:T(1024)} %param.7) | copy-start | bytes 12292
  37.2 1.9 %copy-start.7 = (bf16[1024,1536]{1,0:T(8,128)(2,1)S(1)}, bf16[1024,1536]{1,0:T(8,128)(2,1)}, u32[]{:S(2)}) copy-start(bf16[1024,1536]{1,0:T(8,128)(2,1)} %w_ref.3) | copy-start | bytes 9437188
  42.0 19.7 %all-to-all-start.1 = ((bf16[32,8,512]{2,1,0:T(8,128)(2,1)}), bf16[32,8,512]{2,1,0:T(8,128)(2,1)S(1)}, u32[]{:S(2)}, u32[]{:S(2)}) async-start(bf16[32,8,512]{2,1,0:T(8,128)(2,1)} %bitcast.4), calls=%async_computation.1 | async-start | bytes 524288 | tf_op jit(solution)/shard_map/all_to_all | solution.py:341
  51.8 1.9 %copy-start.8 = (bf16[1024,1536]{1,0:T(8,128)(2,1)S(1)}, bf16[1024,1536]{1,0:T(8,128)(2,1)}, u32[]{:S(2)}) copy-start(bf16[1024,1536]{1,0:T(8,128)(2,1)} %w_ref.3) | copy-start | bytes 9437188

commit v3 on v2

--- a/solution.py
+++ b/solution.py
@@ -34,6 +34,7 @@
 EMPTY_ABOVE = 64.0
 
 ALL_VMEM = 67043328
+PACK_VMEM = ALL_VMEM - 409600
 SOME_VMEM = 24 << 20
 
 VMEM = pltpu.VMEM
@@ -75,7 +76,10 @@
 PACK_STEP = 64
 
 
-def pack_kernel(names_ref, tokens_ref, send_ref, group_ref, rows, out, name_sem, sem, out_sem):
+def pack_kernel(
+    names_ref, tokens_ref, send_ref, hot_ref, head_ref, tail_ref,
+    group_ref, rows, edge, out, name_sem, sem, edge_sem, out_sem,
+):
     north = lax.axis_index("lat") == 0
     pole = jnp.where(north, 0, 1)
     start = jnp.where(north, 0, RH - CAP)
@@ -83,6 +87,12 @@
     names.start()
     copy = pltpu.make_async_copy(tokens_ref.at[pl.ds(start, CAP)], rows, sem)
     copy.start()
+    edges = [
+        pltpu.make_async_copy(tokens_ref.at[:, pl.ds(k * (RW - 8), 8)], edge.at[k], edge_sem.at[k])
+        for k in range(2)
+    ]
+    for each in edges:
+        each.start()
     names.wait()
     lane = lax.broadcasted_iota(jnp.int32, (8, CAP_TOKENS), 1)
     slot = slot_rows(group_ref, pole, lane)[0:1]
@@ -94,84 +104,63 @@
         hit = lax.broadcasted_iota(jnp.int32, (PACK_STEP, CAP_TOKENS), 0) + n * PACK_STEP == slot
         hot = hit.astype(jnp.float32)
         filled = jnp.max(hot, axis=1, keepdims=True) > 0.5
-        moved = jnp.dot(hot.astype(jnp.bfloat16), x, preferred_element_type=jnp.float32)
+        hot = hot.astype(jnp.bfloat16)
+        hot_ref[at, :] = hot
+        moved = jnp.dot(hot, x, preferred_element_type=jnp.float32)
         out[at, :] = jnp.where(filled, moved, EMPTY).astype(jnp.bfloat16)
         sends.append(pltpu.make_async_copy(out.at[at], send_ref.at[at], out_sem.at[n]))
         sends[n].start()
-    for send in sends:
-        send.wait()
-
-
-def edge_kernel(own_ref, head_ref, tail_ref):
+    for each in edges:
+        each.wait()
     lower = lax.broadcasted_iota(jnp.int32, (8, D), 0) < HALF
     for r in range(0, RH, 4):
         heads, tails = [], []
         for i in (r, r + 2):
-            first = [own_ref[i + k, 0:8].astype(jnp.float32) for k in range(2)]
-            last = [own_ref[i + k, 24:32].astype(jnp.float32) for k in range(2)]
+            first = [edge[0, i + k].astype(jnp.float32) for k in range(2)]
+            last = [edge[1, i + k].astype(jnp.float32) for k in range(2)]
             heads.append(jnp.where(lower, first[0], pltpu.roll(first[1], HALF, 0)))
             tails.append(jnp.where(lower, pltpu.roll(last[0], HALF, 0), last[1]))
         head_ref[r * 4 : r * 4 + 16] = jnp.concatenate(heads, 0).astype(jnp.bfloat16)
         tail_ref[r * 4 : r * 4 + 16] = jnp.concatenate(tails, 0).astype(jnp.bfloat16)
-
-
-def undo_kernel(names_ref, undo_ref, group_ref, name_sem):
-    names = pltpu.make_async_copy(names_ref, group_ref, name_sem)
-    names.start()
-    lat = lax.axis_index("lat")
-    north = lat == 0
-    polar = north | (lat == lax.axis_size("lat") - 1)
-    pole = jnp.where(north, 0, 1)
-    token = lax.broadcasted_iota(jnp.int32, (CAP_TOKENS, 128), 0)
-    names.wait()
-    slot = slot_rows(group_ref, pole, token)
-    slot = jnp.where(polar, slot, -1)
-    for i in range(0, SLOT_TOKENS, 128):
-        hit = lax.broadcasted_iota(jnp.int32, (CAP_TOKENS, 128), 1) + i == slot
-        undo_ref[:, i : i + 128] = hit.astype(jnp.float32).astype(jnp.bfloat16)
+    for send in sends:
+        send.wait()
 
 
 RIM_SIDE = HALF * HALF
 RIM = HALF * RW + 2 * RIM_SIDE
 
 
-def rim_kernel(own_ref, left_ref, right_ref, up_ref, down_ref, sem):
-    copies = []
-    for n, (out, first) in enumerate(((up_ref, 0), (down_ref, RH - HALF))):
+def row_kernel(own_ref, gain_in, up_ref, down_ref, gain_ref):
+    gain_ref[...] = gain_in[...]
+    for out, first in ((up_ref, 0), (down_ref, RH - HALF)):
         for r in range(HALF):
-            at = pl.ds(r * RW, RW)
-            copies.append(pltpu.make_async_copy(own_ref.at[first + r], out.at[at], sem.at[n * 6 + r]))
+            out[r * RW : r * RW + RW] = own_ref[first + r]
+
+
+def rim_kernel(left_ref, right_ref, up_in, down_in, up_ref, down_ref):
+    for out, first in ((up_ref, 0), (down_ref, RH - HALF)):
         for k, side in enumerate((left_ref, right_ref)):
-            at = pl.ds(HALF * RW + k * RIM_SIDE, RIM_SIDE)
-            part = side.at[pl.ds(first * HALF, RIM_SIDE)]
-            copies.append(pltpu.make_async_copy(part, out.at[at], sem.at[n * 6 + 4 + k]))
-    for copy in copies:
-        copy.start()
-    for copy in copies:
-        copy.wait()
+            at = HALF * RW + k * RIM_SIDE
+            out[at : at + RIM_SIDE] = side[first * HALF : first * HALF + RIM_SIDE]
 
 
 W_STEP = 256
 
 
-def cap_norm_kernel(x_ref, gain_ref, normed, empty_ref):
+def cap_kernel(x_ref, gain_ref, w_ref, out_ref, normed, qkv):
+    n = SLOT_TOKENS
     gain = gain_ref[...]
-    for i in range(0, SLOT_TOKENS, 32):
+    for i in range(0, n, 32):
         normed[i : i + 32] = norm_rows(x_ref[i : i + 32].astype(jnp.float32), gain).astype(jnp.bfloat16)
     pick = (lax.broadcasted_iota(jnp.int32, (8, 128), 1) == 0).astype(jnp.bfloat16)
     first = lax.dot_general(
         pick, x_ref[:, 0:128], (((1,), (1,)), ((), ())), preferred_element_type=jnp.float32
     )
-    empty_ref[...] = jnp.where(first > EMPTY_ABOVE, masked_score, 0.0)
-
-
-def cap_kernel(normed, empty_ref, w_ref, out_ref, qkv):
-    n = SLOT_TOKENS
-    empty = empty_ref[0:1]
-    for j in range(0, 3 * HW, W_STEP):
-        w = w_ref[:, j : j + W_STEP]
-        part = jnp.dot(normed[...], w, preferred_element_type=jnp.float32)
-        qkv[:, j : j + W_STEP] = part.astype(jnp.bfloat16)
+    empty = jnp.where(first[0:1] > EMPTY_ABOVE, masked_score, 0.0)
+    for j in range(3 * HW // W_STEP):
+        at = slice(j * W_STEP, j * W_STEP + W_STEP)
+        part = jnp.dot(normed[...], w_ref[:, at], preferred_element_type=jnp.float32)
+        qkv[:, at] = part.astype(jnp.bfloat16)
     low = lax.broadcasted_iota(jnp.int32, (n, 128), 1) < HD
     for pair in range(HEADS // 2):
         at = pair * 128
@@ -190,8 +179,17 @@
         out_ref[:, at : at + 128] = jnp.where(low, mixed[0], mixed[1]).astype(jnp.bfloat16)
 
 
-def bias_kernel(table_ref, index_ref, bias_ref):
+def window_kernel(
+    own_ref, north_ref, south_ref, left_ref, right_ref, gain_ref, table_ref, index_ref, hot_ref, w_ref,
+    out_ref, undo_ref, xs, xq, kv, qs, bias, scores, weights, wout, edges,
+):
+    gain = gain_ref[...]
     lat = lax.axis_index("lat")
+
+    polar = (lat == 0) | (lat == lax.axis_size("lat") - 1)
+    undo = jnp.transpose(hot_ref[...].astype(jnp.float32))
+    undo_ref[...] = jnp.where(polar, undo, 0.0).astype(jnp.bfloat16)
+
     lane = lax.broadcasted_iota(jnp.int32, (8, 128), 1)
     first = lane < WTOK
     key_row = (lane % WTOK) // WIN
@@ -217,14 +215,7 @@
                     found.append(jnp.where(high, hi, lo))
                 value = jnp.where(first, found[0], found[1])
                 to = a * 128 + h4 * QROWS + i
-                bias_ref[to : to + 8, :] = jnp.where(off, masked_score, value)
-
-
-def window_kernel(
-    own_ref, north_ref, south_ref, left_ref, right_ref, gain_ref, bias, w_ref,
-    out_ref, xs, xq, kv, qs, scores, weights, wout, edges,
-):
-    gain = gain_ref[...]
+                bias[to : to + 8, :] = jnp.where(off, masked_score, value)
 
     for side, ref in enumerate((left_ref, right_ref)):
         at = HALF * RW + side * RIM_SIDE
@@ -261,13 +252,13 @@
                 to = (a * WIN_B + b) * QROWS + (wr % HALF) * WIN
                 xq[to : to + 16] = both
 
-    for j in range(0, 3 * HW, W_STEP):
-        w = w_ref[:, j : j + W_STEP]
-        if j < HW:
-            qs[:, j : j + W_STEP] = jnp.dot(xq[...], w, preferred_element_type=jnp.float32).astype(jnp.bfloat16)
+    for j in range(3 * HW // W_STEP):
+        at = slice(j * W_STEP, j * W_STEP + W_STEP)
+        if j * W_STEP < HW:
+            qs[:, at] = jnp.dot(xq[...], w_ref[:, at], preferred_element_type=jnp.float32).astype(jnp.bfloat16)
         else:
-            part = jnp.dot(xs[...], w, preferred_element_type=jnp.float32)
-            kv[:, j - HW : j - HW + W_STEP] = part.astype(jnp.bfloat16)
+            to = slice(j * W_STEP - HW, j * W_STEP - HW + W_STEP)
+            kv[:, to] = jnp.dot(xs[...], w_ref[:, at], preferred_element_type=jnp.float32).astype(jnp.bfloat16)
 
     head = lax.broadcasted_iota(jnp.int32, (QROWS, HW), 1) // HD % 4
     blank = jnp.zeros((WTOK, HW // 2), jnp.bfloat16)
@@ -325,7 +316,7 @@
     return jax.ShapeDtypeStruct(shape, dtype)
 
 
-def call(kernel, outs, ins, out_specs, scratch, vmem, flops, nbytes, trans=0):
+def call(kernel, outs, ins, out_specs, scratch, vmem, flops, nbytes, trans=0, aliases=None):
     return pl.pallas_call(
         kernel,
         out_shape=outs,
@@ -333,6 +324,7 @@
         out_specs=out_specs,
         scratch_shapes=scratch,
         compiler_params=pltpu.CompilerParams(vmem_limit_bytes=vmem),
+        input_output_aliases=aliases or {},
         cost_estimate=pl.CostEstimate(flops=flops, bytes_accessed=nbytes, transcendentals=trans),
     )
 
@@ -348,18 +340,22 @@
     gain = ln_gain.reshape(1, D)
     groups = cap_group.transpose(0, 2, 3, 1)
 
-    packed = call(
-        pack_kernel, sds((SLOT_TOKENS, D), bf16),
-        [aspec(), hspec()], hspec(),
+    side = sds((RH * HALF, D), bf16)
+    packed, hot, head, tail = call(
+        pack_kernel,
+        (sds((SLOT_TOKENS, D), bf16), sds((SLOT_TOKENS, CAP_TOKENS), bf16), side, side),
+        [aspec(), hspec()], (hspec(),) + (vspec(),) * 3,
         [
             SMEM((2, CAP, 1, TILE_COLS), jnp.int32),
             VMEM((CAP, RW, D), bf16),
+            VMEM((2, RH, 8, D), bf16),
             VMEM((SLOT_TOKENS, D), bf16),
             pltpu.SemaphoreType.DMA,
             pltpu.SemaphoreType.DMA,
+            pltpu.SemaphoreType.DMA((2,)),
             pltpu.SemaphoreType.DMA((SLOT_TOKENS // PACK_STEP,)),
         ],
-        ALL_VMEM, 2 * SLOT_TOKENS * CAP_TOKENS * D, 1 << 20,
+        PACK_VMEM, 2 * SLOT_TOKENS * CAP_TOKENS * D, 1 << 20,
     )(groups, tokens)
     arrived = exchange(packed.reshape(lon_count, MOST * TW, D)).reshape(SLOT_TOKENS, D)
 
@@ -367,60 +363,45 @@
     up = [(i + 1, i) for i in range(lat_count - 1)]
     east = [(i, (i + 1) % lon_count) for i in range(lon_count)]
     west = [((i + 1) % lon_count, i) for i in range(lon_count)]
-    side = sds((RH * HALF, D), bf16)
-    head, tail = call(
-        edge_kernel, (side, side), [vspec()], (vspec(), vspec()), [],
-        SOME_VMEM, 1 << 18, 3 << 18,
-    )(tokens)
     left = lax.ppermute(tail, "lon", east)
     right = lax.ppermute(head, "lon", west)
-    undo = call(
-        undo_kernel, sds((CAP_TOKENS, SLOT_TOKENS), bf16), [aspec()], vspec(),
-        [SMEM((2, CAP, 1, TILE_COLS), jnp.int32), pltpu.SemaphoreType.DMA],
-        SOME_VMEM, 1 << 18, 1 << 16,
-    )(groups)
     rim = sds((RIM, D), bf16)
+    to_north, to_south, gain = call(
+        row_kernel, (rim, rim, sds((1, D), f32)), [vspec()] * 2, (vspec(),) * 3, [],
+        SOME_VMEM, 1 << 10, 1 << 20,
+    )(tokens, gain)
     to_north, to_south = call(
-        rim_kernel, (rim, rim), [aspec(), aspec(), aspec()], (vspec(), vspec()),
-        [pltpu.SemaphoreType.DMA((12,))],
-        SOME_VMEM, 1 << 10, 3 << 19,
-    )(tokens, left, right)
+        rim_kernel, (rim, rim), [vspec()] * 4, (vspec(), vspec()), [],
+        SOME_VMEM, 1 << 10, 1 << 18, aliases={2: 0, 3: 1},
+    )(left, right, to_north, to_south)
     north = lax.ppermute(to_south, "lat", down)
     south = lax.ppermute(to_north, "lat", up)
 
-    bias = call(
-        bias_kernel, sds((2 * 128, 128), f32),
-        [vspec(), vspec()], vspec(), [],
-        SOME_VMEM, 1 << 18, 1 << 18,
-    )(bias_table, bias_index)
-
-    normed, empty = call(
-        cap_norm_kernel, (sds((SLOT_TOKENS, D), bf16), sds((8, SLOT_TOKENS), f32)),
-        [vspec()] * 2, (vspec(), vspec()), [],
-        SOME_VMEM, 8 << 20, 3 << 20,
-    )(arrived, gain)
     cap_result = call(
         cap_kernel, sds((SLOT_TOKENS, HW), bf16),
-        [vspec()] * 3, vspec(), [VMEM((SLOT_TOKENS, 3 * HW), bf16)],
+        [vspec()] * 3, vspec(),
+        [VMEM((SLOT_TOKENS, D), bf16), VMEM((SLOT_TOKENS, 3 * HW), bf16)],
         SOME_VMEM, 1100 << 20, 4 << 20, 1 << 19,
-    )(normed, empty, w_qkv)
+    )(arrived, gain, w_qkv)
     returned = exchange(cap_result.reshape(lon_count, MOST * TW, HW)).reshape(SLOT_TOKENS, HW)
 
-    win_out = call(
-        window_kernel, sds((RH * RW, HW), f32),
-        [vspec()] * 8, vspec(),
+    win_out, undo = call(
+        window_kernel,
+        (sds((RH * RW, HW), f32), sds((CAP_TOKENS, SLOT_TOKENS), bf16)),
+        [vspec()] * 10, (vspec(), vspec()),
         [
             VMEM((N_WIN * WTOK, D), bf16),
             VMEM((N_WIN * QROWS, D), bf16),
             VMEM((N_WIN * WTOK, 2 * HW), bf16),
             VMEM((N_WIN * QROWS, HW), bf16),
+            VMEM((2 * 128, 128), f32),
             VMEM((N_WIN * 128, 128), f32),
             VMEM((N_WIN * 128, 128), bf16),
             VMEM((N_WIN, QROWS, HW), f32),
             VMEM((2, 64, D), f32),
         ],
         SOME_VMEM, 2300 << 20, 6 << 20, 1 << 18,
-    )(tokens, north, south, left, right, gain, bias, w_qkv)
+    )(tokens, north, south, left, right, gain, bias_table, bias_index, hot, w_qkv)
     mixed = call(
         join_kernel, sds((RH * RW, HW), bf16),
         [vspec()] * 3, vspec(), [],
@@ -431,6 +412,4 @@
 
 def solution(mesh):
     placed = (P("lat", "lon", None), P(), P(), P(), P(), P(None, "lon", None, None))
-    return jax.shard_map(
-        layer, mesh=mesh, in_specs=placed, out_specs=P("lat", "lon", None), check_vma=False
-    )
+    return jax.shard_map(layer, mesh=mesh, in_specs=placed, out_specs=P("lat", "lon", None), check_vma=False)

time: 63.6 us -> 61.9 us (0.973)
  Pallas kernels: 12 us -> 10.4 us
    pallas_call x7 -> x4, Pallas kernels: 8.16 us -> 6.48 us  [the longest x1 3.62 us: layer(): call(window_kernel, (sds((RH * RW, HW), f32), sds((CAP_TOKENS, SLOT_TOKEN...]
    all_to_all x2, waiting for transfers between devices: 4.51 us -> 5.74 us  [exchange(): return lax.all_to_all(block, 'lon', split_axis=0, concat_axis=0, tiled=True)]
    ppermute x1, waiting for transfers between devices: 4.16 us -> 3.4 us  [layer(): right = lax.ppermute(head, 'lon', west)]
    unnamed x18 -> x16, local copies, waits for them, and re-layouts: 5.52 us -> 5.52 us
  transfers between devices with their start and end apart: 6 -> 6, of which waited for: 3 -> 3; matrix products, arithmetic and copies ran while one was open for 0% -> 0% of each run, Pallas kernels for 14% -> 11%
where the time goes in v3:
time: 61.9 us; the launch traced here: 60.9 us
  starting transfers between devices  35.3 us (57%)
  Pallas kernels  10.4 us (17%)
  waiting for transfers between devices  9.47 us (15%)
  local copies, waits for them, and re-layouts  5.52 us (9%)
    all_to_all x2, starting transfers between devices, exchange(): return lax.all_to_all(block, 'lon', split_axis=0, concat_axis=0, tiled=True)  20.5 us
    ppermute x1, starting transfers between devices, layer(): south = lax.ppermute(to_north, 'lat', up)  6.38 us
    all_to_all x2, waiting for transfers between devices, exchange(): return lax.all_to_all(block, 'lon', split_axis=0, concat_axis=0, tiled=True)  5.74 us
    unnamed x16, local copies, waits for them, and re-layouts  5.52 us
    pallas_call x1, Pallas kernels, layer(): call(window_kernel, (sds((RH * RW, HW), f32), sds((CAP_TOKENS, SLOT_TOKEN...  3.62 us
    ppermute x1, waiting for transfers between devices, layer(): right = lax.ppermute(head, 'lon', west)  3.4 us
    ppermute x1, starting transfers between devices, layer(): left = lax.ppermute(tail, 'lon', east)  3.37 us
    ppermute x1, starting transfers between devices, layer(): north = lax.ppermute(to_south, 'lat', down)  3.12 us
  transfers between devices with their start and end apart: 6, of which 3 were waited for; matrix products, arithmetic and copies ran while one was open for 0% of the time, Pallas kernels for 11%

profile of v3, /device:TPU:41, one launch (start us, length us, event | category | flops | bytes accessed | tf_op | source)
XLA Modules:
  0.0 60.9 jit_solution(6757629639820472613)
XLA Ops:
  0.0 2.8 %shard_map.64 = (bf16[256,1024]{1,0:T(8,128)(2,1)}, bf16[256,128]{1,0:T(8,128)(2,1)}, bf16[32,1024]{1,0:T(8,128)(2,1)}, bf16[32,1024]{1,0:T(8,128)(2,1)}) custom-call(s32[2,4,1,8]{3,2,1,0:T(1,128)} %bitcast.11, bf16[8,32,1024]{2,1,0:T(8,128)(2,1)} %own_ref.3), custom_call_target="tpu_custom_call" | custom-call | flops 67108864 | bytes 1048576 | tf_op jit(solution)/shard_map/pallas_call | solution.py:344
  2.8 0.0 copy-start.1
  2.8 0.0 copy-start.5
  2.8 0.0 copy-start.6
  2.9 0.0 copy-start.7
  2.9 12.4 %all-to-all-start = ((bf16[32,8,1024]{2,1,0:T(8,128)(2,1)}), bf16[32,8,1024]{2,1,0:T(8,128)(2,1)S(1)}, u32[]{:S(2)}, u32[]{:S(2)}) async-start(bf16[32,8,1024]{2,1,0:T(8,128)(2,1)} %bitcast.10), calls=%async_computation | async-start | bytes 1048576 | tf_op jit(solution)/shard_map/all_to_all | solution.py:333
  15.2 3.4 %collective-permute-start = (bf16[32,1024]{1,0:T(8,128)(2,1)}, bf16[32,1024]{1,0:T(8,128)(2,1)S(1)}, u32[]{:S(2)}, u32[]{:S(2)}) collective-permute-start(bf16[32,1024]{1,0:T(8,128)(2,1)} %get-tuple-element.16), channel_id=1, source_target_pairs={{0,1},{1,2},{2,3},{3,4},{4,5},{5,6},{6,7},{7,8},{8,9},{9,10},{10,1... | collective-permute-start | bytes 196616 | tf_op jit(solution)/shard_map/ppermute | solution.py:366
  18.6 1.9 %collective-permute-start.1 = (bf16[32,1024]{1,0:T(8,128)(2,1)}, bf16[32,1024]{1,0:T(8,128)(2,1)S(1)}, u32[]{:S(2)}, u32[]{:S(2)}) collective-permute-start(bf16[32,1024]{1,0:T(8,128)(2,1)} %get-tuple-element.17), channel_id=1, source_target_pairs={{1,0},{2,1},{3,2},{4,3},{5,4},{6,5},{7,6},{8,7},{9,8},{10,9},{11,1... | collective-permute-start | bytes 196616 | tf_op jit(solution)/shard_map/ppermute | solution.py:367
  20.5 0.0 copy-start
  20.6 1.0 %copy-done = bf16[8,32,1024]{2,1,0:T(8,128)(2,1)S(1)} copy-done((bf16[8,32,1024]{2,1,0:T(8,128)(2,1)S(1)}, bf16[8,32,1024]{2,1,0:T(8,128)(2,1)}, u32[]{:S(2)}) %copy-start) | copy-done | bytes 524312
  21.6 0.0 copy-start.2
  21.6 0.7 %copy-done.2 = f32[1024]{0:T(1024)S(1)} copy-done((f32[1024]{0:T(1024)S(1)}, f32[1024]{0:T(1024)}, u32[]{:S(2)}) %copy-start.2) | copy-done | bytes 4120
  22.3 0.3 collective-permute-done.left_ref
  22.6 3.4 %collective-permute-done.1.right_ref = bf16[32,1024]{1,0:T(8,128)(2,1)S(1)} collective-permute-done((bf16[32,1024]{1,0:T(8,128)(2,1)}, bf16[32,1024]{1,0:T(8,128)(2,1)S(1)}, u32[]{:S(2)}, u32[]{:S(2)}) %collective-permute-start.1) | collective-permute-done | bytes 65568 | tf_op jit(solution)/shard_map/ppermute | solution.py:367
  26.1 3.1 %collective-permute-start.2 = (bf16[160,1024]{1,0:T(8,128)(2,1)S(1)}, bf16[160,1024]{1,0:T(8,128)(2,1)S(1)}, u32[]{:S(2)}, u32[]{:S(2)}) collective-permute-start(bf16[160,1024]{1,0:T(8,128)(2,1)S(1)} %get-tuple-element.20), channel_id=1, source_target_pairs={{0,32},{32,64},{64,96},{96,128},{128,160},{160,192},{192,224},{224... | collective-permute-start | bytes 983048 | tf_op jit(solution)/shard_map/ppermute | solution.py:377
  29.2 6.4 %collective-permute-start.3 = (bf16[160,1024]{1,0:T(8,128)(2,1)S(1)}, bf16[160,1024]{1,0:T(8,128)(2,1)S(1)}, u32[]{:S(2)}, u32[]{:S(2)}) collective-permute-start(bf16[160,1024]{1,0:T(8,128)(2,1)S(1)} %get-tuple-element.21), channel_id=1, source_target_pairs={{32,0},{64,32},{96,64},{128,96},{160,128},{192,160},{224,192},{256... | collective-permute-start | bytes 983048 | tf_op jit(solution)/shard_map/ppermute | solution.py:378
  35.6 0.0 all-to-all-done
  35.6 0.0 copy-start.3
  35.6 1.9 %copy-done.3 = bf16[1024,1536]{1,0:T(8,128)(2,1)S(1)} copy-done((bf16[1024,1536]{1,0:T(8,128)(2,1)S(1)}, bf16[1024,1536]{1,0:T(8,128)(2,1)}, u32[]{:S(2)}) %copy-start.3) | copy-done | bytes 3145752
  37.5 3.0 %shard_map.68 = bf16[256,512]{1,0:T(8,128)(2,1)} custom-call(bf16[256,1024]{1,0:T(8,128)(2,1)S(1)} %bitcast.8, f32[1,1024]{1,0:T(1,128)S(1)} %get-tuple-element.22.gain_ref, bf16[1024,1536]{1,0:T(8,128)(2,1)S(1)} %copy-done.3), custom_call_target="tpu_custom_call" | custom-call | flops 1153433600 | bytes 4194304 | tf_op jit(solution)/shard_map/pallas_call | solution.py:380
  40.5 8.1 %all-to-all-start.1 = ((bf16[32,8,512]{2,1,0:T(8,128)(2,1)}), bf16[32,8,512]{2,1,0:T(8,128)(2,1)S(1)}, u32[]{:S(2)}, u32[]{:S(2)}) async-start(bf16[32,8,512]{2,1,0:T(8,128)(2,1)} %bitcast.4), calls=%async_computation.1 | async-start | bytes 524288 | tf_op jit(solution)/shard_map/all_to_all | solution.py:333
  48.7 0.0 collective-permute-done.2.north_ref
  48.7 0.0 collective-permute-done.3.south_ref
  48.7 0.0 copy-done.1
  48.7 0.0 copy-done.5
  48.7 0.0 copy-done.6
  48.7 0.0 copy-done.7
  48.7 0.0 copy-start.4
  48.7 1.9 %copy-done.4 = bf16[1024,1536]{1,0:T(8,128)(2,1)S(1)} copy-done((bf16[1024,1536]{1,0:T(8,128)(2,1)S(1)}, bf16[1024,1536]{1,0:T(8,128)(2,1)}, u32[]{:S(2)}) %copy-start.4) | copy-done | bytes 3145752
  50.6 3.6 %shard_map.67 = (f32[256,512]{1,0:T(8,128)S(1)}, bf16[128,256]{1,0:T(8,128)(2,1)S(1)}) custom-call(bf16[8,32,1024]{2,1,0:T(8,128)(2,1)S(1)} %copy-done.1, bf16[160,1024]{1,0:T(8,128)(2,1)S(1)} %collective-permute-done.2.north_ref, bf16[160,1024]{1,0:T(8,128)(2,1)S(1)} %collective-permute-done.3.south_ref, ...), custom_call_target="tpu_custom_call" | custom-call | flops 2411724800 | bytes 6291456 | tf_op jit(solution)/shard_map/pallas_call | solution.py:388
  54.2 5.7 %all-to-all-done.1 = bf16[32,8,512]{2,1,0:T(8,128)(2,1)S(1)} async-done(((bf16[32,8,512]{2,1,0:T(8,128)(2,1)}), bf16[32,8,512]{2,1,0:T(8,128)(2,1)S(1)}, u32[]{:S(2)}, u32[]{:S(2)}) %all-to-all-start.1) | async-done | bytes 262176 | tf_op jit(solution)/shard_map/all_to_all | solution.py:333
  60.0 0.9 %shard_map.69 = bf16[256,512]{1,0:T(8,128)(2,1)} custom-call(f32[256,512]{1,0:T(8,128)S(1)} %get-tuple-element.24.win_ref, bf16[256,512]{1,0:T(8,128)(2,1)S(1)} %bitcast.7, bf16[128,256]{1,0:T(8,128)(2,1)S(1)} %get-tuple-element.26.undo_ref), custom_call_target="tpu_custom_call" | custom-call | flops 33554432 | bytes 1048576 | tf_op jit(solution)/shard_map/pallas_call | solution.py:405
  (2 shorter events, 0.0 us)
Async XLA Ops:
  2.8 45.9 %copy-start.1 = (bf16[8,32,1024]{2,1,0:T(8,128)(2,1)S(1)}, bf16[8,32,1024]{2,1,0:T(8,128)(2,1)}, u32[]{:S(2)}) copy-start(bf16[8,32,1024]{2,1,0:T(8,128)(2,1)} %own_ref.3) | copy-start | bytes 1572868
  2.8 45.9 %copy-start.5 = (bf16[256,128]{1,0:T(8,128)(2,1)S(1)}, bf16[256,128]{1,0:T(8,128)(2,1)}, u32[]{:S(2)}) copy-start(bf16[256,128]{1,0:T(8,128)(2,1)} %get-tuple-element.23.hot_ref) | copy-start | bytes 196612
  2.8 45.9 %copy-start.6 = (s32[64,64]{1,0:T(8,128)S(1)}, s32[64,64]{1,0:T(8,128)}, u32[]{:S(2)}) copy-start(s32[64,64]{1,0:T(8,128)} %index_ref.1) | copy-start | bytes 49156
  2.9 45.9 %copy-start.7 = (f32[8,225]{1,0:T(8,128)S(1)}, f32[8,225]{1,0:T(8,128)}, u32[]{:S(2)}) copy-start(f32[8,225]{1,0:T(8,128)} %table_ref.1) | copy-start | bytes 21604
  2.9 32.7 %all-to-all-start = ((bf16[32,8,1024]{2,1,0:T(8,128)(2,1)}), bf16[32,8,1024]{2,1,0:T(8,128)(2,1)S(1)}, u32[]{:S(2)}, u32[]{:S(2)}) async-start(bf16[32,8,1024]{2,1,0:T(8,128)(2,1)} %bitcast.10), calls=%async_computation | async-start | bytes 1048576 | tf_op jit(solution)/shard_map/all_to_all | solution.py:333
  15.2 7.4 %collective-permute-start = (bf16[32,1024]{1,0:T(8,128)(2,1)}, bf16[32,1024]{1,0:T(8,128)(2,1)S(1)}, u32[]{:S(2)}, u32[]{:S(2)}) collective-permute-start(bf16[32,1024]{1,0:T(8,128)(2,1)} %get-tuple-element.16), channel_id=1, source_target_pairs={{0,1},{1,2},{2,3},{3,4},{4,5},{5,6},{6,7},{7,8},{8,9},{9,10},{10,1... | collective-permute-start | bytes 196616 | tf_op jit(solution)/shard_map/ppermute | solution.py:366
  18.6 7.4 %collective-permute-start.1 = (bf16[32,1024]{1,0:T(8,128)(2,1)}, bf16[32,1024]{1,0:T(8,128)(2,1)S(1)}, u32[]{:S(2)}, u32[]{:S(2)}) collective-permute-start(bf16[32,1024]{1,0:T(8,128)(2,1)} %get-tuple-element.17), channel_id=1, source_target_pairs={{1,0},{2,1},{3,2},{4,3},{5,4},{6,5},{7,6},{8,7},{9,8},{10,9},{11,1... | collective-permute-start | bytes 196616 | tf_op jit(solution)/shard_map/ppermute | solution.py:367
  20.5 1.0 %copy-start = (bf16[8,32,1024]{2,1,0:T(8,128)(2,1)S(1)}, bf16[8,32,1024]{2,1,0:T(8,128)(2,1)}, u32[]{:S(2)}) copy-start(bf16[8,32,1024]{2,1,0:T(8,128)(2,1)} %own_ref.3) | copy-start | bytes 1572868
  21.6 0.7 %copy-start.2 = (f32[1024]{0:T(1024)S(1)}, f32[1024]{0:T(1024)}, u32[]{:S(2)}) copy-start(f32[1024]{0:T(1024)} %param.7) | copy-start | bytes 12292
  26.1 22.6 %collective-permute-start.2 = (bf16[160,1024]{1,0:T(8,128)(2,1)S(1)}, bf16[160,1024]{1,0:T(8,128)(2,1)S(1)}, u32[]{:S(2)}, u32[]{:S(2)}) collective-permute-start(bf16[160,1024]{1,0:T(8,128)(2,1)S(1)} %get-tuple-element.20), channel_id=1, source_target_pairs={{0,32},{32,64},{64,96},{96,128},{128,160},{160,192},{192,224},{224... | collective-permute-start | bytes 983048 | tf_op jit(solution)/shard_map/ppermute | solution.py:377
  29.2 19.5 %collective-permute-start.3 = (bf16[160,1024]{1,0:T(8,128)(2,1)S(1)}, bf16[160,1024]{1,0:T(8,128)(2,1)S(1)}, u32[]{:S(2)}, u32[]{:S(2)}) collective-permute-start(bf16[160,1024]{1,0:T(8,128)(2,1)S(1)} %get-tuple-element.21), channel_id=1, source_target_pairs={{32,0},{64,32},{96,64},{128,96},{160,128},{192,160},{224,192},{256... | collective-permute-start | bytes 983048 | tf_op jit(solution)/shard_map/ppermute | solution.py:378
  35.6 1.9 %copy-start.3 = (bf16[1024,1536]{1,0:T(8,128)(2,1)S(1)}, bf16[1024,1536]{1,0:T(8,128)(2,1)}, u32[]{:S(2)}) copy-start(bf16[1024,1536]{1,0:T(8,128)(2,1)} %w_ref.3) | copy-start | bytes 9437188
  40.5 19.5 %all-to-all-start.1 = ((bf16[32,8,512]{2,1,0:T(8,128)(2,1)}), bf16[32,8,512]{2,1,0:T(8,128)(2,1)S(1)}, u32[]{:S(2)}, u32[]{:S(2)}) async-start(bf16[32,8,512]{2,1,0:T(8,128)(2,1)} %bitcast.4), calls=%async_computation.1 | async-start | bytes 524288 | tf_op jit(solution)/shard_map/all_to_all | solution.py:333
  48.7 1.9 %copy-start.4 = (bf16[1024,1536]{1,0:T(8,128)(2,1)S(1)}, bf16[1024,1536]{1,0:T(8,128)(2,1)}, u32[]{:S(2)}) copy-start(bf16[1024,1536]{1,0:T(8,128)(2,1)} %w_ref.3) | copy-start | bytes 9437188

commit v4 on v3

--- a/solution.py
+++ b/solution.py
@@ -77,8 +77,8 @@
 
 
 def pack_kernel(
-    names_ref, tokens_ref, send_ref, hot_ref, head_ref, tail_ref,
-    group_ref, rows, edge, out, name_sem, sem, edge_sem, out_sem,
+    names_ref, tokens_ref, send_ref, hot_out, head_out, tail_out,
+    group_ref, rows, edge, out, hot_ref, head_ref, tail_ref, name_sem, sem, edge_sem, out_sem, side_sem,
 ):
     north = lax.axis_index("lat") == 0
     pole = jnp.where(north, 0, 1)
@@ -110,6 +110,8 @@
         out[at, :] = jnp.where(filled, moved, EMPTY).astype(jnp.bfloat16)
         sends.append(pltpu.make_async_copy(out.at[at], send_ref.at[at], out_sem.at[n]))
         sends[n].start()
+    sends.append(pltpu.make_async_copy(hot_ref, hot_out, side_sem.at[0]))
+    sends[-1].start()
     for each in edges:
         each.wait()
     lower = lax.broadcasted_iota(jnp.int32, (8, D), 0) < HALF
@@ -122,26 +124,21 @@
             tails.append(jnp.where(lower, pltpu.roll(last[0], HALF, 0), last[1]))
         head_ref[r * 4 : r * 4 + 16] = jnp.concatenate(heads, 0).astype(jnp.bfloat16)
         tail_ref[r * 4 : r * 4 + 16] = jnp.concatenate(tails, 0).astype(jnp.bfloat16)
+    for n, (part, to) in enumerate(((head_ref, head_out), (tail_ref, tail_out))):
+        sends.append(pltpu.make_async_copy(part, to, side_sem.at[n + 1]))
+        sends[-1].start()
     for send in sends:
         send.wait()
 
 
-RIM_SIDE = HALF * HALF
-RIM = HALF * RW + 2 * RIM_SIDE
-
-
-def row_kernel(own_ref, gain_in, up_ref, down_ref, gain_ref):
+SIDE = HALF * HALF
+
+
+def corner_kernel(left_ref, right_ref, gain_in, up_ref, down_ref, gain_ref):
     gain_ref[...] = gain_in[...]
-    for out, first in ((up_ref, 0), (down_ref, RH - HALF)):
-        for r in range(HALF):
-            out[r * RW : r * RW + RW] = own_ref[first + r]
-
-
-def rim_kernel(left_ref, right_ref, up_in, down_in, up_ref, down_ref):
-    for out, first in ((up_ref, 0), (down_ref, RH - HALF)):
+    for out, first in ((up_ref, 0), (down_ref, (RH - HALF) * HALF)):
         for k, side in enumerate((left_ref, right_ref)):
-            at = HALF * RW + k * RIM_SIDE
-            out[at : at + RIM_SIDE] = side[first * HALF : first * HALF + RIM_SIDE]
+            out[k * SIDE : k * SIDE + SIDE] = side[first : first + SIDE]
 
 
 W_STEP = 256
@@ -180,7 +177,7 @@
 
 
 def window_kernel(
-    own_ref, north_ref, south_ref, left_ref, right_ref, gain_ref, table_ref, index_ref, hot_ref, w_ref,
+    own_ref, north_ref, south_ref, north_side, south_side, left_ref, right_ref, gain_ref, table_ref, index_ref, hot_ref, w_ref,
     out_ref, undo_ref, xs, xq, kv, qs, bias, scores, weights, wout, edges,
 ):
     gain = gain_ref[...]
@@ -218,11 +215,11 @@
                 bias[to : to + 8, :] = jnp.where(off, masked_score, value)
 
     for side, ref in enumerate((left_ref, right_ref)):
-        at = HALF * RW + side * RIM_SIDE
+        at = side * SIDE
         for to, x in (
-            (0, north_ref[at : at + RIM_SIDE]),
-            (RIM_SIDE, ref[...]),
-            (3 * RIM_SIDE, south_ref[at : at + RIM_SIDE]),
+            (0, north_side[at : at + SIDE]),
+            (SIDE, ref[...]),
+            (3 * SIDE, south_side[at : at + SIDE]),
         ):
             edges[side, to : to + x.shape[0]] = norm_rows(x.astype(jnp.float32), gain)
     lower = lax.broadcasted_iota(jnp.int32, (8, D), 0) < HALF
@@ -232,8 +229,7 @@
         blocks = [[], []]
         for k in range(2):
             ref, i = rows[r + k]
-            x = ref[i] if ref is own_ref else ref[i * RW : i * RW + RW]
-            normed = norm_rows(x.astype(jnp.float32), gain)
+            normed = norm_rows(ref[i].astype(jnp.float32), gain)
             turned = [pltpu.roll(normed[j * 8 : j * 8 + 8], HALF, 0) for j in range(4)]
             lo = edges[0, r * 4 : r * 4 + 8]
             hi = edges[1, r * 4 : r * 4 + 8]
@@ -344,16 +340,20 @@
     packed, hot, head, tail = call(
         pack_kernel,
         (sds((SLOT_TOKENS, D), bf16), sds((SLOT_TOKENS, CAP_TOKENS), bf16), side, side),
-        [aspec(), hspec()], (hspec(),) + (vspec(),) * 3,
+        [aspec(), hspec()], (hspec(),) * 4,
         [
             SMEM((2, CAP, 1, TILE_COLS), jnp.int32),
             VMEM((CAP, RW, D), bf16),
             VMEM((2, RH, 8, D), bf16),
             VMEM((SLOT_TOKENS, D), bf16),
+            VMEM((SLOT_TOKENS, CAP_TOKENS), bf16),
+            VMEM((RH * HALF, D), bf16),
+            VMEM((RH * HALF, D), bf16),
             pltpu.SemaphoreType.DMA,
             pltpu.SemaphoreType.DMA,
             pltpu.SemaphoreType.DMA((2,)),
             pltpu.SemaphoreType.DMA((SLOT_TOKENS // PACK_STEP,)),
+            pltpu.SemaphoreType.DMA((3,)),
         ],
         PACK_VMEM, 2 * SLOT_TOKENS * CAP_TOKENS * D, 1 << 20,
     )(groups, tokens)
@@ -363,19 +363,18 @@
     up = [(i + 1, i) for i in range(lat_count - 1)]
     east = [(i, (i + 1) % lon_count) for i in range(lon_count)]
     west = [((i + 1) % lon_count, i) for i in range(lon_count)]
+    tied, _ = lax.optimization_barrier((tokens, packed))
+    north = lax.ppermute(tied[RH - HALF :], "lat", down)
+    south = lax.ppermute(tied[:HALF], "lat", up)
     left = lax.ppermute(tail, "lon", east)
     right = lax.ppermute(head, "lon", west)
-    rim = sds((RIM, D), bf16)
+    pair = sds((2 * SIDE, D), bf16)
     to_north, to_south, gain = call(
-        row_kernel, (rim, rim, sds((1, D), f32)), [vspec()] * 2, (vspec(),) * 3, [],
-        SOME_VMEM, 1 << 10, 1 << 20,
-    )(tokens, gain)
-    to_north, to_south = call(
-        rim_kernel, (rim, rim), [vspec()] * 4, (vspec(), vspec()), [],
-        SOME_VMEM, 1 << 10, 1 << 18, aliases={2: 0, 3: 1},
-    )(left, right, to_north, to_south)
-    north = lax.ppermute(to_south, "lat", down)
-    south = lax.ppermute(to_north, "lat", up)
+        corner_kernel, (pair, pair, sds((1, D), f32)), [vspec()] * 3, (vspec(),) * 3, [],
+        SOME_VMEM, 1 << 10, 1 << 19,
+    )(left, right, gain)
+    north_side = lax.ppermute(to_south, "lat", down)
+    south_side = lax.ppermute(to_north, "lat", up)
 
     cap_result = call(
         cap_kernel, sds((SLOT_TOKENS, HW), bf16),
@@ -388,7 +387,7 @@
     win_out, undo = call(
         window_kernel,
         (sds((RH * RW, HW), f32), sds((CAP_TOKENS, SLOT_TOKENS), bf16)),
-        [vspec()] * 10, (vspec(), vspec()),
+        [vspec()] * 12, (vspec(), vspec()),
         [
             VMEM((N_WIN * WTOK, D), bf16),
             VMEM((N_WIN * QROWS, D), bf16),
@@ -401,7 +400,7 @@
             VMEM((2, 64, D), f32),
         ],
         SOME_VMEM, 2300 << 20, 6 << 20, 1 << 18,
-    )(tokens, north, south, left, right, gain, bias_table, bias_index, hot, w_qkv)
+    )(tokens, north, south, north_side, south_side, left, right, gain, bias_table, bias_index, hot, w_qkv)
     mixed = call(
         join_kernel, sds((RH * RW, HW), bf16),
         [vspec()] * 3, vspec(), [],

time: 61.9 us -> 76 us (1.23)
  the two profiles are of different devices: /device:TPU:41 before, /device:TPU:57 now
where the time goes in v4:
time: 76 us; the launch traced here: 75.4 us
  starting transfers between devices  38.7 us (51%)
  waiting for transfers between devices  22.4 us (29%)
  Pallas kernels  9.66 us (13%)
  local copies, waits for them, and re-layouts  4.52 us (6%)
    all_to_all x2, starting transfers between devices, exchange(): return lax.all_to_all(block, 'lon', split_axis=0, concat_axis=0, tiled=True)  17.2 us
    ppermute x1, waiting for transfers between devices, layer(): north_side = lax.ppermute(to_south, 'lat', down)  11.1 us
    ppermute x1, starting transfers between devices, layer(): south_side = lax.ppermute(to_north, 'lat', up)  6.37 us
    ppermute x1, starting transfers between devices, layer(): south = lax.ppermute(tied[:HALF], 'lat', up)  5.96 us
    all_to_all x2, waiting for transfers between devices, exchange(): return lax.all_to_all(block, 'lon', split_axis=0, concat_axis=0, tiled=True)  5.71 us
    unnamed x14, local copies, waits for them, and re-layouts  4.48 us
    pallas_call x1, Pallas kernels, layer(): call(window_kernel, (sds((RH * RW, HW), f32), sds((CAP_TOKENS, SLOT_TOKEN...  3.56 us
    ppermute x1, waiting for transfers between devices, layer(): right = lax.ppermute(head, 'lon', west)  3.4 us
  transfers between devices with their start and end apart: 8, of which 4 were waited for; matrix products, arithmetic and copies ran while one was open for 0% of the time, Pallas kernels for 5%

profile of v4, /device:TPU:57, one launch (start us, length us, event | category | flops | bytes accessed | tf_op | source)
XLA Modules:
  0.0 75.4 jit_solution(14310312324131233876)
XLA Ops:
  0.0 2.2 %shard_map.64 = (bf16[256,1024]{1,0:T(8,128)(2,1)}, bf16[256,128]{1,0:T(8,128)(2,1)}, bf16[32,1024]{1,0:T(8,128)(2,1)}, bf16[32,1024]{1,0:T(8,128)(2,1)}) custom-call(s32[2,4,1,8]{3,2,1,0:T(1,128)} %bitcast.11, bf16[8,32,1024]{2,1,0:T(8,128)(2,1)} %own_ref.1), custom_call_target="tpu_custom_call" | custom-call | flops 67108864 | bytes 1048576 | tf_op jit(solution)/shard_map/pallas_call | solution.py:340
  2.2 0.0 copy-start
  2.2 0.0 copy-start.4
  2.2 0.0 copy-start.5
  2.2 0.0 copy-start.6
  2.3 12.4 %all-to-all-start = ((bf16[32,8,1024]{2,1,0:T(8,128)(2,1)}), bf16[32,8,1024]{2,1,0:T(8,128)(2,1)S(1)}, u32[]{:S(2)}, u32[]{:S(2)}) async-start(bf16[32,8,1024]{2,1,0:T(8,128)(2,1)} %bitcast.10), calls=%async_computation | async-start | bytes 1048576 | tf_op jit(solution)/shard_map/all_to_all | solution.py:329
  14.6 3.4 %collective-permute-start.2 = (bf16[32,1024]{1,0:T(8,128)(2,1)}, bf16[32,1024]{1,0:T(8,128)(2,1)S(1)}, u32[]{:S(2)}, u32[]{:S(2)}) collective-permute-start(bf16[32,1024]{1,0:T(8,128)(2,1)} %get-tuple-element.17), channel_id=1, source_target_pairs={{0,1},{1,2},{2,3},{3,4},{4,5},{5,6},{6,7},{7,8},{8,9},{9,10},{10,1... | collective-permute-start | bytes 196616 | tf_op jit(solution)/shard_map/ppermute | solution.py:369
  18.0 1.9 %collective-permute-start.3 = (bf16[32,1024]{1,0:T(8,128)(2,1)}, bf16[32,1024]{1,0:T(8,128)(2,1)S(1)}, u32[]{:S(2)}, u32[]{:S(2)}) collective-permute-start(bf16[32,1024]{1,0:T(8,128)(2,1)} %get-tuple-element.18), channel_id=1, source_target_pairs={{1,0},{2,1},{3,2},{4,3},{5,4},{6,5},{7,6},{8,7},{9,8},{10,9},{11,1... | collective-permute-start | bytes 196616 | tf_op jit(solution)/shard_map/ppermute | solution.py:370
  19.9 2.1 %collective-permute-done.2.left_ref = bf16[32,1024]{1,0:T(8,128)(2,1)S(1)} collective-permute-done((bf16[32,1024]{1,0:T(8,128)(2,1)}, bf16[32,1024]{1,0:T(8,128)(2,1)S(1)}, u32[]{:S(2)}, u32[]{:S(2)}) %collective-permute-start.2) | collective-permute-done | bytes 65568 | tf_op jit(solution)/shard_map/ppermute | solution.py:369
  22.0 3.4 %collective-permute-done.3.right_ref = bf16[32,1024]{1,0:T(8,128)(2,1)S(1)} collective-permute-done((bf16[32,1024]{1,0:T(8,128)(2,1)}, bf16[32,1024]{1,0:T(8,128)(2,1)S(1)}, u32[]{:S(2)}, u32[]{:S(2)}) %collective-permute-start.3) | collective-permute-done | bytes 65568 | tf_op jit(solution)/shard_map/ppermute | solution.py:370
  25.4 0.7 copy-done.1
  26.1 5.7 %all-to-all-done = bf16[32,8,1024]{2,1,0:T(8,128)(2,1)S(1)} async-done(((bf16[32,8,1024]{2,1,0:T(8,128)(2,1)}), bf16[32,8,1024]{2,1,0:T(8,128)(2,1)S(1)}, u32[]{:S(2)}, u32[]{:S(2)}) %all-to-all-start) | async-done | bytes 524320 | tf_op jit(solution)/shard_map/all_to_all | solution.py:329
  31.9 1.9 %copy-done.2 = bf16[1024,1536]{1,0:T(8,128)(2,1)S(1)} copy-done((bf16[1024,1536]{1,0:T(8,128)(2,1)S(1)}, bf16[1024,1536]{1,0:T(8,128)(2,1)}, u32[]{:S(2)}) %copy-start.2) | copy-done | bytes 3145752
  33.7 3.0 %shard_map.67 = bf16[256,512]{1,0:T(8,128)(2,1)} custom-call(bf16[256,1024]{1,0:T(8,128)(2,1)S(1)} %bitcast.8, f32[1,1024]{1,0:T(1,128)S(1)} %get-tuple-element.21.gain_ref, bf16[1024,1536]{1,0:T(8,128)(2,1)S(1)} %copy-done.2), custom_call_target="tpu_custom_call" | custom-call | flops 1153433600 | bytes 4194304 | tf_op jit(solution)/shard_map/pallas_call | solution.py:379
  36.7 4.9 %all-to-all-start.1 = ((bf16[32,8,512]{2,1,0:T(8,128)(2,1)}), bf16[32,8,512]{2,1,0:T(8,128)(2,1)S(1)}, u32[]{:S(2)}, u32[]{:S(2)}) async-start(bf16[32,8,512]{2,1,0:T(8,128)(2,1)} %bitcast.4), calls=%async_computation.1 | async-start | bytes 524288 | tf_op jit(solution)/shard_map/all_to_all | solution.py:329
  41.6 0.0 copy-done
  41.7 6.0 %collective-permute-start.1 = (bf16[4,32,1024]{2,1,0:T(8,128)(2,1)S(1)}, bf16[4,32,1024]{2,1,0:T(8,128)(2,1)S(1)}, u32[]{:S(2)}, u32[]{:S(2)}) collective-permute-start(bf16[4,32,1024]{2,1,0:T(8,128)(2,1)S(1)} %get-tuple-element.25), channel_id=1, source_target_pairs={{32,0},{64,32},{96,64},{128,96},{160,128},{192,160},{224,192},{256... | collective-permute-start | bytes 786440 | tf_op jit(solution)/shard_map/ppermute | solution.py:368
  47.6 1.9 %collective-permute-start = (bf16[4,32,1024]{2,1,0:T(8,128)(2,1)S(1)}, bf16[4,32,1024]{2,1,0:T(8,128)(2,1)S(1)}, u32[]{:S(2)}, u32[]{:S(2)}) collective-permute-start(bf16[4,32,1024]{2,1,0:T(8,128)(2,1)S(1)} %get-tuple-element.26), channel_id=1, source_target_pairs={{0,32},{32,64},{64,96},{96,128},{128,160},{160,192},{192,224},{224... | collective-permute-start | bytes 786440 | tf_op jit(solution)/shard_map/ppermute | solution.py:367
  49.6 1.9 %collective-permute-start.4 = (bf16[32,1024]{1,0:T(8,128)(2,1)S(1)}, bf16[32,1024]{1,0:T(8,128)(2,1)S(1)}, u32[]{:S(2)}, u32[]{:S(2)}) collective-permute-start(bf16[32,1024]{1,0:T(8,128)(2,1)S(1)} %get-tuple-element.19), channel_id=1, source_target_pairs={{0,32},{32,64},{64,96},{96,128},{128,160},{160,192},{192,224},{224... | collective-permute-start | bytes 196616 | tf_op jit(solution)/shard_map/ppermute | solution.py:376
  51.5 6.4 %collective-permute-start.5 = (bf16[32,1024]{1,0:T(8,128)(2,1)S(1)}, bf16[32,1024]{1,0:T(8,128)(2,1)S(1)}, u32[]{:S(2)}, u32[]{:S(2)}) collective-permute-start(bf16[32,1024]{1,0:T(8,128)(2,1)S(1)} %get-tuple-element.20), channel_id=1, source_target_pairs={{32,0},{64,32},{96,64},{128,96},{160,128},{192,160},{224,192},{256... | collective-permute-start | bytes 196616 | tf_op jit(solution)/shard_map/ppermute | solution.py:377
  57.9 11.1 %collective-permute-done.4.north_side = bf16[32,1024]{1,0:T(8,128)(2,1)S(1)} collective-permute-done((bf16[32,1024]{1,0:T(8,128)(2,1)S(1)}, bf16[32,1024]{1,0:T(8,128)(2,1)S(1)}, u32[]{:S(2)}, u32[]{:S(2)}) %collective-permute-start.4) | collective-permute-done | bytes 65568 | tf_op jit(solution)/shard_map/ppermute | solution.py:376
  69.0 0.0 collective-permute-done.5.south_side
  69.0 0.0 collective-permute-done.1.south_ref
  69.0 0.0 collective-permute-done.north_ref
  69.0 0.0 copy-done.4
  69.0 0.0 copy-done.5
  69.0 0.0 copy-done.6
  69.1 0.0 copy-start.3
  69.1 1.9 %copy-done.3 = bf16[1024,1536]{1,0:T(8,128)(2,1)S(1)} copy-done((bf16[1024,1536]{1,0:T(8,128)(2,1)S(1)}, bf16[1024,1536]{1,0:T(8,128)(2,1)}, u32[]{:S(2)}) %copy-start.3) | copy-done | bytes 3145752
  71.0 3.6 %shard_map.66 = (f32[256,512]{1,0:T(8,128)S(1)}, bf16[128,256]{1,0:T(8,128)(2,1)S(1)}) custom-call(bf16[8,32,1024]{2,1,0:T(8,128)(2,1)S(1)} %copy-done, bf16[4,32,1024]{2,1,0:T(8,128)(2,1)S(1)} %collective-permute-done.north_ref, bf16[4,32,1024]{2,1,0:T(8,128)(2,1)S(1)} %collective-permute-done.1.south_ref, ...), custom_call_target="tpu_custom_call" | custom-call | flops 2411724800 | bytes 6291456 | tf_op jit(solution)/shard_map/pallas_call | solution.py:387
  74.5 0.0 all-to-all-done.1
  74.5 0.9 %shard_map.68 = bf16[256,512]{1,0:T(8,128)(2,1)} custom-call(f32[256,512]{1,0:T(8,128)S(1)} %get-tuple-element.23.win_ref, bf16[256,512]{1,0:T(8,128)(2,1)S(1)} %bitcast.7, bf16[128,256]{1,0:T(8,128)(2,1)S(1)} %get-tuple-element.24.undo_ref), custom_call_target="tpu_custom_call" | custom-call | flops 33554432 | bytes 1048576 | tf_op jit(solution)/shard_map/pallas_call | solution.py:404
  (4 shorter events, 0.0 us)
Async XLA Ops:
  2.2 39.4 %copy-start = (bf16[8,32,1024]{2,1,0:T(8,128)(2,1)S(1)}, bf16[8,32,1024]{2,1,0:T(8,128)(2,1)}, u32[]{:S(2)}) copy-start(bf16[8,32,1024]{2,1,0:T(8,128)(2,1)} %own_ref.1) | copy-start | bytes 1572868
  2.2 66.8 %copy-start.4 = (bf16[256,128]{1,0:T(8,128)(2,1)S(1)}, bf16[256,128]{1,0:T(8,128)(2,1)}, u32[]{:S(2)}) copy-start(bf16[256,128]{1,0:T(8,128)(2,1)} %get-tuple-element.22.hot_ref) | copy-start | bytes 196612
  2.2 66.8 %copy-start.5 = (s32[64,64]{1,0:T(8,128)S(1)}, s32[64,64]{1,0:T(8,128)}, u32[]{:S(2)}) copy-start(s32[64,64]{1,0:T(8,128)} %index_ref.1) | copy-start | bytes 49156
  2.2 66.8 %copy-start.6 = (f32[8,225]{1,0:T(8,128)S(1)}, f32[8,225]{1,0:T(8,128)}, u32[]{:S(2)}) copy-start(f32[8,225]{1,0:T(8,128)} %table_ref.1) | copy-start | bytes 21604
  2.3 29.6 %all-to-all-start = ((bf16[32,8,1024]{2,1,0:T(8,128)(2,1)}), bf16[32,8,1024]{2,1,0:T(8,128)(2,1)S(1)}, u32[]{:S(2)}, u32[]{:S(2)}) async-start(bf16[32,8,1024]{2,1,0:T(8,128)(2,1)} %bitcast.10), calls=%async_computation | async-start | bytes 1048576 | tf_op jit(solution)/shard_map/all_to_all | solution.py:329
  14.6 7.4 %collective-permute-start.2 = (bf16[32,1024]{1,0:T(8,128)(2,1)}, bf16[32,1024]{1,0:T(8,128)(2,1)S(1)}, u32[]{:S(2)}, u32[]{:S(2)}) collective-permute-start(bf16[32,1024]{1,0:T(8,128)(2,1)} %get-tuple-element.17), channel_id=1, source_target_pairs={{0,1},{1,2},{2,3},{3,4},{4,5},{5,6},{6,7},{7,8},{8,9},{9,10},{10,1... | collective-permute-start | bytes 196616 | tf_op jit(solution)/shard_map/ppermute | solution.py:369
  18.0 7.4 %collective-permute-start.3 = (bf16[32,1024]{1,0:T(8,128)(2,1)}, bf16[32,1024]{1,0:T(8,128)(2,1)S(1)}, u32[]{:S(2)}, u32[]{:S(2)}) collective-permute-start(bf16[32,1024]{1,0:T(8,128)(2,1)} %get-tuple-element.18), channel_id=1, source_target_pairs={{1,0},{2,1},{3,2},{4,3},{5,4},{6,5},{7,6},{8,7},{9,8},{10,9},{11,1... | collective-permute-start | bytes 196616 | tf_op jit(solution)/shard_map/ppermute | solution.py:370
  25.4 0.7 copy-start.1
  31.9 1.9 %copy-start.2 = (bf16[1024,1536]{1,0:T(8,128)(2,1)S(1)}, bf16[1024,1536]{1,0:T(8,128)(2,1)}, u32[]{:S(2)}) copy-start(bf16[1024,1536]{1,0:T(8,128)(2,1)} %w_ref.3) | copy-start | bytes 9437188
  36.7 37.8 %all-to-all-start.1 = ((bf16[32,8,512]{2,1,0:T(8,128)(2,1)}), bf16[32,8,512]{2,1,0:T(8,128)(2,1)S(1)}, u32[]{:S(2)}, u32[]{:S(2)}) async-start(bf16[32,8,512]{2,1,0:T(8,128)(2,1)} %bitcast.4), calls=%async_computation.1 | async-start | bytes 524288 | tf_op jit(solution)/shard_map/all_to_all | solution.py:329
  41.7 27.3 %collective-permute-start.1 = (bf16[4,32,1024]{2,1,0:T(8,128)(2,1)S(1)}, bf16[4,32,1024]{2,1,0:T(8,128)(2,1)S(1)}, u32[]{:S(2)}, u32[]{:S(2)}) collective-permute-start(bf16[4,32,1024]{2,1,0:T(8,128)(2,1)S(1)} %get-tuple-element.25), channel_id=1, source_target_pairs={{32,0},{64,32},{96,64},{128,96},{160,128},{192,160},{224,192},{256... | collective-permute-start | bytes 786440 | tf_op jit(solution)/shard_map/ppermute | solution.py:368
  47.6 21.4 %collective-permute-start = (bf16[4,32,1024]{2,1,0:T(8,128)(2,1)S(1)}, bf16[4,32,1024]{2,1,0:T(8,128)(2,1)S(1)}, u32[]{:S(2)}, u32[]{:S(2)}) collective-permute-start(bf16[4,32,1024]{2,1,0:T(8,128)(2,1)S(1)} %get-tuple-element.26), channel_id=1, source_target_pairs={{0,32},{32,64},{64,96},{96,128},{128,160},{160,192},{192,224},{224... | collective-permute-start | bytes 786440 | tf_op jit(solution)/shard_map/ppermute | solution.py:367
  49.6 19.4 %collective-permute-start.4 = (bf16[32,1024]{1,0:T(8,128)(2,1)S(1)}, bf16[32,1024]{1,0:T(8,128)(2,1)S(1)}, u32[]{:S(2)}, u32[]{:S(2)}) collective-permute-start(bf16[32,1024]{1,0:T(8,128)(2,1)S(1)} %get-tuple-element.19), channel_id=1, source_target_pairs={{0,32},{32,64},{64,96},{96,128},{128,160},{160,192},{192,224},{224... | collective-permute-start | bytes 196616 | tf_op jit(solution)/shard_map/ppermute | solution.py:376
  51.5 17.5 %collective-permute-start.5 = (bf16[32,1024]{1,0:T(8,128)(2,1)S(1)}, bf16[32,1024]{1,0:T(8,128)(2,1)S(1)}, u32[]{:S(2)}, u32[]{:S(2)}) collective-permute-start(bf16[32,1024]{1,0:T(8,128)(2,1)S(1)} %get-tuple-element.20), channel_id=1, source_target_pairs={{32,0},{64,32},{96,64},{128,96},{160,128},{192,160},{224,192},{256... | collective-permute-start | bytes 196616 | tf_op jit(solution)/shard_map/ppermute | solution.py:377
  69.1 1.9 %copy-start.3 = (bf16[1024,1536]{1,0:T(8,128)(2,1)S(1)}, bf16[1024,1536]{1,0:T(8,128)(2,1)}, u32[]{:S(2)}) copy-start(bf16[1024,1536]{1,0:T(8,128)(2,1)} %w_ref.3) | copy-start | bytes 9437188

commit v5 on v4

--- a/solution.py
+++ b/solution.py
@@ -76,10 +76,7 @@
 PACK_STEP = 64
 
 
-def pack_kernel(
-    names_ref, tokens_ref, send_ref, hot_out, head_out, tail_out,
-    group_ref, rows, edge, out, hot_ref, head_ref, tail_ref, name_sem, sem, edge_sem, out_sem, side_sem,
-):
+def pack_kernel(names_ref, tokens_ref, send_ref, hot_ref, group_ref, rows, out, hot, name_sem, sem, out_sem):
     north = lax.axis_index("lat") == 0
     pole = jnp.where(north, 0, 1)
     start = jnp.where(north, 0, RH - CAP)
@@ -87,12 +84,6 @@
     names.start()
     copy = pltpu.make_async_copy(tokens_ref.at[pl.ds(start, CAP)], rows, sem)
     copy.start()
-    edges = [
-        pltpu.make_async_copy(tokens_ref.at[:, pl.ds(k * (RW - 8), 8)], edge.at[k], edge_sem.at[k])
-        for k in range(2)
-    ]
-    for each in edges:
-        each.start()
     names.wait()
     lane = lax.broadcasted_iota(jnp.int32, (8, CAP_TOKENS), 1)
     slot = slot_rows(group_ref, pole, lane)[0:1]
@@ -102,43 +93,65 @@
     for n in range(SLOT_TOKENS // PACK_STEP):
         at = pl.ds(n * PACK_STEP, PACK_STEP)
         hit = lax.broadcasted_iota(jnp.int32, (PACK_STEP, CAP_TOKENS), 0) + n * PACK_STEP == slot
-        hot = hit.astype(jnp.float32)
-        filled = jnp.max(hot, axis=1, keepdims=True) > 0.5
-        hot = hot.astype(jnp.bfloat16)
-        hot_ref[at, :] = hot
-        moved = jnp.dot(hot, x, preferred_element_type=jnp.float32)
+        here = hit.astype(jnp.float32)
+        filled = jnp.max(here, axis=1, keepdims=True) > 0.5
+        here = here.astype(jnp.bfloat16)
+        hot[at, :] = here
+        moved = jnp.dot(here, x, preferred_element_type=jnp.float32)
         out[at, :] = jnp.where(filled, moved, EMPTY).astype(jnp.bfloat16)
         sends.append(pltpu.make_async_copy(out.at[at], send_ref.at[at], out_sem.at[n]))
         sends[n].start()
-    sends.append(pltpu.make_async_copy(hot_ref, hot_out, side_sem.at[0]))
+    sends.append(pltpu.make_async_copy(hot, hot_ref, out_sem.at[len(sends)]))
     sends[-1].start()
-    for each in edges:
-        each.wait()
+    for send in sends:
+        send.wait()
+
+
+def edge_kernel(own_ref, north_ref, south_ref, head_ref, tail_ref):
     lower = lax.broadcasted_iota(jnp.int32, (8, D), 0) < HALF
-    for r in range(0, RH, 4):
+    pairs = [(north_ref, 0), (north_ref, 2)]
+    pairs += [(own_ref, i) for i in range(0, RH, 2)]
+    pairs += [(south_ref, 0), (south_ref, 2)]
+    for n in range(0, len(pairs), 2):
         heads, tails = [], []
-        for i in (r, r + 2):
-            first = [edge[0, i + k].astype(jnp.float32) for k in range(2)]
-            last = [edge[1, i + k].astype(jnp.float32) for k in range(2)]
+        for ref, i in pairs[n : n + 2]:
+            first = [ref[i + k, 0:8].astype(jnp.float32) for k in range(2)]
+            last = [ref[i + k, 24:32].astype(jnp.float32) for k in range(2)]
             heads.append(jnp.where(lower, first[0], pltpu.roll(first[1], HALF, 0)))
             tails.append(jnp.where(lower, pltpu.roll(last[0], HALF, 0), last[1]))
-        head_ref[r * 4 : r * 4 + 16] = jnp.concatenate(heads, 0).astype(jnp.bfloat16)
-        tail_ref[r * 4 : r * 4 + 16] = jnp.concatenate(tails, 0).astype(jnp.bfloat16)
-    for n, (part, to) in enumerate(((head_ref, head_out), (tail_ref, tail_out))):
-        sends.append(pltpu.make_async_copy(part, to, side_sem.at[n + 1]))
-        sends[-1].start()
-    for send in sends:
-        send.wait()
-
-
-SIDE = HALF * HALF
-
-
-def corner_kernel(left_ref, right_ref, gain_in, up_ref, down_ref, gain_ref):
+        head_ref[n * 8 : n * 8 + 16] = jnp.concatenate(heads, 0).astype(jnp.bfloat16)
+        tail_ref[n * 8 : n * 8 + 16] = jnp.concatenate(tails, 0).astype(jnp.bfloat16)
+
+
+def bias_kernel(table_ref, index_ref, gain_in, bias, gain_ref):
     gain_ref[...] = gain_in[...]
-    for out, first in ((up_ref, 0), (down_ref, (RH - HALF) * HALF)):
-        for k, side in enumerate((left_ref, right_ref)):
-            out[k * SIDE : k * SIDE + SIDE] = side[first : first + SIDE]
+    lat = lax.axis_index("lat")
+    lane = lax.broadcasted_iota(jnp.int32, (8, 128), 1)
+    first = lane < WTOK
+    key_row = (lane % WTOK) // WIN
+    off_north = (lat == 0) & (key_row < HALF)
+    off_south = (lat == lax.axis_size("lat") - 1) & (key_row >= HALF)
+    tables = []
+    for h in range(HEADS):
+        parts = [table_ref[h : h + 1, c : c + 128] for c in (0, BIAS_ROWS - 128)]
+        tables.append([jnp.broadcast_to(part, (8, 128)) for part in parts])
+    for a in range(2):
+        off = off_north if a == 0 else off_south
+        for i in range(0, QROWS, 8):
+            at = (QROWS if a == 0 else 0) + i
+            idx = index_ref[at : at + 8, :]
+            idx = jnp.concatenate([idx, idx], axis=1)
+            high = idx >= 128
+            inner = jnp.where(high, idx - (BIAS_ROWS - 128), idx)
+            for h4 in range(4):
+                found = []
+                for h in (h4, h4 + 4):
+                    lo = jnp.take_along_axis(tables[h][0], inner, axis=1)
+                    hi = jnp.take_along_axis(tables[h][1], inner, axis=1)
+                    found.append(jnp.where(high, hi, lo))
+                value = jnp.where(first, found[0], found[1])
+                to = a * 128 + h4 * QROWS + i
+                bias[to : to + 8, :] = jnp.where(off, masked_score, value)
 
 
 W_STEP = 256
@@ -177,8 +190,8 @@
 
 
 def window_kernel(
-    own_ref, north_ref, south_ref, north_side, south_side, left_ref, right_ref, gain_ref, table_ref, index_ref, hot_ref, w_ref,
-    out_ref, undo_ref, xs, xq, kv, qs, bias, scores, weights, wout, edges,
+    own_ref, north_ref, south_ref, left_ref, right_ref, gain_ref, bias, hot_ref, w_ref,
+    out_ref, undo_ref, xs, xq, kv, qs, scores, weights, wout, edges,
 ):
     gain = gain_ref[...]
     lat = lax.axis_index("lat")
@@ -187,41 +200,9 @@
     undo = jnp.transpose(hot_ref[...].astype(jnp.float32))
     undo_ref[...] = jnp.where(polar, undo, 0.0).astype(jnp.bfloat16)
 
-    lane = lax.broadcasted_iota(jnp.int32, (8, 128), 1)
-    first = lane < WTOK
-    key_row = (lane % WTOK) // WIN
-    off_north = (lat == 0) & (key_row < HALF)
-    off_south = (lat == lax.axis_size("lat") - 1) & (key_row >= HALF)
-    tables = []
-    for h in range(HEADS):
-        parts = [table_ref[h : h + 1, c : c + 128] for c in (0, BIAS_ROWS - 128)]
-        tables.append([jnp.broadcast_to(part, (8, 128)) for part in parts])
-    for a in range(2):
-        off = off_north if a == 0 else off_south
-        for i in range(0, QROWS, 8):
-            at = (QROWS if a == 0 else 0) + i
-            idx = index_ref[at : at + 8, :]
-            idx = jnp.concatenate([idx, idx], axis=1)
-            high = idx >= 128
-            inner = jnp.where(high, idx - (BIAS_ROWS - 128), idx)
-            for h4 in range(4):
-                found = []
-                for h in (h4, h4 + 4):
-                    lo = jnp.take_along_axis(tables[h][0], inner, axis=1)
-                    hi = jnp.take_along_axis(tables[h][1], inner, axis=1)
-                    found.append(jnp.where(high, hi, lo))
-                value = jnp.where(first, found[0], found[1])
-                to = a * 128 + h4 * QROWS + i
-                bias[to : to + 8, :] = jnp.where(off, masked_score, value)
-
     for side, ref in enumerate((left_ref, right_ref)):
-        at = side * SIDE
-        for to, x in (
-            (0, north_side[at : at + SIDE]),
-            (SIDE, ref[...]),
-            (3 * SIDE, south_side[at : at + SIDE]),
-        ):
-            edges[side, to : to + x.shape[0]] = norm_rows(x.astype(jnp.float32), gain)
+        for i in range(0, 64, 32):
+            edges[side, i : i + 32] = norm_rows(ref[i : i + 32].astype(jnp.float32), gain)
     lower = lax.broadcasted_iota(jnp.int32, (8, D), 0) < HALF
     rows = [(north_ref, i) for i in range(HALF)] + [(own_ref, i) for i in range(RH)]
     rows += [(south_ref, i) for i in range(HALF)]
@@ -336,24 +317,17 @@
     gain = ln_gain.reshape(1, D)
     groups = cap_group.transpose(0, 2, 3, 1)
 
-    side = sds((RH * HALF, D), bf16)
-    packed, hot, head, tail = call(
-        pack_kernel,
-        (sds((SLOT_TOKENS, D), bf16), sds((SLOT_TOKENS, CAP_TOKENS), bf16), side, side),
-        [aspec(), hspec()], (hspec(),) * 4,
+    packed, hot = call(
+        pack_kernel, (sds((SLOT_TOKENS, D), bf16), sds((SLOT_TOKENS, CAP_TOKENS), bf16)),
+        [aspec(), hspec()], (hspec(), hspec()),
         [
             SMEM((2, CAP, 1, TILE_COLS), jnp.int32),
             VMEM((CAP, RW, D), bf16),
-            VMEM((2, RH, 8, D), bf16),
             VMEM((SLOT_TOKENS, D), bf16),
             VMEM((SLOT_TOKENS, CAP_TOKENS), bf16),
-            VMEM((RH * HALF, D), bf16),
-            VMEM((RH * HALF, D), bf16),
             pltpu.SemaphoreType.DMA,
             pltpu.SemaphoreType.DMA,
-            pltpu.SemaphoreType.DMA((2,)),
-            pltpu.SemaphoreType.DMA((SLOT_TOKENS // PACK_STEP,)),
-            pltpu.SemaphoreType.DMA((3,)),
+            pltpu.SemaphoreType.DMA((SLOT_TOKENS // PACK_STEP + 1,)),
         ],
         PACK_VMEM, 2 * SLOT_TOKENS * CAP_TOKENS * D, 1 << 20,
     )(groups, tokens)
@@ -366,15 +340,17 @@
     tied, _ = lax.optimization_barrier((tokens, packed))
     north = lax.ppermute(tied[RH - HALF :], "lat", down)
     south = lax.ppermute(tied[:HALF], "lat", up)
+    bias, gain = call(
+        bias_kernel, (sds((2 * 128, 128), f32), sds((1, D), f32)), [vspec()] * 3, (vspec(), vspec()), [],
+        SOME_VMEM, 1 << 18, 1 << 18,
+    )(bias_table, bias_index, gain)
+    side = sds(((RH + WIN) * HALF, D), bf16)
+    head, tail = call(
+        edge_kernel, (side, side), [vspec()] * 3, (vspec(), vspec()), [],
+        SOME_VMEM, 4 << 30, 3 << 19,
+    )(tokens, north, south)
     left = lax.ppermute(tail, "lon", east)
     right = lax.ppermute(head, "lon", west)
-    pair = sds((2 * SIDE, D), bf16)
-    to_north, to_south, gain = call(
-        corner_kernel, (pair, pair, sds((1, D), f32)), [vspec()] * 3, (vspec(),) * 3, [],
-        SOME_VMEM, 1 << 10, 1 << 19,
-    )(left, right, gain)
-    north_side = lax.ppermute(to_south, "lat", down)
-    south_side = lax.ppermute(to_north, "lat", up)
 
     cap_result = call(
         cap_kernel, sds((SLOT_TOKENS, HW), bf16),
@@ -387,20 +363,19 @@
     win_out, undo = call(
         window_kernel,
         (sds((RH * RW, HW), f32), sds((CAP_TOKENS, SLOT_TOKENS), bf16)),
-        [vspec()] * 12, (vspec(), vspec()),
+        [vspec()] * 9, (vspec(), vspec()),
         [
             VMEM((N_WIN * WTOK, D), bf16),
             VMEM((N_WIN * QROWS, D), bf16),
             VMEM((N_WIN * WTOK, 2 * HW), bf16),
             VMEM((N_WIN * QROWS, HW), bf16),
-            VMEM((2 * 128, 128), f32),
             VMEM((N_WIN * 128, 128), f32),
             VMEM((N_WIN * 128, 128), bf16),
             VMEM((N_WIN, QROWS, HW), f32),
             VMEM((2, 64, D), f32),
         ],
         SOME_VMEM, 2300 << 20, 6 << 20, 1 << 18,
-    )(tokens, north, south, north_side, south_side, left, right, gain, bias_table, bias_index, hot, w_qkv)
+    )(tokens, north, south, left, right, gain, bias, hot, w_qkv)
     mixed = call(
         join_kernel, sds((RH * RW, HW), bf16),
         [vspec()] * 3, vspec(), [],

time: 76 us -> 57.7 us (0.76)
  the two profiles are of different devices: /device:TPU:57 before, /device:TPU:31 now
where the time goes in v5:
time: 57.7 us; the launch traced here: 57.1 us
  starting transfers between devices  32.2 us (56%)
  Pallas kernels  10.1 us (18%)
  waiting for transfers between devices  9.48 us (16%)
  local copies, waits for them, and re-layouts  5.17 us (9%)
    all_to_all x2, starting transfers between devices, exchange(): return lax.all_to_all(block, 'lon', split_axis=0, concat_axis=0, tiled=True)  17.1 us
    ppermute x1, starting transfers between devices, layer(): north = lax.ppermute(tied[RH - HALF:], 'lat', down)  7.05 us
    ppermute x1, waiting for transfers between devices, layer(): right = lax.ppermute(head, 'lon', west)  5.16 us
    unnamed x14, local copies, waits for them, and re-layouts  4.04 us
    all_to_all x2, waiting for transfers between devices, exchange(): return lax.all_to_all(block, 'lon', split_axis=0, concat_axis=0, tiled=True)  3.92 us
    pallas_call x1, Pallas kernels, layer(): call(window_kernel, (sds((RH * RW, HW), f32), sds((CAP_TOKENS, SLOT_TOKEN...  3.64 us
    ppermute x1, starting transfers between devices, layer(): left = lax.ppermute(tail, 'lon', east)  3.63 us
    pallas_call x1, Pallas kernels, layer(): call(cap_kernel, sds((SLOT_TOKENS, HW), bf16), [vspec()] * 3, vspec(), [V...  2.98 us
  transfers between devices with their start and end apart: 6, of which 3 were waited for; matrix products, arithmetic and copies ran while one was open for 2% of the time, Pallas kernels for 13%

profile of v5, /device:TPU:31, one launch (start us, length us, event | category | flops | bytes accessed | tf_op | source)
XLA Modules:
  0.0 57.1 jit_solution(1741544094935448346)
XLA Ops:
  0.0 2.0 %shard_map.64 = (bf16[256,1024]{1,0:T(8,128)(2,1)}, bf16[256,128]{1,0:T(8,128)(2,1)}) custom-call(s32[2,4,1,8]{3,2,1,0:T(1,128)} %bitcast.11, bf16[8,32,1024]{2,1,0:T(8,128)(2,1)} %own_ref.3), custom_call_target="tpu_custom_call" | custom-call | flops 67108864 | bytes 1048576 | tf_op jit(solution)/shard_map/pallas_call | solution.py:320
  2.0 12.2 %all-to-all-start = ((bf16[32,8,1024]{2,1,0:T(8,128)(2,1)}), bf16[32,8,1024]{2,1,0:T(8,128)(2,1)S(1)}, u32[]{:S(2)}, u32[]{:S(2)}) async-start(bf16[32,8,1024]{2,1,0:T(8,128)(2,1)} %bitcast.10), calls=%async_computation | async-start | bytes 1048576 | tf_op jit(solution)/shard_map/all_to_all | solution.py:310
  14.3 0.0 copy-start
  14.3 1.1 %fusion = (bf16[4,32,1024]{2,1,0:T(8,128)(2,1)S(1)}, bf16[4,32,1024]{2,1,0:T(8,128)(2,1)S(1)}) fusion(bf16[8,32,1024]{2,1,0:T(8,128)(2,1)} %own_ref.3), kind=kLoop, calls=%fused_computation | loop fusion | bytes 1048576 | tf_op jit(solution)/shard_map/slice | solution.py:342
  15.4 2.5 %collective-permute-start.1 = (bf16[4,32,1024]{2,1,0:T(8,128)(2,1)S(1)}, bf16[4,32,1024]{2,1,0:T(8,128)(2,1)S(1)}, u32[]{:S(2)}, u32[]{:S(2)}) collective-permute-start(bf16[4,32,1024]{2,1,0:T(8,128)(2,1)S(1)} %get-tuple-element.23), channel_id=1, source_target_pairs={{32,0},{64,32},{96,64},{128,96},{160,128},{192,160},{224,192},{256... | collective-permute-start | bytes 786440 | tf_op jit(solution)/shard_map/ppermute | solution.py:342
  17.9 7.0 %collective-permute-start = (bf16[4,32,1024]{2,1,0:T(8,128)(2,1)S(1)}, bf16[4,32,1024]{2,1,0:T(8,128)(2,1)S(1)}, u32[]{:S(2)}, u32[]{:S(2)}) collective-permute-start(bf16[4,32,1024]{2,1,0:T(8,128)(2,1)S(1)} %get-tuple-element.24), channel_id=1, source_target_pairs={{0,32},{32,64},{64,96},{96,128},{128,160},{160,192},{192,224},{224... | collective-permute-start | bytes 786440 | tf_op jit(solution)/shard_map/ppermute | solution.py:341
  24.9 0.0 copy-start.1
  25.0 0.7 %copy-done.1 = s32[64,64]{1,0:T(8,128)S(1)} copy-done((s32[64,64]{1,0:T(8,128)S(1)}, s32[64,64]{1,0:T(8,128)}, u32[]{:S(2)}) %copy-start.1) | copy-done | bytes 16408
  25.7 0.0 copy-start.2
  25.7 0.7 %copy-done.2 = f32[8,225]{1,0:T(8,128)S(1)} copy-done((f32[8,225]{1,0:T(8,128)S(1)}, f32[8,225]{1,0:T(8,128)}, u32[]{:S(2)}) %copy-start.2) | copy-done | bytes 7224
  26.4 0.0 copy-start.3
  26.4 0.7 %copy-done.3 = f32[1024]{0:T(1024)S(1)} copy-done((f32[1024]{0:T(1024)S(1)}, f32[1024]{0:T(1024)}, u32[]{:S(2)}) %copy-start.3) | copy-done | bytes 4120
  27.1 0.5 shard_map.66
  27.6 3.9 %all-to-all-done = bf16[32,8,1024]{2,1,0:T(8,128)(2,1)S(1)} async-done(((bf16[32,8,1024]{2,1,0:T(8,128)(2,1)}), bf16[32,8,1024]{2,1,0:T(8,128)(2,1)S(1)}, u32[]{:S(2)}, u32[]{:S(2)}) %all-to-all-start) | async-done | bytes 524320 | tf_op jit(solution)/shard_map/all_to_all | solution.py:310
  31.5 1.9 %copy-done.4 = bf16[1024,1536]{1,0:T(8,128)(2,1)S(1)} copy-done((bf16[1024,1536]{1,0:T(8,128)(2,1)S(1)}, bf16[1024,1536]{1,0:T(8,128)(2,1)}, u32[]{:S(2)}) %copy-start.4) | copy-done | bytes 3145752
  33.4 3.0 %shard_map.68 = bf16[256,512]{1,0:T(8,128)(2,1)} custom-call(bf16[256,1024]{1,0:T(8,128)(2,1)S(1)} %bitcast.8, f32[1,1024]{1,0:T(1,128)S(1)} %get-tuple-element.18.gain_ref, bf16[1024,1536]{1,0:T(8,128)(2,1)S(1)} %copy-done.4), custom_call_target="tpu_custom_call" | custom-call | flops 1153433600 | bytes 4194304 | tf_op jit(solution)/shard_map/pallas_call | solution.py:355
  36.4 4.9 %all-to-all-start.1 = ((bf16[32,8,512]{2,1,0:T(8,128)(2,1)}), bf16[32,8,512]{2,1,0:T(8,128)(2,1)S(1)}, u32[]{:S(2)}, u32[]{:S(2)}) async-start(bf16[32,8,512]{2,1,0:T(8,128)(2,1)} %bitcast.4), calls=%async_computation.1 | async-start | bytes 524288 | tf_op jit(solution)/shard_map/all_to_all | solution.py:310
  41.3 0.0 copy-start.5
  41.3 0.0 copy-start.6
  41.3 0.0 collective-permute-done.1.south_ref
  41.3 0.0 collective-permute-done.north_ref
  41.3 0.0 copy-done
  41.4 0.1 shard_map.65
  41.4 3.6 %collective-permute-start.2 = (bf16[64,1024]{1,0:T(8,128)(2,1)S(1)}, bf16[64,1024]{1,0:T(8,128)(2,1)S(1)}, u32[]{:S(2)}, u32[]{:S(2)}) collective-permute-start(bf16[64,1024]{1,0:T(8,128)(2,1)S(1)} %get-tuple-element.16), channel_id=1, source_target_pairs={{0,1},{1,2},{2,3},{3,4},{4,5},{5,6},{6,7},{7,8},{8,9},{9,10},{10,1... | collective-permute-start | bytes 393224 | tf_op jit(solution)/shard_map/ppermute | solution.py:352
  45.1 1.9 %collective-permute-start.3 = (bf16[64,1024]{1,0:T(8,128)(2,1)S(1)}, bf16[64,1024]{1,0:T(8,128)(2,1)S(1)}, u32[]{:S(2)}, u32[]{:S(2)}) collective-permute-start(bf16[64,1024]{1,0:T(8,128)(2,1)S(1)} %get-tuple-element.17), channel_id=1, source_target_pairs={{1,0},{2,1},{3,2},{4,3},{5,4},{6,5},{7,6},{8,7},{9,8},{10,9},{11,1... | collective-permute-start | bytes 393224 | tf_op jit(solution)/shard_map/ppermute | solution.py:353
  47.0 0.4 collective-permute-done.2.left_ref
  47.4 5.2 %collective-permute-done.3.right_ref = bf16[64,1024]{1,0:T(8,128)(2,1)S(1)} collective-permute-done((bf16[64,1024]{1,0:T(8,128)(2,1)S(1)}, bf16[64,1024]{1,0:T(8,128)(2,1)S(1)}, u32[]{:S(2)}, u32[]{:S(2)}) %collective-permute-start.3) | collective-permute-done | bytes 131104 | tf_op jit(solution)/shard_map/ppermute | solution.py:353
  52.6 0.0 copy-done.5
  52.6 0.0 copy-done.6
  52.6 3.6 %shard_map.67 = (f32[256,512]{1,0:T(8,128)S(1)}, bf16[128,256]{1,0:T(8,128)(2,1)S(1)}) custom-call(bf16[8,32,1024]{2,1,0:T(8,128)(2,1)S(1)} %copy-done, bf16[4,32,1024]{2,1,0:T(8,128)(2,1)S(1)} %collective-permute-done.north_ref, bf16[4,32,1024]{2,1,0:T(8,128)(2,1)S(1)} %collective-permute-done.1.south_ref, ...), custom_call_target="tpu_custom_call" | custom-call | flops 2411724800 | bytes 6291456 | tf_op jit(solution)/shard_map/pallas_call | solution.py:363
  56.2 0.0 all-to-all-done.1
  56.2 0.9 %shard_map.69 = bf16[256,512]{1,0:T(8,128)(2,1)} custom-call(f32[256,512]{1,0:T(8,128)S(1)} %get-tuple-element.21.win_ref, bf16[256,512]{1,0:T(8,128)(2,1)S(1)} %bitcast.7, bf16[128,256]{1,0:T(8,128)(2,1)S(1)} %get-tuple-element.22.undo_ref), custom_call_target="tpu_custom_call" | custom-call | flops 33554432 | bytes 1048576 | tf_op jit(solution)/shard_map/pallas_call | solution.py:379
  (1 shorter events, 0.0 us)
Async XLA Ops:
  2.0 29.5 %all-to-all-start = ((bf16[32,8,1024]{2,1,0:T(8,128)(2,1)}), bf16[32,8,1024]{2,1,0:T(8,128)(2,1)S(1)}, u32[]{:S(2)}, u32[]{:S(2)}) async-start(bf16[32,8,1024]{2,1,0:T(8,128)(2,1)} %bitcast.10), calls=%async_computation | async-start | bytes 1048576 | tf_op jit(solution)/shard_map/all_to_all | solution.py:310
  14.3 27.1 %copy-start = (bf16[8,32,1024]{2,1,0:T(8,128)(2,1)S(1)}, bf16[8,32,1024]{2,1,0:T(8,128)(2,1)}, u32[]{:S(2)}) copy-start(bf16[8,32,1024]{2,1,0:T(8,128)(2,1)} %own_ref.3) | copy-start | bytes 1572868
  15.4 25.9 %collective-permute-start.1 = (bf16[4,32,1024]{2,1,0:T(8,128)(2,1)S(1)}, bf16[4,32,1024]{2,1,0:T(8,128)(2,1)S(1)}, u32[]{:S(2)}, u32[]{:S(2)}) collective-permute-start(bf16[4,32,1024]{2,1,0:T(8,128)(2,1)S(1)} %get-tuple-element.23), channel_id=1, source_target_pairs={{32,0},{64,32},{96,64},{128,96},{160,128},{192,160},{224,192},{256... | collective-permute-start | bytes 786440 | tf_op jit(solution)/shard_map/ppermute | solution.py:342
  17.9 23.4 %collective-permute-start = (bf16[4,32,1024]{2,1,0:T(8,128)(2,1)S(1)}, bf16[4,32,1024]{2,1,0:T(8,128)(2,1)S(1)}, u32[]{:S(2)}, u32[]{:S(2)}) collective-permute-start(bf16[4,32,1024]{2,1,0:T(8,128)(2,1)S(1)} %get-tuple-element.24), channel_id=1, source_target_pairs={{0,32},{32,64},{64,96},{96,128},{128,160},{160,192},{192,224},{224... | collective-permute-start | bytes 786440 | tf_op jit(solution)/shard_map/ppermute | solution.py:341
  24.9 0.8 %copy-start.1 = (s32[64,64]{1,0:T(8,128)S(1)}, s32[64,64]{1,0:T(8,128)}, u32[]{:S(2)}) copy-start(s32[64,64]{1,0:T(8,128)} %index_ref.1) | copy-start | bytes 49156
  25.7 0.7 %copy-start.2 = (f32[8,225]{1,0:T(8,128)S(1)}, f32[8,225]{1,0:T(8,128)}, u32[]{:S(2)}) copy-start(f32[8,225]{1,0:T(8,128)} %table_ref.1) | copy-start | bytes 21604
  26.4 0.7 %copy-start.3 = (f32[1024]{0:T(1024)S(1)}, f32[1024]{0:T(1024)}, u32[]{:S(2)}) copy-start(f32[1024]{0:T(1024)} %param.7) | copy-start | bytes 12292
  31.5 1.9 %copy-start.4 = (bf16[1024,1536]{1,0:T(8,128)(2,1)S(1)}, bf16[1024,1536]{1,0:T(8,128)(2,1)}, u32[]{:S(2)}) copy-start(bf16[1024,1536]{1,0:T(8,128)(2,1)} %w_ref.3) | copy-start | bytes 9437188
  36.4 19.8 %all-to-all-start.1 = ((bf16[32,8,512]{2,1,0:T(8,128)(2,1)}), bf16[32,8,512]{2,1,0:T(8,128)(2,1)S(1)}, u32[]{:S(2)}, u32[]{:S(2)}) async-start(bf16[32,8,512]{2,1,0:T(8,128)(2,1)} %bitcast.4), calls=%async_computation.1 | async-start | bytes 524288 | tf_op jit(solution)/shard_map/all_to_all | solution.py:310
  41.3 11.3 %copy-start.5 = (bf16[1024,1536]{1,0:T(8,128)(2,1)S(1)}, bf16[1024,1536]{1,0:T(8,128)(2,1)}, u32[]{:S(2)}) copy-start(bf16[1024,1536]{1,0:T(8,128)(2,1)} %w_ref.3) | copy-start | bytes 9437188
  41.3 11.3 %copy-start.6 = (bf16[256,128]{1,0:T(8,128)(2,1)S(1)}, bf16[256,128]{1,0:T(8,128)(2,1)}, u32[]{:S(2)}) copy-start(bf16[256,128]{1,0:T(8,128)(2,1)} %get-tuple-element.20.hot_ref) | copy-start | bytes 196612
  41.4 6.0 %collective-permute-start.2 = (bf16[64,1024]{1,0:T(8,128)(2,1)S(1)}, bf16[64,1024]{1,0:T(8,128)(2,1)S(1)}, u32[]{:S(2)}, u32[]{:S(2)}) collective-permute-start(bf16[64,1024]{1,0:T(8,128)(2,1)S(1)} %get-tuple-element.16), channel_id=1, source_target_pairs={{0,1},{1,2},{2,3},{3,4},{4,5},{5,6},{6,7},{7,8},{8,9},{9,10},{10,1... | collective-permute-start | bytes 393224 | tf_op jit(solution)/shard_map/ppermute | solution.py:352
  45.1 7.5 %collective-permute-start.3 = (bf16[64,1024]{1,0:T(8,128)(2,1)S(1)}, bf16[64,1024]{1,0:T(8,128)(2,1)S(1)}, u32[]{:S(2)}, u32[]{:S(2)}) collective-permute-start(bf16[64,1024]{1,0:T(8,128)(2,1)S(1)} %get-tuple-element.17), channel_id=1, source_target_pairs={{1,0},{2,1},{3,2},{4,3},{5,4},{6,5},{7,6},{8,7},{9,8},{10,9},{11,1... | collective-permute-start | bytes 393224 | tf_op jit(solution)/shard_map/ppermute | solution.py:353

commit v6 on v5

--- a/solution.py
+++ b/solution.py
@@ -23,8 +23,6 @@
 MOST = 2
 SLOT_TOKENS = GROUPS * MOST * TW
 CAP_TOKENS = CAP * RW
-N_WIN = 10
-WIN_B = 5
 WTOK = WIN * WIN
 QROWS = HALF * WIN
 
@@ -160,7 +158,7 @@
 def cap_kernel(x_ref, gain_ref, w_ref, out_ref, normed, qkv):
     n = SLOT_TOKENS
     gain = gain_ref[...]
-    for i in range(0, n, 32):
+    for i in range(0, SLOT_TOKENS, 32):
         normed[i : i + 32] = norm_rows(x_ref[i : i + 32].astype(jnp.float32), gain).astype(jnp.bfloat16)
     pick = (lax.broadcasted_iota(jnp.int32, (8, 128), 1) == 0).astype(jnp.bfloat16)
     first = lax.dot_general(
@@ -184,51 +182,14 @@
             s = lax.dot_general(qh, k, (((1,), (1,)), ((), ())), preferred_element_type=jnp.float32)
             s = s + empty
             raised = jnp.exp(s - jnp.max(s, axis=-1, keepdims=True))
-            weights = (raised * (1.0 / jnp.sum(raised, axis=-1, keepdims=True))).astype(jnp.bfloat16)
-            mixed.append(jnp.dot(weights, v, preferred_element_type=jnp.float32))
+            vh = jnp.where(mine, v, jnp.ones_like(v))
+            both = jnp.dot(raised.astype(jnp.bfloat16), vh, preferred_element_type=jnp.float32)
+            total = both[:, 127:128] if half == 0 else both[:, 0:1]
+            mixed.append(both * (1.0 / total))
         out_ref[:, at : at + 128] = jnp.where(low, mixed[0], mixed[1]).astype(jnp.bfloat16)
 
 
-def window_kernel(
-    own_ref, north_ref, south_ref, left_ref, right_ref, gain_ref, bias, hot_ref, w_ref,
-    out_ref, undo_ref, xs, xq, kv, qs, scores, weights, wout, edges,
-):
-    gain = gain_ref[...]
-    lat = lax.axis_index("lat")
-
-    polar = (lat == 0) | (lat == lax.axis_size("lat") - 1)
-    undo = jnp.transpose(hot_ref[...].astype(jnp.float32))
-    undo_ref[...] = jnp.where(polar, undo, 0.0).astype(jnp.bfloat16)
-
-    for side, ref in enumerate((left_ref, right_ref)):
-        for i in range(0, 64, 32):
-            edges[side, i : i + 32] = norm_rows(ref[i : i + 32].astype(jnp.float32), gain)
-    lower = lax.broadcasted_iota(jnp.int32, (8, D), 0) < HALF
-    rows = [(north_ref, i) for i in range(HALF)] + [(own_ref, i) for i in range(RH)]
-    rows += [(south_ref, i) for i in range(HALF)]
-    for r in range(0, RH + WIN, 2):
-        blocks = [[], []]
-        for k in range(2):
-            ref, i = rows[r + k]
-            normed = norm_rows(ref[i].astype(jnp.float32), gain)
-            turned = [pltpu.roll(normed[j * 8 : j * 8 + 8], HALF, 0) for j in range(4)]
-            lo = edges[0, r * 4 : r * 4 + 8]
-            hi = edges[1, r * 4 : r * 4 + 8]
-            if k == 0:
-                hi = pltpu.roll(hi, HALF, 0)
-            else:
-                lo = pltpu.roll(lo, HALF, 0)
-            seq = [lo] + turned + [hi]
-            blocks[k] = [jnp.where(lower, seq[b], seq[b + 1]) for b in range(WIN_B)]
-        a, wr = r // WIN, r % WIN
-        for b in range(WIN_B):
-            both = jnp.concatenate([blocks[0][b], blocks[1][b]], 0).astype(jnp.bfloat16)
-            to = (a * WIN_B + b) * WTOK + wr * WIN
-            xs[to : to + 16] = both
-            if (wr >= HALF) == (a == 0):
-                to = (a * WIN_B + b) * QROWS + (wr % HALF) * WIN
-                xq[to : to + 16] = both
-
+def project(xs, xq, w_ref, qs, kv):
     for j in range(3 * HW // W_STEP):
         at = slice(j * W_STEP, j * W_STEP + W_STEP)
         if j * W_STEP < HW:
@@ -237,6 +198,9 @@
             to = slice(j * W_STEP - HW, j * W_STEP - HW + W_STEP)
             kv[:, to] = jnp.dot(xs[...], w_ref[:, at], preferred_element_type=jnp.float32).astype(jnp.bfloat16)
 
+
+def attend(qs, kv, bias, scores, weights, wout):
+    count = qs.shape[0] // QROWS
     head = lax.broadcasted_iota(jnp.int32, (QROWS, HW), 1) // HD % 4
     blank = jnp.zeros((WTOK, HW // 2), jnp.bfloat16)
 
@@ -245,15 +209,15 @@
         low = jnp.concatenate([blank, x[:, HW // 2 :]], 1)
         return jnp.concatenate([top, low], 0)
 
-    for n in range(N_WIN):
+    for n in range(count):
         q = qs[n * QROWS : n * QROWS + QROWS] * jnp.bfloat16(HD ** (-0.5))
         spread = jnp.concatenate([jnp.where(head == h, q, jnp.zeros_like(q)) for h in range(4)], 0)
         k = two_groups(kv[n * WTOK : n * WTOK + WTOK, 0:HW])
         s = lax.dot_general(spread, k, (((1,), (1,)), ((), ())), preferred_element_type=jnp.float32)
-        a = n // WIN_B
+        a = n // (count // 2)
         scores[n * 128 : n * 128 + 128] = s + bias[a * 128 : a * 128 + 128]
     left = lax.broadcasted_iota(jnp.int32, (128, 128), 1) < WTOK
-    for n in range(N_WIN):
+    for n in range(count):
         s = scores[n * 128 : n * 128 + 128]
         top0 = jnp.max(jnp.where(left, s, -jnp.inf), axis=-1, keepdims=True)
         top1 = jnp.max(jnp.where(left, -jnp.inf, s), axis=-1, keepdims=True)
@@ -262,31 +226,98 @@
         sum1 = jnp.sum(jnp.where(left, 0.0, raised), axis=-1, keepdims=True)
         share = jnp.where(left, 1.0 / sum0, 1.0 / sum1)
         weights[n * 128 : n * 128 + 128] = (raised * share).astype(jnp.bfloat16)
-    for n in range(N_WIN):
+    for n in range(count):
         v = two_groups(kv[n * WTOK : n * WTOK + WTOK, HW : 2 * HW])
         o = jnp.dot(weights[n * 128 : n * 128 + 128], v, preferred_element_type=jnp.float32)
         total = o[0:QROWS]
         for h in range(1, 4):
             total = jnp.where(head == h, o[h * QROWS : h * QROWS + QROWS], total)
         wout[n] = total
+
+
+def place(blocks, per_row, r, n, xs, xq):
+    a, wr = r // WIN, r % WIN
+    both = jnp.concatenate(blocks, 0).astype(jnp.bfloat16)
+    to = (a * per_row + n) * WTOK + wr * WIN
+    xs[to : to + 16] = both
+    if (wr >= HALF) == (a == 0):
+        to = (a * per_row + n) * QROWS + (wr % HALF) * WIN
+        xq[to : to + 16] = both
+
+
+INNER = 3
+OUTER = 2
+
+
+def inner_kernel(
+    own_ref, north_ref, south_ref, gain_ref, bias, w_ref, wout, rims_ref, xs, xq, kv, qs, scores, weights,
+):
+    gain = gain_ref[...]
+    lower = lax.broadcasted_iota(jnp.int32, (8, D), 0) < HALF
+    rows = [(north_ref, i) for i in range(HALF)] + [(own_ref, i) for i in range(RH)]
+    rows += [(south_ref, i) for i in range(HALF)]
+    for r in range(0, RH + WIN, 2):
+        turned = []
+        for ref, i in rows[r : r + 2]:
+            normed = norm_rows(ref[i].astype(jnp.float32), gain)
+            turned.append([pltpu.roll(normed[j * 8 : j * 8 + 8], HALF, 0) for j in range(4)])
+        for n in range(INNER):
+            place([jnp.where(lower, row[n], row[n + 1]) for row in turned], INNER, r, n, xs, xq)
+        for side in range(2):
+            both = jnp.concatenate([row[3 * side] for row in turned], 0)
+            rims_ref[side, r * 8 : r * 8 + 16] = both.astype(jnp.bfloat16)
+    project(xs, xq, w_ref, qs, kv)
+    attend(qs, kv, bias, scores, weights, wout)
+
+
+def outer_kernel(
+    left_ref, right_ref, rims_ref, inner_ref, gain_ref, bias, hot_ref, w_ref,
+    out_ref, cap_ref, undo_ref, xs, xq, kv, qs, scores, weights, wout, edges, full,
+):
+    gain = gain_ref[...]
+    lat = lax.axis_index("lat")
+
+    polar = (lat == 0) | (lat == lax.axis_size("lat") - 1)
+    undo = jnp.transpose(hot_ref[...].astype(jnp.float32))
+    undo_ref[...] = jnp.where(polar, undo, 0.0).astype(jnp.bfloat16)
+
+    for side, ref in enumerate((left_ref, right_ref)):
+        for i in range(0, 64, 32):
+            edges[side, i : i + 32] = norm_rows(ref[i : i + 32].astype(jnp.float32), gain)
+    lower = lax.broadcasted_iota(jnp.int32, (8, D), 0) < HALF
+    for r in range(0, RH + WIN, 2):
+        lo = edges[0, r * 4 : r * 4 + 8]
+        hi = edges[1, r * 4 : r * 4 + 8]
+        lows, highs = [lo, pltpu.roll(lo, HALF, 0)], [pltpu.roll(hi, HALF, 0), hi]
+        heads = rims_ref[0, r * 8 : r * 8 + 16].astype(jnp.float32)
+        tails = rims_ref[1, r * 8 : r * 8 + 16].astype(jnp.float32)
+        place([jnp.where(lower, lows[k], heads[k * 8 : k * 8 + 8]) for k in range(2)], OUTER, r, 0, xs, xq)
+        place([jnp.where(lower, tails[k * 8 : k * 8 + 8], highs[k]) for k in range(2)], OUTER, r, 1, xs, xq)
+    project(xs, xq, w_ref, qs, kv)
+    attend(qs, kv, bias, scores, weights, wout)
+
     lower = lax.broadcasted_iota(jnp.int32, (8, HW), 0) < HALF
     for r in range(RH):
         a, wr = r // HALF, r % HALF
-        turned = [
-            pltpu.roll(wout[a * WIN_B + b, wr * WIN : wr * WIN + WIN], HALF, 0) for b in range(WIN_B)
-        ]
+        at = slice(wr * WIN, wr * WIN + WIN)
+        parts = [wout[a * OUTER, at]]
+        parts += [inner_ref[a * INNER + n, at] for n in range(INNER)]
+        parts += [wout[a * OUTER + 1, at]]
+        turned = [pltpu.roll(part, HALF, 0) for part in parts]
         for j in range(4):
             to = r * RW + j * 8
-            out_ref[to : to + 8] = jnp.where(lower, turned[j], turned[j + 1])
-
-
-def join_kernel(win_ref, back_ref, undo_ref, out_ref):
-    north = lax.axis_index("lat") == 0
+            full[to : to + 8] = jnp.where(lower, turned[j], turned[j + 1])
+    out_ref[...] = full[...].astype(jnp.bfloat16)
+    cap_ref[...] = jnp.where(lat == 0, full[0:CAP_TOKENS], full[CAP_TOKENS:])
+
+
+def join_kernel(win_ref, back_ref, undo_ref, out_in, out_ref, mixed, sem):
     cap = jnp.dot(undo_ref[...], back_ref[...], preferred_element_type=jnp.float32)
-    top = win_ref[0:CAP_TOKENS] + jnp.where(north, cap, 0.0)
-    low = win_ref[CAP_TOKENS:] + jnp.where(north, 0.0, cap)
-    out_ref[0:CAP_TOKENS] = top.astype(jnp.bfloat16)
-    out_ref[CAP_TOKENS:] = low.astype(jnp.bfloat16)
+    mixed[...] = (win_ref[...] + cap).astype(jnp.bfloat16)
+    start = jnp.where(lax.axis_index("lat") == 0, 0, CAP_TOKENS)
+    copy = pltpu.make_async_copy(mixed, out_ref.at[pl.ds(pl.multiple_of(start, CAP_TOKENS), CAP_TOKENS)], sem)
+    copy.start()
+    copy.wait()
 
 
 def sds(shape, dtype):
@@ -360,27 +391,36 @@
     )(arrived, gain, w_qkv)
     returned = exchange(cap_result.reshape(lon_count, MOST * TW, HW)).reshape(SLOT_TOKENS, HW)
 
-    win_out, undo = call(
-        window_kernel,
-        (sds((RH * RW, HW), f32), sds((CAP_TOKENS, SLOT_TOKENS), bf16)),
-        [vspec()] * 9, (vspec(), vspec()),
-        [
-            VMEM((N_WIN * WTOK, D), bf16),
-            VMEM((N_WIN * QROWS, D), bf16),
-            VMEM((N_WIN * WTOK, 2 * HW), bf16),
-            VMEM((N_WIN * QROWS, HW), bf16),
-            VMEM((N_WIN * 128, 128), f32),
-            VMEM((N_WIN * 128, 128), bf16),
-            VMEM((N_WIN, QROWS, HW), f32),
-            VMEM((2, 64, D), f32),
-        ],
-        SOME_VMEM, 2300 << 20, 6 << 20, 1 << 18,
-    )(tokens, north, south, left, right, gain, bias, hot, w_qkv)
+    def scratch(count):
+        return [
+            VMEM((count * WTOK, D), bf16),
+            VMEM((count * QROWS, D), bf16),
+            VMEM((count * WTOK, 2 * HW), bf16),
+            VMEM((count * QROWS, HW), bf16),
+            VMEM((count * 128, 128), f32),
+            VMEM((count * 128, 128), bf16),
+        ]
+
+    inner, rims = call(
+        inner_kernel,
+        (sds((2 * INNER, QROWS, HW), f32), sds((2, (RH + WIN) * 8, D), bf16)),
+        [vspec()] * 6, (vspec(), vspec()), scratch(2 * INNER),
+        SOME_VMEM, 1400 << 20, 5 << 20, 1 << 17,
+    )(tokens, north, south, gain, bias, w_qkv)
+    win_out, cap_rows, undo = call(
+        outer_kernel,
+        (sds((RH * RW, HW), bf16), sds((CAP_TOKENS, HW), f32), sds((CAP_TOKENS, SLOT_TOKENS), bf16)),
+        [vspec()] * 8, (vspec(),) * 3,
+        scratch(2 * OUTER)
+        + [VMEM((2 * OUTER, QROWS, HW), f32), VMEM((2, 64, D), f32), VMEM((RH * RW, HW), f32)],
+        SOME_VMEM, 900 << 20, 5 << 20, 1 << 17,
+    )(left, right, rims, inner, gain, bias, hot, w_qkv)
     mixed = call(
         join_kernel, sds((RH * RW, HW), bf16),
-        [vspec()] * 3, vspec(), [],
-        8 << 20, 2 * CAP_TOKENS * SLOT_TOKENS * HW, 1 << 20,
-    )(win_out, returned, undo)
+        [vspec()] * 3 + [aspec()], aspec(),
+        [VMEM((CAP_TOKENS, HW), bf16), pltpu.SemaphoreType.DMA],
+        8 << 20, 2 * CAP_TOKENS * SLOT_TOKENS * HW, 1 << 19, aliases={3: 0},
+    )(cap_rows, returned, undo, win_out)
     return mixed.reshape(RH, RW, HW)
 
 

time: 57.7 us -> 57.4 us (level)
  waiting for transfers between devices: 9.48 us -> 6.98 us
  Pallas kernels: 10.1 us -> 12.3 us
    ppermute x1, waiting for transfers between devices: 5.16 us -> 3.05 us  [layer(): right = lax.ppermute(head, 'lon', west)]
    pallas_call x2 -> x3, Pallas kernels: 4.54 us -> 5.66 us  [the longest x1 2.48 us: layer(): call(inner_kernel, (sds((2 * INNER, QROWS, HW), f32), sds((2, (RH + WIN)...]
    pallas_call x1, Pallas kernels: 2.98 us -> 4.06 us  [layer(): call(cap_kernel, sds((SLOT_TOKENS, HW), bf16), [vspec()] * 3, vspec(), [V...]
  transfers between devices with their start and end apart: 6 -> 6, of which waited for: 3 -> 2; matrix products, arithmetic and copies ran while one was open for 2% -> 2% of each run, Pallas kernels for 13% -> 17%
where the time goes in v6:
time: 57.4 us; the launch traced here: 56.8 us
  starting transfers between devices  32.2 us (56%)
  Pallas kernels  12.3 us (21%)
  waiting for transfers between devices  6.98 us (12%)
  local copies, waits for them, and re-layouts  5.17 us (9%)
    all_to_all x2, starting transfers between devices, exchange(): return lax.all_to_all(block, 'lon', split_axis=0, concat_axis=0, tiled=True)  17.1 us
    ppermute x1, starting transfers between devices, layer(): north = lax.ppermute(tied[RH - HALF:], 'lat', down)  7.05 us
    pallas_call x1, Pallas kernels, layer(): call(cap_kernel, sds((SLOT_TOKENS, HW), bf16), [vspec()] * 3, vspec(), [V...  4.06 us
    unnamed x14, local copies, waits for them, and re-layouts  4.04 us
    all_to_all x2, waiting for transfers between devices, exchange(): return lax.all_to_all(block, 'lon', split_axis=0, concat_axis=0, tiled=True)  3.92 us
    ppermute x1, starting transfers between devices, layer(): left = lax.ppermute(tail, 'lon', east)  3.63 us
    ppermute x1, waiting for transfers between devices, layer(): right = lax.ppermute(head, 'lon', west)  3.05 us
    pallas_call x1, Pallas kernels, layer(): call(inner_kernel, (sds((2 * INNER, QROWS, HW), f32), sds((2, (RH + WIN)...  2.48 us
  transfers between devices with their start and end apart: 6, of which 2 were waited for; matrix products, arithmetic and copies ran while one was open for 2% of the time, Pallas kernels for 17%

profile of v6, /device:TPU:31, one launch (start us, length us, event | category | flops | bytes accessed | tf_op | source)
XLA Modules:
  0.0 56.8 jit_solution(7376360631101863704)
XLA Ops:
  0.0 2.0 %shard_map.64 = (bf16[256,1024]{1,0:T(8,128)(2,1)}, bf16[256,128]{1,0:T(8,128)(2,1)}) custom-call(s32[2,4,1,8]{3,2,1,0:T(1,128)} %bitcast.11, bf16[8,32,1024]{2,1,0:T(8,128)(2,1)} %own_ref.3), custom_call_target="tpu_custom_call" | custom-call | flops 67108864 | bytes 1048576 | tf_op jit(solution)/shard_map/pallas_call | solution.py:351
  2.0 12.2 %all-to-all-start = ((bf16[32,8,1024]{2,1,0:T(8,128)(2,1)}), bf16[32,8,1024]{2,1,0:T(8,128)(2,1)S(1)}, u32[]{:S(2)}, u32[]{:S(2)}) async-start(bf16[32,8,1024]{2,1,0:T(8,128)(2,1)} %bitcast.10), calls=%async_computation | async-start | bytes 1048576 | tf_op jit(solution)/shard_map/all_to_all | solution.py:341
  14.3 0.0 copy-start.2
  14.3 1.1 %fusion = (bf16[4,32,1024]{2,1,0:T(8,128)(2,1)S(1)}, bf16[4,32,1024]{2,1,0:T(8,128)(2,1)S(1)}) fusion(bf16[8,32,1024]{2,1,0:T(8,128)(2,1)} %own_ref.3), kind=kLoop, calls=%fused_computation | loop fusion | bytes 1048576 | tf_op jit(solution)/shard_map/slice | solution.py:373
  15.4 2.5 %collective-permute-start.1 = (bf16[4,32,1024]{2,1,0:T(8,128)(2,1)S(1)}, bf16[4,32,1024]{2,1,0:T(8,128)(2,1)S(1)}, u32[]{:S(2)}, u32[]{:S(2)}) collective-permute-start(bf16[4,32,1024]{2,1,0:T(8,128)(2,1)S(1)} %get-tuple-element.29), channel_id=1, source_target_pairs={{32,0},{64,32},{96,64},{128,96},{160,128},{192,160},{224,192},{256... | collective-permute-start | bytes 786440 | tf_op jit(solution)/shard_map/ppermute | solution.py:373
  17.9 7.0 %collective-permute-start = (bf16[4,32,1024]{2,1,0:T(8,128)(2,1)S(1)}, bf16[4,32,1024]{2,1,0:T(8,128)(2,1)S(1)}, u32[]{:S(2)}, u32[]{:S(2)}) collective-permute-start(bf16[4,32,1024]{2,1,0:T(8,128)(2,1)S(1)} %get-tuple-element.30), channel_id=1, source_target_pairs={{0,32},{32,64},{64,96},{96,128},{128,160},{160,192},{192,224},{224... | collective-permute-start | bytes 786440 | tf_op jit(solution)/shard_map/ppermute | solution.py:372
  24.9 0.0 copy-start.4
  24.9 0.7 %copy-done.4 = s32[64,64]{1,0:T(8,128)S(1)} copy-done((s32[64,64]{1,0:T(8,128)S(1)}, s32[64,64]{1,0:T(8,128)}, u32[]{:S(2)}) %copy-start.4) | copy-done | bytes 16408
  25.7 0.0 copy-start.5
  25.7 0.7 %copy-done.5 = f32[8,225]{1,0:T(8,128)S(1)} copy-done((f32[8,225]{1,0:T(8,128)S(1)}, f32[8,225]{1,0:T(8,128)}, u32[]{:S(2)}) %copy-start.5) | copy-done | bytes 7224
  26.4 0.7 %copy-done.6 = f32[1024]{0:T(1024)S(1)} copy-done((f32[1024]{0:T(1024)S(1)}, f32[1024]{0:T(1024)}, u32[]{:S(2)}) %copy-start.6) | copy-done | bytes 4120
  27.1 0.5 shard_map.66
  27.6 3.9 %all-to-all-done = bf16[32,8,1024]{2,1,0:T(8,128)(2,1)S(1)} async-done(((bf16[32,8,1024]{2,1,0:T(8,128)(2,1)}), bf16[32,8,1024]{2,1,0:T(8,128)(2,1)S(1)}, u32[]{:S(2)}, u32[]{:S(2)}) %all-to-all-start) | async-done | bytes 524320 | tf_op jit(solution)/shard_map/all_to_all | solution.py:341
  31.5 1.9 %copy-done = bf16[1024,1536]{1,0:T(8,128)(2,1)S(1)} copy-done((bf16[1024,1536]{1,0:T(8,128)(2,1)S(1)}, bf16[1024,1536]{1,0:T(8,128)(2,1)}, u32[]{:S(2)}) %copy-start) | copy-done | bytes 3145752
  33.4 4.1 %shard_map.69 = bf16[256,512]{1,0:T(8,128)(2,1)} custom-call(bf16[256,1024]{1,0:T(8,128)(2,1)S(1)} %bitcast.8, f32[1,1024]{1,0:T(1,128)S(1)} %get-tuple-element.21.gain_ref, bf16[1024,1536]{1,0:T(8,128)(2,1)S(1)} %copy-done), custom_call_target="tpu_custom_call" | custom-call | flops 1153433600 | bytes 4194304 | tf_op jit(solution)/shard_map/pallas_call | solution.py:386
  37.4 4.9 %all-to-all-start.1 = ((bf16[32,8,512]{2,1,0:T(8,128)(2,1)}), bf16[32,8,512]{2,1,0:T(8,128)(2,1)S(1)}, u32[]{:S(2)}, u32[]{:S(2)}) async-start(bf16[32,8,512]{2,1,0:T(8,128)(2,1)} %bitcast.4), calls=%async_computation.1 | async-start | bytes 524288 | tf_op jit(solution)/shard_map/all_to_all | solution.py:341
  42.4 0.0 copy-start.1
  42.4 0.0 collective-permute-done.1.south_ref
  42.4 0.0 collective-permute-done.north_ref
  42.4 0.0 copy-done.2
  42.4 0.1 shard_map.65
  42.5 0.0 copy-start.3
  42.5 3.6 %collective-permute-start.2 = (bf16[64,1024]{1,0:T(8,128)(2,1)S(1)}, bf16[64,1024]{1,0:T(8,128)(2,1)S(1)}, u32[]{:S(2)}, u32[]{:S(2)}) collective-permute-start(bf16[64,1024]{1,0:T(8,128)(2,1)S(1)} %get-tuple-element.19), channel_id=1, source_target_pairs={{0,1},{1,2},{2,3},{3,4},{4,5},{5,6},{6,7},{7,8},{8,9},{9,10},{10,1... | collective-permute-start | bytes 393224 | tf_op jit(solution)/shard_map/ppermute | solution.py:383
  46.2 1.9 %collective-permute-start.3 = (bf16[64,1024]{1,0:T(8,128)(2,1)S(1)}, bf16[64,1024]{1,0:T(8,128)(2,1)S(1)}, u32[]{:S(2)}, u32[]{:S(2)}) collective-permute-start(bf16[64,1024]{1,0:T(8,128)(2,1)S(1)} %get-tuple-element.20), channel_id=1, source_target_pairs={{1,0},{2,1},{3,2},{4,3},{5,4},{6,5},{7,6},{8,7},{9,8},{10,9},{11,1... | collective-permute-start | bytes 393224 | tf_op jit(solution)/shard_map/ppermute | solution.py:384
  48.1 0.0 copy-done.1
  48.1 2.5 %shard_map.67 = (f32[6,32,512]{2,1,0:T(8,128)S(1)}, bf16[2,128,1024]{2,1,0:T(8,128)(2,1)S(1)}) custom-call(bf16[8,32,1024]{2,1,0:T(8,128)(2,1)S(1)} %copy-done.2, bf16[4,32,1024]{2,1,0:T(8,128)(2,1)S(1)} %collective-permute-done.north_ref, bf16[4,32,1024]{2,1,0:T(8,128)(2,1)S(1)} %collective-permute-done.1.south_ref, ...), custom_call_target="tpu_custom_call" | custom-call | flops 1468006400 | bytes 5242880 | tf_op jit(solution)/shard_map/pallas_call | solution.py:404
  50.6 0.0 collective-permute-done.2.left_ref
  50.6 3.1 %collective-permute-done.3.right_ref = bf16[64,1024]{1,0:T(8,128)(2,1)S(1)} collective-permute-done((bf16[64,1024]{1,0:T(8,128)(2,1)S(1)}, bf16[64,1024]{1,0:T(8,128)(2,1)S(1)}, u32[]{:S(2)}, u32[]{:S(2)}) %collective-permute-start.3) | collective-permute-done | bytes 131104 | tf_op jit(solution)/shard_map/ppermute | solution.py:384
  53.6 0.0 copy-done.3
  53.6 2.3 %shard_map.68 = (bf16[256,512]{1,0:T(8,128)(2,1)}, f32[128,512]{1,0:T(8,128)S(1)}, bf16[128,256]{1,0:T(8,128)(2,1)S(1)}) custom-call(bf16[64,1024]{1,0:T(8,128)(2,1)S(1)} %collective-permute-done.2.left_ref, bf16[64,1024]{1,0:T(8,128)(2,1)S(1)} %collective-permute-done.3.right_ref, bf16[2,128,1024]{2,1,0:T(8,128)(2,1)S(1)} %get-tuple-element.23.rims_ref, ...), custom_call_target="tpu_custom_call" | custom-call | flops 943718400 | bytes 5242880 | tf_op jit(solution)/shard_map/pallas_call | solution.py:410
  56.0 0.0 all-to-all-done.1
  56.0 0.9 %shard_map.70 = bf16[256,512]{1,0:T(8,128)(2,1)} custom-call(f32[128,512]{1,0:T(8,128)S(1)} %get-tuple-element.26.win_ref, bf16[256,512]{1,0:T(8,128)(2,1)S(1)} %bitcast.7, bf16[128,256]{1,0:T(8,128)(2,1)S(1)} %get-tuple-element.27.undo_ref, bf16[256,512]{1,0:T(8,128)(2,1)} %get-tuple-element.28.out_in), custom_call_target="tpu_custom_call", output_to_operand_aliasing={{}: (3, {})} | custom-call | flops 33554432 | bytes 524288 | tf_op jit(solution)/shard_map/pallas_call | solution.py:418
  (2 shorter events, 0.0 us)
Async XLA Ops:
  2.0 29.5 %all-to-all-start = ((bf16[32,8,1024]{2,1,0:T(8,128)(2,1)}), bf16[32,8,1024]{2,1,0:T(8,128)(2,1)S(1)}, u32[]{:S(2)}, u32[]{:S(2)}) async-start(bf16[32,8,1024]{2,1,0:T(8,128)(2,1)} %bitcast.10), calls=%async_computation | async-start | bytes 1048576 | tf_op jit(solution)/shard_map/all_to_all | solution.py:341
  14.3 28.1 %copy-start.2 = (bf16[8,32,1024]{2,1,0:T(8,128)(2,1)S(1)}, bf16[8,32,1024]{2,1,0:T(8,128)(2,1)}, u32[]{:S(2)}) copy-start(bf16[8,32,1024]{2,1,0:T(8,128)(2,1)} %own_ref.3) | copy-start | bytes 1572868
  15.4 27.0 %collective-permute-start.1 = (bf16[4,32,1024]{2,1,0:T(8,128)(2,1)S(1)}, bf16[4,32,1024]{2,1,0:T(8,128)(2,1)S(1)}, u32[]{:S(2)}, u32[]{:S(2)}) collective-permute-start(bf16[4,32,1024]{2,1,0:T(8,128)(2,1)S(1)} %get-tuple-element.29), channel_id=1, source_target_pairs={{32,0},{64,32},{96,64},{128,96},{160,128},{192,160},{224,192},{256... | collective-permute-start | bytes 786440 | tf_op jit(solution)/shard_map/ppermute | solution.py:373
  17.9 24.5 %collective-permute-start = (bf16[4,32,1024]{2,1,0:T(8,128)(2,1)S(1)}, bf16[4,32,1024]{2,1,0:T(8,128)(2,1)S(1)}, u32[]{:S(2)}, u32[]{:S(2)}) collective-permute-start(bf16[4,32,1024]{2,1,0:T(8,128)(2,1)S(1)} %get-tuple-element.30), channel_id=1, source_target_pairs={{0,32},{32,64},{64,96},{96,128},{128,160},{160,192},{192,224},{224... | collective-permute-start | bytes 786440 | tf_op jit(solution)/shard_map/ppermute | solution.py:372
  24.9 0.8 %copy-start.4 = (s32[64,64]{1,0:T(8,128)S(1)}, s32[64,64]{1,0:T(8,128)}, u32[]{:S(2)}) copy-start(s32[64,64]{1,0:T(8,128)} %index_ref.1) | copy-start | bytes 49156
  25.7 0.7 %copy-start.5 = (f32[8,225]{1,0:T(8,128)S(1)}, f32[8,225]{1,0:T(8,128)}, u32[]{:S(2)}) copy-start(f32[8,225]{1,0:T(8,128)} %table_ref.1) | copy-start | bytes 21604
  26.4 0.7 %copy-start.6 = (f32[1024]{0:T(1024)S(1)}, f32[1024]{0:T(1024)}, u32[]{:S(2)}) copy-start(f32[1024]{0:T(1024)} %param.7) | copy-start | bytes 12292
  31.5 1.9 %copy-start = (bf16[1024,1536]{1,0:T(8,128)(2,1)S(1)}, bf16[1024,1536]{1,0:T(8,128)(2,1)}, u32[]{:S(2)}) copy-start(bf16[1024,1536]{1,0:T(8,128)(2,1)} %w_ref.5) | copy-start | bytes 9437188
  37.4 18.5 %all-to-all-start.1 = ((bf16[32,8,512]{2,1,0:T(8,128)(2,1)}), bf16[32,8,512]{2,1,0:T(8,128)(2,1)S(1)}, u32[]{:S(2)}, u32[]{:S(2)}) async-start(bf16[32,8,512]{2,1,0:T(8,128)(2,1)} %bitcast.4), calls=%async_computation.1 | async-start | bytes 524288 | tf_op jit(solution)/shard_map/all_to_all | solution.py:341
  42.4 5.7 %copy-start.1 = (bf16[1024,1536]{1,0:T(8,128)(2,1)S(1)}, bf16[1024,1536]{1,0:T(8,128)(2,1)}, u32[]{:S(2)}) copy-start(bf16[1024,1536]{1,0:T(8,128)(2,1)} %w_ref.5) | copy-start | bytes 9437188
  42.5 11.1 %copy-start.3 = (bf16[256,128]{1,0:T(8,128)(2,1)S(1)}, bf16[256,128]{1,0:T(8,128)(2,1)}, u32[]{:S(2)}) copy-start(bf16[256,128]{1,0:T(8,128)(2,1)} %get-tuple-element.25.hot_ref) | copy-start | bytes 196612
  42.5 8.1 %collective-permute-start.2 = (bf16[64,1024]{1,0:T(8,128)(2,1)S(1)}, bf16[64,1024]{1,0:T(8,128)(2,1)S(1)}, u32[]{:S(2)}, u32[]{:S(2)}) collective-permute-start(bf16[64,1024]{1,0:T(8,128)(2,1)S(1)} %get-tuple-element.19), channel_id=1, source_target_pairs={{0,1},{1,2},{2,3},{3,4},{4,5},{5,6},{6,7},{7,8},{8,9},{9,10},{10,1... | collective-permute-start | bytes 393224 | tf_op jit(solution)/shard_map/ppermute | solution.py:383
  46.2 7.5 %collective-permute-start.3 = (bf16[64,1024]{1,0:T(8,128)(2,1)S(1)}, bf16[64,1024]{1,0:T(8,128)(2,1)S(1)}, u32[]{:S(2)}, u32[]{:S(2)}) collective-permute-start(bf16[64,1024]{1,0:T(8,128)(2,1)S(1)} %get-tuple-element.20), channel_id=1, source_target_pairs={{1,0},{2,1},{3,2},{4,3},{5,4},{6,5},{7,6},{8,7},{9,8},{10,9},{11,1... | collective-permute-start | bytes 393224 | tf_op jit(solution)/shard_map/ppermute | solution.py:384

commit v7 on v6

--- a/solution.py
+++ b/solution.py
@@ -121,9 +121,15 @@
         tail_ref[n * 8 : n * 8 + 16] = jnp.concatenate(tails, 0).astype(jnp.bfloat16)
 
 
-def bias_kernel(table_ref, index_ref, gain_in, bias, gain_ref):
-    gain_ref[...] = gain_in[...]
+def bias_kernel(table_ref, index_ref, gain_in, hot_ref, own_ref, bias, gain_ref, undo_ref, normed_ref):
+    gain = gain_in[...]
+    gain_ref[...] = gain
+    for r in range(RH):
+        normed_ref[r] = norm_rows(own_ref[r].astype(jnp.float32), gain).astype(jnp.bfloat16)
     lat = lax.axis_index("lat")
+    polar = (lat == 0) | (lat == lax.axis_size("lat") - 1)
+    undo = jnp.transpose(hot_ref[...].astype(jnp.float32))
+    undo_ref[...] = jnp.where(polar, undo, 0.0).astype(jnp.bfloat16)
     lane = lax.broadcasted_iota(jnp.int32, (8, 128), 1)
     first = lane < WTOK
     key_row = (lane % WTOK) // WIN
@@ -182,10 +188,8 @@
             s = lax.dot_general(qh, k, (((1,), (1,)), ((), ())), preferred_element_type=jnp.float32)
             s = s + empty
             raised = jnp.exp(s - jnp.max(s, axis=-1, keepdims=True))
-            vh = jnp.where(mine, v, jnp.ones_like(v))
-            both = jnp.dot(raised.astype(jnp.bfloat16), vh, preferred_element_type=jnp.float32)
-            total = both[:, 127:128] if half == 0 else both[:, 0:1]
-            mixed.append(both * (1.0 / total))
+            both = jnp.dot(raised.astype(jnp.bfloat16), v, preferred_element_type=jnp.float32)
+            mixed.append(both * (1.0 / jnp.sum(raised, axis=-1, keepdims=True)))
         out_ref[:, at : at + 128] = jnp.where(low, mixed[0], mixed[1]).astype(jnp.bfloat16)
 
 
@@ -259,7 +263,9 @@
     for r in range(0, RH + WIN, 2):
         turned = []
         for ref, i in rows[r : r + 2]:
-            normed = norm_rows(ref[i].astype(jnp.float32), gain)
+            normed = ref[i].astype(jnp.float32)
+            if ref is not own_ref:
+                normed = norm_rows(normed, gain)
             turned.append([pltpu.roll(normed[j * 8 : j * 8 + 8], HALF, 0) for j in range(4)])
         for n in range(INNER):
             place([jnp.where(lower, row[n], row[n + 1]) for row in turned], INNER, r, n, xs, xq)
@@ -271,15 +277,10 @@
 
 
 def outer_kernel(
-    left_ref, right_ref, rims_ref, inner_ref, gain_ref, bias, hot_ref, w_ref,
-    out_ref, cap_ref, undo_ref, xs, xq, kv, qs, scores, weights, wout, edges, full,
+    left_ref, right_ref, rims_ref, inner_ref, gain_ref, bias, w_ref, out_ref, cap_ref, xs, xq, kv, qs, scores, weights, wout, edges, full,
 ):
     gain = gain_ref[...]
     lat = lax.axis_index("lat")
-
-    polar = (lat == 0) | (lat == lax.axis_size("lat") - 1)
-    undo = jnp.transpose(hot_ref[...].astype(jnp.float32))
-    undo_ref[...] = jnp.where(polar, undo, 0.0).astype(jnp.bfloat16)
 
     for side, ref in enumerate((left_ref, right_ref)):
         for i in range(0, 64, 32):
@@ -371,10 +372,15 @@
     tied, _ = lax.optimization_barrier((tokens, packed))
     north = lax.ppermute(tied[RH - HALF :], "lat", down)
     south = lax.ppermute(tied[:HALF], "lat", up)
-    bias, gain = call(
-        bias_kernel, (sds((2 * 128, 128), f32), sds((1, D), f32)), [vspec()] * 3, (vspec(), vspec()), [],
-        SOME_VMEM, 1 << 18, 1 << 18,
-    )(bias_table, bias_index, gain)
+    bias, gain, undo, normed = call(
+        bias_kernel,
+        (
+            sds((2 * 128, 128), f32), sds((1, D), f32), sds((CAP_TOKENS, SLOT_TOKENS), bf16),
+            sds((RH, RW, D), bf16),
+        ),
+        [vspec()] * 5, (vspec(),) * 4, [],
+        SOME_VMEM, 1 << 20, 3 << 19,
+    )(bias_table, bias_index, gain, hot, tokens)
     side = sds(((RH + WIN) * HALF, D), bf16)
     head, tail = call(
         edge_kernel, (side, side), [vspec()] * 3, (vspec(), vspec()), [],
@@ -406,15 +412,14 @@
         (sds((2 * INNER, QROWS, HW), f32), sds((2, (RH + WIN) * 8, D), bf16)),
         [vspec()] * 6, (vspec(), vspec()), scratch(2 * INNER),
         SOME_VMEM, 1400 << 20, 5 << 20, 1 << 17,
-    )(tokens, north, south, gain, bias, w_qkv)
-    win_out, cap_rows, undo = call(
+    )(normed, north, south, gain, bias, w_qkv)
+    win_out, cap_rows = call(
         outer_kernel,
-        (sds((RH * RW, HW), bf16), sds((CAP_TOKENS, HW), f32), sds((CAP_TOKENS, SLOT_TOKENS), bf16)),
-        [vspec()] * 8, (vspec(),) * 3,
+        (sds((RH * RW, HW), bf16), sds((CAP_TOKENS, HW), f32)), [vspec()] * 7, (vspec(),) * 2,
         scratch(2 * OUTER)
         + [VMEM((2 * OUTER, QROWS, HW), f32), VMEM((2, 64, D), f32), VMEM((RH * RW, HW), f32)],
         SOME_VMEM, 900 << 20, 5 << 20, 1 << 17,
-    )(left, right, rims, inner, gain, bias, hot, w_qkv)
+    )(left, right, rims, inner, gain, bias, w_qkv)
     mixed = call(
         join_kernel, sds((RH * RW, HW), bf16),
         [vspec()] * 3 + [aspec()], aspec(),

time: 57.4 us -> 59.1 us (1.030)
  starting transfers between devices: 32.2 us -> 35.1 us
  waiting for transfers between devices: 6.98 us -> 4.36 us
  local copies, waits for them, and re-layouts: 5.17 us -> 7.05 us
  Pallas kernels: 12.3 us -> 11.7 us
    all_to_all x2, starting transfers between devices: 17.1 us -> 20.1 us  [exchange(): return lax.all_to_all(block, 'lon', split_axis=0, concat_axis=0, tiled=True)]
    all_to_all x2, waiting for transfers between devices: 3.92 us -> 1.01 us  [exchange(): return lax.all_to_all(block, 'lon', split_axis=0, concat_axis=0, tiled=True)]
    unnamed x14 -> x16, local copies, waits for them, and re-layouts: 4.04 us -> 5.92 us
    pallas_call x1, Pallas kernels: 4.06 us -> 2.76 us  [layer(): call(cap_kernel, sds((SLOT_TOKENS, HW), bf16), [vspec()] * 3, vspec(), [V...]
    pallas_call x2, Pallas kernels: 2.82 us -> 3.84 us  [the longest x1 2.33 us: layer(): call(outer_kernel, (sds((RH * RW, HW), bf16), sds((CAP_TOKENS, HW), f32))...]
  transfers between devices with their start and end apart: 6 -> 6, of which waited for: 2 -> 2; matrix products, arithmetic and copies ran while one was open for 2% -> 2% of each run, Pallas kernels for 17% -> 15%
where the time goes in v7:
time: 59.1 us; the launch traced here: 58.4 us
  starting transfers between devices  35.1 us (59%)
  Pallas kernels  11.7 us (20%)
  local copies, waits for them, and re-layouts  7.05 us (12%)
  waiting for transfers between devices  4.36 us (7%)
    all_to_all x2, starting transfers between devices, exchange(): return lax.all_to_all(block, 'lon', split_axis=0, concat_axis=0, tiled=True)  20.1 us
    ppermute x1, starting transfers between devices, layer(): north = lax.ppermute(tied[RH - HALF:], 'lat', down)  7.05 us
    unnamed x16, local copies, waits for them, and re-layouts  5.92 us
    ppermute x1, starting transfers between devices, layer(): left = lax.ppermute(tail, 'lon', east)  3.63 us
    ppermute x1, waiting for transfers between devices, layer(): right = lax.ppermute(head, 'lon', west)  3.34 us
    pallas_call x1, Pallas kernels, layer(): call(cap_kernel, sds((SLOT_TOKENS, HW), bf16), [vspec()] * 3, vspec(), [V...  2.76 us
    ppermute x1, starting transfers between devices, layer(): south = lax.ppermute(tied[:HALF], 'lat', up)  2.45 us
    pallas_call x1, Pallas kernels, layer(): call(outer_kernel, (sds((RH * RW, HW), bf16), sds((CAP_TOKENS, HW), f32))...  2.33 us
  transfers between devices with their start and end apart: 6, of which 2 were waited for; matrix products, arithmetic and copies ran while one was open for 2% of the time, Pallas kernels for 15%

profile of v7, /device:TPU:31, one launch (start us, length us, event | category | flops | bytes accessed | tf_op | source)
XLA Modules:
  0.0 58.4 jit_solution(525262501907870088)
XLA Ops:
  0.0 2.0 %shard_map.64 = (bf16[256,1024]{1,0:T(8,128)(2,1)}, bf16[256,128]{1,0:T(8,128)(2,1)}) custom-call(s32[2,4,1,8]{3,2,1,0:T(1,128)} %bitcast.11, bf16[8,32,1024]{2,1,0:T(8,128)(2,1)} %own_ref.3), custom_call_target="tpu_custom_call" | custom-call | flops 67108864 | bytes 1048576 | tf_op jit(solution)/shard_map/pallas_call | solution.py:352
  2.0 12.2 %all-to-all-start = ((bf16[32,8,1024]{2,1,0:T(8,128)(2,1)}), bf16[32,8,1024]{2,1,0:T(8,128)(2,1)S(1)}, u32[]{:S(2)}, u32[]{:S(2)}) async-start(bf16[32,8,1024]{2,1,0:T(8,128)(2,1)} %bitcast.10), calls=%async_computation | async-start | bytes 1048576 | tf_op jit(solution)/shard_map/all_to_all | solution.py:342
  14.3 0.0 copy-start.1
  14.3 1.1 %fusion = (bf16[4,32,1024]{2,1,0:T(8,128)(2,1)S(1)}, bf16[4,32,1024]{2,1,0:T(8,128)(2,1)S(1)}) fusion(bf16[8,32,1024]{2,1,0:T(8,128)(2,1)} %own_ref.3), kind=kLoop, calls=%fused_computation | loop fusion | bytes 1048576 | tf_op jit(solution)/shard_map/slice | solution.py:374
  15.4 2.5 %collective-permute-start.1 = (bf16[4,32,1024]{2,1,0:T(8,128)(2,1)S(1)}, bf16[4,32,1024]{2,1,0:T(8,128)(2,1)S(1)}, u32[]{:S(2)}, u32[]{:S(2)}) collective-permute-start(bf16[4,32,1024]{2,1,0:T(8,128)(2,1)S(1)} %get-tuple-element.31), channel_id=1, source_target_pairs={{32,0},{64,32},{96,64},{128,96},{160,128},{192,160},{224,192},{256... | collective-permute-start | bytes 786440 | tf_op jit(solution)/shard_map/ppermute | solution.py:374
  17.9 7.0 %collective-permute-start = (bf16[4,32,1024]{2,1,0:T(8,128)(2,1)S(1)}, bf16[4,32,1024]{2,1,0:T(8,128)(2,1)S(1)}, u32[]{:S(2)}, u32[]{:S(2)}) collective-permute-start(bf16[4,32,1024]{2,1,0:T(8,128)(2,1)S(1)} %get-tuple-element.32), channel_id=1, source_target_pairs={{0,32},{32,64},{64,96},{96,128},{128,160},{160,192},{192,224},{224... | collective-permute-start | bytes 786440 | tf_op jit(solution)/shard_map/ppermute | solution.py:373
  24.9 0.0 copy-start
  24.9 1.0 %copy-done = bf16[8,32,1024]{2,1,0:T(8,128)(2,1)S(1)} copy-done((bf16[8,32,1024]{2,1,0:T(8,128)(2,1)S(1)}, bf16[8,32,1024]{2,1,0:T(8,128)(2,1)}, u32[]{:S(2)}) %copy-start) | copy-done | bytes 524312
  26.0 0.0 copy-start.4
  26.0 0.8 %copy-done.4 = bf16[256,128]{1,0:T(8,128)(2,1)S(1)} copy-done((bf16[256,128]{1,0:T(8,128)(2,1)S(1)}, bf16[256,128]{1,0:T(8,128)(2,1)}, u32[]{:S(2)}) %copy-start.4) | copy-done | bytes 65560
  26.8 0.8 %copy-done.5 = s32[64,64]{1,0:T(8,128)S(1)} copy-done((s32[64,64]{1,0:T(8,128)S(1)}, s32[64,64]{1,0:T(8,128)}, u32[]{:S(2)}) %copy-start.5) | copy-done | bytes 16408
  27.6 0.7 %copy-done.6 = f32[8,225]{1,0:T(8,128)S(1)} copy-done((f32[8,225]{1,0:T(8,128)S(1)}, f32[8,225]{1,0:T(8,128)}, u32[]{:S(2)}) %copy-start.6) | copy-done | bytes 7224
  28.3 0.7 %copy-done.7 = f32[1024]{0:T(1024)S(1)} copy-done((f32[1024]{0:T(1024)S(1)}, f32[1024]{0:T(1024)}, u32[]{:S(2)}) %copy-start.7) | copy-done | bytes 4120
  29.0 1.5 %shard_map.66 = (f32[256,128]{1,0:T(8,128)S(1)}, f32[1,1024]{1,0:T(1,128)S(1)}, bf16[128,256]{1,0:T(8,128)(2,1)S(1)}, bf16[8,32,1024]{2,1,0:T(8,128)(2,1)S(1)}) custom-call(f32[8,225]{1,0:T(8,128)S(1)} %copy-done.6, s32[64,64]{1,0:T(8,128)S(1)} %copy-done.5, f32[1,1024]{1,0:T(1,128)S(1)} %bitcast.9, bf16[256,128]{1,0:T(8,128)(2,1)S(1)} %copy-done.4, ...), custom_call_target="tpu_custom_call" | custom-call | flops 1048576 | bytes 1572864 | tf_op jit(solution)/shard_map/pallas_call | solution.py:375
  30.5 1.0 %all-to-all-done = bf16[32,8,1024]{2,1,0:T(8,128)(2,1)S(1)} async-done(((bf16[32,8,1024]{2,1,0:T(8,128)(2,1)}), bf16[32,8,1024]{2,1,0:T(8,128)(2,1)S(1)}, u32[]{:S(2)}, u32[]{:S(2)}) %all-to-all-start) | async-done | bytes 524320 | tf_op jit(solution)/shard_map/all_to_all | solution.py:342
  31.5 1.9 %copy-done.2 = bf16[1024,1536]{1,0:T(8,128)(2,1)S(1)} copy-done((bf16[1024,1536]{1,0:T(8,128)(2,1)S(1)}, bf16[1024,1536]{1,0:T(8,128)(2,1)}, u32[]{:S(2)}) %copy-start.2) | copy-done | bytes 3145752
  33.4 2.8 %shard_map.69 = bf16[256,512]{1,0:T(8,128)(2,1)} custom-call(bf16[256,1024]{1,0:T(8,128)(2,1)S(1)} %bitcast.8, f32[1,1024]{1,0:T(1,128)S(1)} %get-tuple-element.24.gain_ref, bf16[1024,1536]{1,0:T(8,128)(2,1)S(1)} %copy-done.2), custom_call_target="tpu_custom_call" | custom-call | flops 1153433600 | bytes 4194304 | tf_op jit(solution)/shard_map/pallas_call | solution.py:392
  36.1 7.8 %all-to-all-start.1 = ((bf16[32,8,512]{2,1,0:T(8,128)(2,1)}), bf16[32,8,512]{2,1,0:T(8,128)(2,1)S(1)}, u32[]{:S(2)}, u32[]{:S(2)}) async-start(bf16[32,8,512]{2,1,0:T(8,128)(2,1)} %bitcast.4), calls=%async_computation.1 | async-start | bytes 524288 | tf_op jit(solution)/shard_map/all_to_all | solution.py:342
  44.0 0.0 copy-start.3
  44.0 0.0 collective-permute-done.1.south_ref
  44.0 0.0 collective-permute-done.north_ref
  44.0 0.0 copy-done.1
  44.0 0.1 shard_map.65
  44.1 3.6 %collective-permute-start.2 = (bf16[64,1024]{1,0:T(8,128)(2,1)S(1)}, bf16[64,1024]{1,0:T(8,128)(2,1)S(1)}, u32[]{:S(2)}, u32[]{:S(2)}) collective-permute-start(bf16[64,1024]{1,0:T(8,128)(2,1)S(1)} %get-tuple-element.20), channel_id=1, source_target_pairs={{0,1},{1,2},{2,3},{3,4},{4,5},{5,6},{6,7},{7,8},{8,9},{9,10},{10,1... | collective-permute-start | bytes 393224 | tf_op jit(solution)/shard_map/ppermute | solution.py:389
  47.8 1.9 %collective-permute-start.3 = (bf16[64,1024]{1,0:T(8,128)(2,1)S(1)}, bf16[64,1024]{1,0:T(8,128)(2,1)S(1)}, u32[]{:S(2)}, u32[]{:S(2)}) collective-permute-start(bf16[64,1024]{1,0:T(8,128)(2,1)S(1)} %get-tuple-element.21), channel_id=1, source_target_pairs={{1,0},{2,1},{3,2},{4,3},{5,4},{6,5},{7,6},{8,7},{9,8},{10,9},{11,1... | collective-permute-start | bytes 393224 | tf_op jit(solution)/shard_map/ppermute | solution.py:390
  49.7 0.0 copy-done.3
  49.7 2.2 %shard_map.67 = (f32[6,32,512]{2,1,0:T(8,128)S(1)}, bf16[2,128,1024]{2,1,0:T(8,128)(2,1)S(1)}) custom-call(bf16[8,32,1024]{2,1,0:T(8,128)(2,1)S(1)} %get-tuple-element.23.own_ref, bf16[4,32,1024]{2,1,0:T(8,128)(2,1)S(1)} %collective-permute-done.north_ref, bf16[4,32,1024]{2,1,0:T(8,128)(2,1)S(1)} %collective-permute-done.1.south_ref, ...), custom_call_target="tpu_custom_call" | custom-call | flops 1468006400 | bytes 5242880 | tf_op jit(solution)/shard_map/pallas_call | solution.py:410
  51.9 0.0 collective-permute-done.2.left_ref
  51.9 3.3 %collective-permute-done.3.right_ref = bf16[64,1024]{1,0:T(8,128)(2,1)S(1)} collective-permute-done((bf16[64,1024]{1,0:T(8,128)(2,1)S(1)}, bf16[64,1024]{1,0:T(8,128)(2,1)S(1)}, u32[]{:S(2)}, u32[]{:S(2)}) %collective-permute-start.3) | collective-permute-done | bytes 131104 | tf_op jit(solution)/shard_map/ppermute | solution.py:390
  55.2 2.3 %shard_map.68 = (bf16[256,512]{1,0:T(8,128)(2,1)}, f32[128,512]{1,0:T(8,128)S(1)}) custom-call(bf16[64,1024]{1,0:T(8,128)(2,1)S(1)} %collective-permute-done.2.left_ref, bf16[64,1024]{1,0:T(8,128)(2,1)S(1)} %collective-permute-done.3.right_ref, bf16[2,128,1024]{2,1,0:T(8,128)(2,1)S(1)} %get-tuple-element.26.rims_ref, ...), custom_call_target="tpu_custom_call" | custom-call | flops 943718400 | bytes 5242880 | tf_op jit(solution)/shard_map/pallas_call | solution.py:416
  57.6 0.0 all-to-all-done.1
  57.6 0.9 %shard_map.70 = bf16[256,512]{1,0:T(8,128)(2,1)} custom-call(f32[128,512]{1,0:T(8,128)S(1)} %get-tuple-element.28.win_ref, bf16[256,512]{1,0:T(8,128)(2,1)S(1)} %bitcast.7, bf16[128,256]{1,0:T(8,128)(2,1)S(1)} %get-tuple-element.29.undo_ref, bf16[256,512]{1,0:T(8,128)(2,1)} %get-tuple-element.30.out_in), custom_call_target="tpu_custom_call", output_to_operand_aliasing={{}: (3, {})} | custom-call | flops 33554432 | bytes 524288 | tf_op jit(solution)/shard_map/pallas_call | solution.py:423
  (4 shorter events, 0.0 us)
Async XLA Ops:
  2.0 29.5 %all-to-all-start = ((bf16[32,8,1024]{2,1,0:T(8,128)(2,1)}), bf16[32,8,1024]{2,1,0:T(8,128)(2,1)S(1)}, u32[]{:S(2)}, u32[]{:S(2)}) async-start(bf16[32,8,1024]{2,1,0:T(8,128)(2,1)} %bitcast.10), calls=%async_computation | async-start | bytes 1048576 | tf_op jit(solution)/shard_map/all_to_all | solution.py:342
  14.3 29.8 %copy-start.1 = (bf16[8,32,1024]{2,1,0:T(8,128)(2,1)S(1)}, bf16[8,32,1024]{2,1,0:T(8,128)(2,1)}, u32[]{:S(2)}) copy-start(bf16[8,32,1024]{2,1,0:T(8,128)(2,1)} %own_ref.3) | copy-start | bytes 1572868
  15.4 28.6 %collective-permute-start.1 = (bf16[4,32,1024]{2,1,0:T(8,128)(2,1)S(1)}, bf16[4,32,1024]{2,1,0:T(8,128)(2,1)S(1)}, u32[]{:S(2)}, u32[]{:S(2)}) collective-permute-start(bf16[4,32,1024]{2,1,0:T(8,128)(2,1)S(1)} %get-tuple-element.31), channel_id=1, source_target_pairs={{32,0},{64,32},{96,64},{128,96},{160,128},{192,160},{224,192},{256... | collective-permute-start | bytes 786440 | tf_op jit(solution)/shard_map/ppermute | solution.py:374
  17.9 26.1 %collective-permute-start = (bf16[4,32,1024]{2,1,0:T(8,128)(2,1)S(1)}, bf16[4,32,1024]{2,1,0:T(8,128)(2,1)S(1)}, u32[]{:S(2)}, u32[]{:S(2)}) collective-permute-start(bf16[4,32,1024]{2,1,0:T(8,128)(2,1)S(1)} %get-tuple-element.32), channel_id=1, source_target_pairs={{0,32},{32,64},{64,96},{96,128},{128,160},{160,192},{192,224},{224... | collective-permute-start | bytes 786440 | tf_op jit(solution)/shard_map/ppermute | solution.py:373
  24.9 1.0 %copy-start = (bf16[8,32,1024]{2,1,0:T(8,128)(2,1)S(1)}, bf16[8,32,1024]{2,1,0:T(8,128)(2,1)}, u32[]{:S(2)}) copy-start(bf16[8,32,1024]{2,1,0:T(8,128)(2,1)} %own_ref.3) | copy-start | bytes 1572868
  26.0 0.8 %copy-start.4 = (bf16[256,128]{1,0:T(8,128)(2,1)S(1)}, bf16[256,128]{1,0:T(8,128)(2,1)}, u32[]{:S(2)}) copy-start(bf16[256,128]{1,0:T(8,128)(2,1)} %get-tuple-element.22.hot_ref) | copy-start | bytes 196612
  26.8 0.8 %copy-start.5 = (s32[64,64]{1,0:T(8,128)S(1)}, s32[64,64]{1,0:T(8,128)}, u32[]{:S(2)}) copy-start(s32[64,64]{1,0:T(8,128)} %index_ref.1) | copy-start | bytes 49156
  27.6 0.7 %copy-start.6 = (f32[8,225]{1,0:T(8,128)S(1)}, f32[8,225]{1,0:T(8,128)}, u32[]{:S(2)}) copy-start(f32[8,225]{1,0:T(8,128)} %table_ref.1) | copy-start | bytes 21604
  28.3 0.7 %copy-start.7 = (f32[1024]{0:T(1024)S(1)}, f32[1024]{0:T(1024)}, u32[]{:S(2)}) copy-start(f32[1024]{0:T(1024)} %param.7) | copy-start | bytes 12292
  31.5 1.9 %copy-start.2 = (bf16[1024,1536]{1,0:T(8,128)(2,1)S(1)}, bf16[1024,1536]{1,0:T(8,128)(2,1)}, u32[]{:S(2)}) copy-start(bf16[1024,1536]{1,0:T(8,128)(2,1)} %w_ref.5) | copy-start | bytes 9437188
  36.1 21.4 %all-to-all-start.1 = ((bf16[32,8,512]{2,1,0:T(8,128)(2,1)}), bf16[32,8,512]{2,1,0:T(8,128)(2,1)S(1)}, u32[]{:S(2)}, u32[]{:S(2)}) async-start(bf16[32,8,512]{2,1,0:T(8,128)(2,1)} %bitcast.4), calls=%async_computation.1 | async-start | bytes 524288 | tf_op jit(solution)/shard_map/all_to_all | solution.py:342
  44.0 5.7 %copy-start.3 = (bf16[1024,1536]{1,0:T(8,128)(2,1)S(1)}, bf16[1024,1536]{1,0:T(8,128)(2,1)}, u32[]{:S(2)}) copy-start(bf16[1024,1536]{1,0:T(8,128)(2,1)} %w_ref.5) | copy-start | bytes 9437188
  44.1 7.8 %collective-permute-start.2 = (bf16[64,1024]{1,0:T(8,128)(2,1)S(1)}, bf16[64,1024]{1,0:T(8,128)(2,1)S(1)}, u32[]{:S(2)}, u32[]{:S(2)}) collective-permute-start(bf16[64,1024]{1,0:T(8,128)(2,1)S(1)} %get-tuple-element.20), channel_id=1, source_target_pairs={{0,1},{1,2},{2,3},{3,4},{4,5},{5,6},{6,7},{7,8},{8,9},{9,10},{10,1... | collective-permute-start | bytes 393224 | tf_op jit(solution)/shard_map/ppermute | solution.py:389
  47.8 7.5 %collective-permute-start.3 = (bf16[64,1024]{1,0:T(8,128)(2,1)S(1)}, bf16[64,1024]{1,0:T(8,128)(2,1)S(1)}, u32[]{:S(2)}, u32[]{:S(2)}) collective-permute-start(bf16[64,1024]{1,0:T(8,128)(2,1)S(1)} %get-tuple-element.21), channel_id=1, source_target_pairs={{1,0},{2,1},{3,2},{4,3},{5,4},{6,5},{7,6},{8,7},{9,8},{10,9},{11,1... | collective-permute-start | bytes 393224 | tf_op jit(solution)/shard_map/ppermute | solution.py:390

commit v8 on v6

--- a/solution.py
+++ b/solution.py
@@ -182,10 +182,8 @@
             s = lax.dot_general(qh, k, (((1,), (1,)), ((), ())), preferred_element_type=jnp.float32)
             s = s + empty
             raised = jnp.exp(s - jnp.max(s, axis=-1, keepdims=True))
-            vh = jnp.where(mine, v, jnp.ones_like(v))
-            both = jnp.dot(raised.astype(jnp.bfloat16), vh, preferred_element_type=jnp.float32)
-            total = both[:, 127:128] if half == 0 else both[:, 0:1]
-            mixed.append(both * (1.0 / total))
+            both = jnp.dot(raised.astype(jnp.bfloat16), v, preferred_element_type=jnp.float32)
+            mixed.append(both * (1.0 / jnp.sum(raised, axis=-1, keepdims=True)))
         out_ref[:, at : at + 128] = jnp.where(low, mixed[0], mixed[1]).astype(jnp.bfloat16)
 
 
@@ -360,7 +358,7 @@
             pltpu.SemaphoreType.DMA,
             pltpu.SemaphoreType.DMA((SLOT_TOKENS // PACK_STEP + 1,)),
         ],
-        PACK_VMEM, 2 * SLOT_TOKENS * CAP_TOKENS * D, 1 << 20,
+        PACK_VMEM, 4 << 30, 1 << 20,
     )(groups, tokens)
     arrived = exchange(packed.reshape(lon_count, MOST * TW, D)).reshape(SLOT_TOKENS, D)
 

time: 57.4 us -> 55.3 us (0.963)
  the two profiles are of different devices: /device:TPU:31 before, /device:TPU:1 now
where the time goes in v8:
time: 55.3 us; the launch traced here: 54.9 us
  starting transfers between devices  28.9 us (52%)
  waiting for transfers between devices  11.7 us (21%)
  Pallas kernels  11.1 us (20%)
  local copies, waits for them, and re-layouts  3.05 us (6%)
    all_to_all x2, starting transfers between devices, exchange(): return lax.all_to_all(block, 'lon', split_axis=0, concat_axis=0, tiled=True)  17.9 us
    all_to_all x2, waiting for transfers between devices, exchange(): return lax.all_to_all(block, 'lon', split_axis=0, concat_axis=0, tiled=True)  9.54 us
    ppermute x1, starting transfers between devices, layer(): north = lax.ppermute(tied[RH - HALF:], 'lat', down)  4 us
    ppermute x1, starting transfers between devices, layer(): left = lax.ppermute(tail, 'lon', east)  3.81 us
    pallas_call x1, Pallas kernels, layer(): call(cap_kernel, sds((SLOT_TOKENS, HW), bf16), [vspec()] * 3, vspec(), [V...  2.77 us
    pallas_call x1, Pallas kernels, layer(): call(inner_kernel, (sds((2 * INNER, QROWS, HW), f32), sds((2, (RH + WIN)...  2.48 us
    pallas_call x1, Pallas kernels, layer(): call(outer_kernel, (sds((RH * RW, HW), bf16), sds((CAP_TOKENS, HW), f32),...  2.33 us
    ppermute x1, waiting for transfers between devices, layer(): right = lax.ppermute(head, 'lon', west)  2.15 us
  transfers between devices with their start and end apart: 6, of which 2 were waited for; matrix products, arithmetic and copies ran while one was open for 2% of the time, Pallas kernels for 15%

profile of v8, /device:TPU:1, one launch (start us, length us, event | category | flops | bytes accessed | tf_op | source)
XLA Modules:
  0.0 54.9 jit_solution(5651265966685093922)
XLA Ops:
  0.0 0.0 copy-start.5
  0.0 0.0 copy-start.6
  0.0 2.1 %shard_map.64 = (bf16[256,1024]{1,0:T(8,128)(2,1)}, bf16[256,128]{1,0:T(8,128)(2,1)}) custom-call(s32[2,4,1,8]{3,2,1,0:T(1,128)} %bitcast.11, bf16[8,32,1024]{2,1,0:T(8,128)(2,1)} %own_ref.3), custom_call_target="tpu_custom_call" | custom-call | flops 4294967296 | bytes 1048576 | tf_op jit(solution)/shard_map/pallas_call | solution.py:349
  2.1 13.0 %all-to-all-start = ((bf16[32,8,1024]{2,1,0:T(8,128)(2,1)}), bf16[32,8,1024]{2,1,0:T(8,128)(2,1)S(1)}, u32[]{:S(2)}, u32[]{:S(2)}) async-start(bf16[32,8,1024]{2,1,0:T(8,128)(2,1)} %bitcast.10), calls=%async_computation | async-start | bytes 1048576 | tf_op jit(solution)/shard_map/all_to_all | solution.py:339
  15.1 0.0 copy-start.2
  15.1 1.1 %fusion = (bf16[4,32,1024]{2,1,0:T(8,128)(2,1)S(1)}, bf16[4,32,1024]{2,1,0:T(8,128)(2,1)S(1)}) fusion(bf16[8,32,1024]{2,1,0:T(8,128)(2,1)} %own_ref.3), kind=kLoop, calls=%fused_computation | loop fusion | bytes 1048576 | tf_op jit(solution)/shard_map/slice | solution.py:371
  16.2 1.3 %collective-permute-start.1 = (bf16[4,32,1024]{2,1,0:T(8,128)(2,1)S(1)}, bf16[4,32,1024]{2,1,0:T(8,128)(2,1)S(1)}, u32[]{:S(2)}, u32[]{:S(2)}) collective-permute-start(bf16[4,32,1024]{2,1,0:T(8,128)(2,1)S(1)} %get-tuple-element.29), channel_id=1, source_target_pairs={{32,0},{64,32},{96,64},{128,96},{160,128},{192,160},{224,192},{256... | collective-permute-start | bytes 786440 | tf_op jit(solution)/shard_map/ppermute | solution.py:371
  17.5 4.0 %collective-permute-start = (bf16[4,32,1024]{2,1,0:T(8,128)(2,1)S(1)}, bf16[4,32,1024]{2,1,0:T(8,128)(2,1)S(1)}, u32[]{:S(2)}, u32[]{:S(2)}) collective-permute-start(bf16[4,32,1024]{2,1,0:T(8,128)(2,1)S(1)} %get-tuple-element.30), channel_id=1, source_target_pairs={{0,32},{32,64},{64,96},{96,128},{128,160},{160,192},{192,224},{224... | collective-permute-start | bytes 786440 | tf_op jit(solution)/shard_map/ppermute | solution.py:370
  21.5 0.0 copy-done.4
  21.5 0.0 copy-done.5
  21.5 0.0 copy-done.6
  21.6 0.5 shard_map.66
  22.1 9.5 %all-to-all-done = bf16[32,8,1024]{2,1,0:T(8,128)(2,1)S(1)} async-done(((bf16[32,8,1024]{2,1,0:T(8,128)(2,1)}), bf16[32,8,1024]{2,1,0:T(8,128)(2,1)S(1)}, u32[]{:S(2)}, u32[]{:S(2)}) %all-to-all-start) | async-done | bytes 524320 | tf_op jit(solution)/shard_map/all_to_all | solution.py:339
  31.6 1.9 %copy-done = bf16[1024,1536]{1,0:T(8,128)(2,1)S(1)} copy-done((bf16[1024,1536]{1,0:T(8,128)(2,1)S(1)}, bf16[1024,1536]{1,0:T(8,128)(2,1)}, u32[]{:S(2)}) %copy-start) | copy-done | bytes 3145752
  33.5 2.8 %shard_map.69 = bf16[256,512]{1,0:T(8,128)(2,1)} custom-call(bf16[256,1024]{1,0:T(8,128)(2,1)S(1)} %bitcast.8, f32[1,1024]{1,0:T(1,128)S(1)} %get-tuple-element.21.gain_ref, bf16[1024,1536]{1,0:T(8,128)(2,1)S(1)} %copy-done), custom_call_target="tpu_custom_call" | custom-call | flops 1153433600 | bytes 4194304 | tf_op jit(solution)/shard_map/pallas_call | solution.py:384
  36.2 4.9 %all-to-all-start.1 = ((bf16[32,8,512]{2,1,0:T(8,128)(2,1)}), bf16[32,8,512]{2,1,0:T(8,128)(2,1)S(1)}, u32[]{:S(2)}, u32[]{:S(2)}) async-start(bf16[32,8,512]{2,1,0:T(8,128)(2,1)} %bitcast.4), calls=%async_computation.1 | async-start | bytes 524288 | tf_op jit(solution)/shard_map/all_to_all | solution.py:339
  41.1 0.0 copy-start.1
  41.2 0.0 collective-permute-done.1.south_ref
  41.2 0.0 collective-permute-done.north_ref
  41.2 0.0 copy-done.2
  41.2 0.1 shard_map.65
  41.3 0.0 copy-start.3
  41.3 3.8 %collective-permute-start.2 = (bf16[64,1024]{1,0:T(8,128)(2,1)S(1)}, bf16[64,1024]{1,0:T(8,128)(2,1)S(1)}, u32[]{:S(2)}, u32[]{:S(2)}) collective-permute-start(bf16[64,1024]{1,0:T(8,128)(2,1)S(1)} %get-tuple-element.19), channel_id=1, source_target_pairs={{0,1},{1,2},{2,3},{3,4},{4,5},{5,6},{6,7},{7,8},{8,9},{9,10},{10,1... | collective-permute-start | bytes 393224 | tf_op jit(solution)/shard_map/ppermute | solution.py:381
  45.1 1.9 %collective-permute-start.3 = (bf16[64,1024]{1,0:T(8,128)(2,1)S(1)}, bf16[64,1024]{1,0:T(8,128)(2,1)S(1)}, u32[]{:S(2)}, u32[]{:S(2)}) collective-permute-start(bf16[64,1024]{1,0:T(8,128)(2,1)S(1)} %get-tuple-element.20), channel_id=1, source_target_pairs={{1,0},{2,1},{3,2},{4,3},{5,4},{6,5},{7,6},{8,7},{9,8},{10,9},{11,1... | collective-permute-start | bytes 393224 | tf_op jit(solution)/shard_map/ppermute | solution.py:382
  47.0 0.0 copy-done.1
  47.0 2.5 %shard_map.67 = (f32[6,32,512]{2,1,0:T(8,128)S(1)}, bf16[2,128,1024]{2,1,0:T(8,128)(2,1)S(1)}) custom-call(bf16[8,32,1024]{2,1,0:T(8,128)(2,1)S(1)} %copy-done.2, bf16[4,32,1024]{2,1,0:T(8,128)(2,1)S(1)} %collective-permute-done.north_ref, bf16[4,32,1024]{2,1,0:T(8,128)(2,1)S(1)} %collective-permute-done.1.south_ref, ...), custom_call_target="tpu_custom_call" | custom-call | flops 1468006400 | bytes 5242880 | tf_op jit(solution)/shard_map/pallas_call | solution.py:402
  49.5 0.0 collective-permute-done.2.left_ref
  49.5 2.1 %collective-permute-done.3.right_ref = bf16[64,1024]{1,0:T(8,128)(2,1)S(1)} collective-permute-done((bf16[64,1024]{1,0:T(8,128)(2,1)S(1)}, bf16[64,1024]{1,0:T(8,128)(2,1)S(1)}, u32[]{:S(2)}, u32[]{:S(2)}) %collective-permute-start.3) | collective-permute-done | bytes 131104 | tf_op jit(solution)/shard_map/ppermute | solution.py:382
  51.7 0.0 copy-done.3
  51.7 2.3 %shard_map.68 = (bf16[256,512]{1,0:T(8,128)(2,1)}, f32[128,512]{1,0:T(8,128)S(1)}, bf16[128,256]{1,0:T(8,128)(2,1)S(1)}) custom-call(bf16[64,1024]{1,0:T(8,128)(2,1)S(1)} %collective-permute-done.2.left_ref, bf16[64,1024]{1,0:T(8,128)(2,1)S(1)} %collective-permute-done.3.right_ref, bf16[2,128,1024]{2,1,0:T(8,128)(2,1)S(1)} %get-tuple-element.23.rims_ref, ...), custom_call_target="tpu_custom_call" | custom-call | flops 943718400 | bytes 5242880 | tf_op jit(solution)/shard_map/pallas_call | solution.py:408
  54.0 0.0 all-to-all-done.1
  54.0 0.9 %shard_map.70 = bf16[256,512]{1,0:T(8,128)(2,1)} custom-call(f32[128,512]{1,0:T(8,128)S(1)} %get-tuple-element.26.win_ref, bf16[256,512]{1,0:T(8,128)(2,1)S(1)} %bitcast.7, bf16[128,256]{1,0:T(8,128)(2,1)S(1)} %get-tuple-element.27.undo_ref, bf16[256,512]{1,0:T(8,128)(2,1)} %get-tuple-element.28.out_in), custom_call_target="tpu_custom_call", output_to_operand_aliasing={{}: (3, {})} | custom-call | flops 33554432 | bytes 524288 | tf_op jit(solution)/shard_map/pallas_call | solution.py:416
  (2 shorter events, 0.0 us)
Async XLA Ops:
  0.0 21.5 %copy-start.4 = (s32[64,64]{1,0:T(8,128)S(1)}, s32[64,64]{1,0:T(8,128)}, u32[]{:S(2)}) copy-start(s32[64,64]{1,0:T(8,128)} %index_ref.1) | copy-start | bytes 49156
  0.0 21.5 %copy-start.5 = (f32[8,225]{1,0:T(8,128)S(1)}, f32[8,225]{1,0:T(8,128)}, u32[]{:S(2)}) copy-start(f32[8,225]{1,0:T(8,128)} %table_ref.1) | copy-start | bytes 21604
  0.0 21.5 %copy-start.6 = (f32[1024]{0:T(1024)S(1)}, f32[1024]{0:T(1024)}, u32[]{:S(2)}) copy-start(f32[1024]{0:T(1024)} %param.7) | copy-start | bytes 12292
  2.1 29.5 %all-to-all-start = ((bf16[32,8,1024]{2,1,0:T(8,128)(2,1)}), bf16[32,8,1024]{2,1,0:T(8,128)(2,1)S(1)}, u32[]{:S(2)}, u32[]{:S(2)}) async-start(bf16[32,8,1024]{2,1,0:T(8,128)(2,1)} %bitcast.10), calls=%async_computation | async-start | bytes 1048576 | tf_op jit(solution)/shard_map/all_to_all | solution.py:339
  15.1 26.1 %copy-start.2 = (bf16[8,32,1024]{2,1,0:T(8,128)(2,1)S(1)}, bf16[8,32,1024]{2,1,0:T(8,128)(2,1)}, u32[]{:S(2)}) copy-start(bf16[8,32,1024]{2,1,0:T(8,128)(2,1)} %own_ref.3) | copy-start | bytes 1572868
  16.2 24.9 %collective-permute-start.1 = (bf16[4,32,1024]{2,1,0:T(8,128)(2,1)S(1)}, bf16[4,32,1024]{2,1,0:T(8,128)(2,1)S(1)}, u32[]{:S(2)}, u32[]{:S(2)}) collective-permute-start(bf16[4,32,1024]{2,1,0:T(8,128)(2,1)S(1)} %get-tuple-element.29), channel_id=1, source_target_pairs={{32,0},{64,32},{96,64},{128,96},{160,128},{192,160},{224,192},{256... | collective-permute-start | bytes 786440 | tf_op jit(solution)/shard_map/ppermute | solution.py:371
  17.5 23.7 %collective-permute-start = (bf16[4,32,1024]{2,1,0:T(8,128)(2,1)S(1)}, bf16[4,32,1024]{2,1,0:T(8,128)(2,1)S(1)}, u32[]{:S(2)}, u32[]{:S(2)}) collective-permute-start(bf16[4,32,1024]{2,1,0:T(8,128)(2,1)S(1)} %get-tuple-element.30), channel_id=1, source_target_pairs={{0,32},{32,64},{64,96},{96,128},{128,160},{160,192},{192,224},{224... | collective-permute-start | bytes 786440 | tf_op jit(solution)/shard_map/ppermute | solution.py:370
  31.6 1.9 %copy-start = (bf16[1024,1536]{1,0:T(8,128)(2,1)S(1)}, bf16[1024,1536]{1,0:T(8,128)(2,1)}, u32[]{:S(2)}) copy-start(bf16[1024,1536]{1,0:T(8,128)(2,1)} %w_ref.5) | copy-start | bytes 9437188
  36.2 17.8 %all-to-all-start.1 = ((bf16[32,8,512]{2,1,0:T(8,128)(2,1)}), bf16[32,8,512]{2,1,0:T(8,128)(2,1)S(1)}, u32[]{:S(2)}, u32[]{:S(2)}) async-start(bf16[32,8,512]{2,1,0:T(8,128)(2,1)} %bitcast.4), calls=%async_computation.1 | async-start | bytes 524288 | tf_op jit(solution)/shard_map/all_to_all | solution.py:339
  41.1 5.9 %copy-start.1 = (bf16[1024,1536]{1,0:T(8,128)(2,1)S(1)}, bf16[1024,1536]{1,0:T(8,128)(2,1)}, u32[]{:S(2)}) copy-start(bf16[1024,1536]{1,0:T(8,128)(2,1)} %w_ref.5) | copy-start | bytes 9437188
  41.3 10.4 %copy-start.3 = (bf16[256,128]{1,0:T(8,128)(2,1)S(1)}, bf16[256,128]{1,0:T(8,128)(2,1)}, u32[]{:S(2)}) copy-start(bf16[256,128]{1,0:T(8,128)(2,1)} %get-tuple-element.25.hot_ref) | copy-start | bytes 196612
  41.3 8.2 %collective-permute-start.2 = (bf16[64,1024]{1,0:T(8,128)(2,1)S(1)}, bf16[64,1024]{1,0:T(8,128)(2,1)S(1)}, u32[]{:S(2)}, u32[]{:S(2)}) collective-permute-start(bf16[64,1024]{1,0:T(8,128)(2,1)S(1)} %get-tuple-element.19), channel_id=1, source_target_pairs={{0,1},{1,2},{2,3},{3,4},{4,5},{5,6},{6,7},{7,8},{8,9},{9,10},{10,1... | collective-permute-start | bytes 393224 | tf_op jit(solution)/shard_map/ppermute | solution.py:381
  45.1 6.6 %collective-permute-start.3 = (bf16[64,1024]{1,0:T(8,128)(2,1)S(1)}, bf16[64,1024]{1,0:T(8,128)(2,1)S(1)}, u32[]{:S(2)}, u32[]{:S(2)}) collective-permute-start(bf16[64,1024]{1,0:T(8,128)(2,1)S(1)} %get-tuple-element.20), channel_id=1, source_target_pairs={{1,0},{2,1},{3,2},{4,3},{5,4},{6,5},{7,6},{8,7},{9,8},{10,9},{11,1... | collective-permute-start | bytes 393224 | tf_op jit(solution)/shard_map/ppermute | solution.py:382

commit v9 on v8

--- a/solution.py
+++ b/solution.py
@@ -105,7 +105,8 @@
         send.wait()
 
 
-def edge_kernel(own_ref, north_ref, south_ref, head_ref, tail_ref):
+def edge_kernel(own_ref, north_ref, south_ref, near_ref, far_ref):
+    even = lax.rem(lax.axis_index("lon"), 2) == 0
     lower = lax.broadcasted_iota(jnp.int32, (8, D), 0) < HALF
     pairs = [(north_ref, 0), (north_ref, 2)]
     pairs += [(own_ref, i) for i in range(0, RH, 2)]
@@ -117,8 +118,9 @@
             last = [ref[i + k, 24:32].astype(jnp.float32) for k in range(2)]
             heads.append(jnp.where(lower, first[0], pltpu.roll(first[1], HALF, 0)))
             tails.append(jnp.where(lower, pltpu.roll(last[0], HALF, 0), last[1]))
-        head_ref[n * 8 : n * 8 + 16] = jnp.concatenate(heads, 0).astype(jnp.bfloat16)
-        tail_ref[n * 8 : n * 8 + 16] = jnp.concatenate(tails, 0).astype(jnp.bfloat16)
+        head, tail = jnp.concatenate(heads, 0), jnp.concatenate(tails, 0)
+        near_ref[n * 8 : n * 8 + 16] = jnp.where(even, tail, head).astype(jnp.bfloat16)
+        far_ref[n * 8 : n * 8 + 16] = jnp.where(even, head, tail).astype(jnp.bfloat16)
 
 
 def bias_kernel(table_ref, index_ref, gain_in, bias, gain_ref):
@@ -269,7 +271,7 @@
 
 
 def outer_kernel(
-    left_ref, right_ref, rims_ref, inner_ref, gain_ref, bias, hot_ref, w_ref,
+    near_ref, far_ref, rims_ref, inner_ref, gain_ref, bias, hot_ref, w_ref,
     out_ref, cap_ref, undo_ref, xs, xq, kv, qs, scores, weights, wout, edges, full,
 ):
     gain = gain_ref[...]
@@ -279,9 +281,12 @@
     undo = jnp.transpose(hot_ref[...].astype(jnp.float32))
     undo_ref[...] = jnp.where(polar, undo, 0.0).astype(jnp.bfloat16)
 
-    for side, ref in enumerate((left_ref, right_ref)):
-        for i in range(0, 64, 32):
-            edges[side, i : i + 32] = norm_rows(ref[i : i + 32].astype(jnp.float32), gain)
+    even = lax.rem(lax.axis_index("lon"), 2) == 0
+    for i in range(0, 64, 32):
+        near = norm_rows(near_ref[i : i + 32].astype(jnp.float32), gain)
+        far = norm_rows(far_ref[i : i + 32].astype(jnp.float32), gain)
+        edges[0, i : i + 32] = jnp.where(even, far, near)
+        edges[1, i : i + 32] = jnp.where(even, near, far)
     lower = lax.broadcasted_iota(jnp.int32, (8, D), 0) < HALF
     for r in range(0, RH + WIN, 2):
         lo = edges[0, r * 4 : r * 4 + 8]
@@ -364,8 +369,8 @@
 
     down = [(i, i + 1) for i in range(lat_count - 1)]
     up = [(i + 1, i) for i in range(lat_count - 1)]
-    east = [(i, (i + 1) % lon_count) for i in range(lon_count)]
-    west = [((i + 1) % lon_count, i) for i in range(lon_count)]
+    pairs = [(i, i + 1 - 2 * (i % 2)) for i in range(lon_count)]
+    across = [(i, (i - 1 + 2 * (i % 2)) % lon_count) for i in range(lon_count)]
     tied, _ = lax.optimization_barrier((tokens, packed))
     north = lax.ppermute(tied[RH - HALF :], "lat", down)
     south = lax.ppermute(tied[:HALF], "lat", up)
@@ -374,12 +379,12 @@
         SOME_VMEM, 1 << 18, 1 << 18,
     )(bias_table, bias_index, gain)
     side = sds(((RH + WIN) * HALF, D), bf16)
-    head, tail = call(
+    near, far = call(
         edge_kernel, (side, side), [vspec()] * 3, (vspec(), vspec()), [],
         SOME_VMEM, 4 << 30, 3 << 19,
     )(tokens, north, south)
-    left = lax.ppermute(tail, "lon", east)
-    right = lax.ppermute(head, "lon", west)
+    far = lax.ppermute(far, "lon", across)
+    near = lax.ppermute(near, "lon", pairs)
 
     cap_result = call(
         cap_kernel, sds((SLOT_TOKENS, HW), bf16),
@@ -412,7 +417,7 @@
         scratch(2 * OUTER)
         + [VMEM((2 * OUTER, QROWS, HW), f32), VMEM((2, 64, D), f32), VMEM((RH * RW, HW), f32)],
         SOME_VMEM, 900 << 20, 5 << 20, 1 << 17,
-    )(left, right, rims, inner, gain, bias, hot, w_qkv)
+    )(near, far, rims, inner, gain, bias, hot, w_qkv)
     mixed = call(
         join_kernel, sds((RH * RW, HW), bf16),
         [vspec()] * 3 + [aspec()], aspec(),

time: 55.3 us -> 55.2 us (level)
  the two profiles are of different devices: /device:TPU:1 before, /device:TPU:2 now
where the time goes in v9:
time: 55.2 us; the launch traced here: 54.8 us
  starting transfers between devices  29.6 us (54%)
  Pallas kernels  11.1 us (20%)
  waiting for transfers between devices  10.9 us (20%)
  local copies, waits for them, and re-layouts  3.05 us (6%)
    all_to_all x2, starting transfers between devices, exchange(): return lax.all_to_all(block, 'lon', split_axis=0, concat_axis=0, tiled=True)  15.6 us
    all_to_all x2, waiting for transfers between devices, exchange(): return lax.all_to_all(block, 'lon', split_axis=0, concat_axis=0, tiled=True)  10.1 us
    ppermute x1, starting transfers between devices, layer(): far = lax.ppermute(far, 'lon', across)  5.85 us
    ppermute x1, starting transfers between devices, layer(): north = lax.ppermute(tied[RH - HALF:], 'lat', down)  3.4 us
    pallas_call x1, Pallas kernels, layer(): call(cap_kernel, sds((SLOT_TOKENS, HW), bf16), [vspec()] * 3, vspec(), [V...  2.77 us
    pallas_call x1, Pallas kernels, layer(): call(inner_kernel, (sds((2 * INNER, QROWS, HW), f32), sds((2, (RH + WIN)...  2.47 us
    ppermute x1, starting transfers between devices, layer(): south = lax.ppermute(tied[:HALF], 'lat', up)  2.44 us
    pallas_call x1, Pallas kernels, layer(): call(outer_kernel, (sds((RH * RW, HW), bf16), sds((CAP_TOKENS, HW), f32),...  2.35 us
  transfers between devices with their start and end apart: 6, of which 2 were waited for; matrix products, arithmetic and copies ran while one was open for 2% of the time, Pallas kernels for 15%

profile of v9, /device:TPU:2, one launch (start us, length us, event | category | flops | bytes accessed | tf_op | source)
XLA Modules:
  0.0 54.8 jit_solution(10590249701313797911)
XLA Ops:
  0.0 0.0 copy-start.4
  0.0 0.0 copy-start.5
  0.0 2.1 %shard_map.64 = (bf16[256,1024]{1,0:T(8,128)(2,1)}, bf16[256,128]{1,0:T(8,128)(2,1)}) custom-call(s32[2,4,1,8]{3,2,1,0:T(1,128)} %bitcast.11, bf16[8,32,1024]{2,1,0:T(8,128)(2,1)} %own_ref.3), custom_call_target="tpu_custom_call" | custom-call | flops 4294967296 | bytes 1048576 | tf_op jit(solution)/shard_map/pallas_call | solution.py:354
  2.1 11.7 %all-to-all-start = ((bf16[32,8,1024]{2,1,0:T(8,128)(2,1)}), bf16[32,8,1024]{2,1,0:T(8,128)(2,1)S(1)}, u32[]{:S(2)}, u32[]{:S(2)}) async-start(bf16[32,8,1024]{2,1,0:T(8,128)(2,1)} %bitcast.10), calls=%async_computation | async-start | bytes 1048576 | tf_op jit(solution)/shard_map/all_to_all | solution.py:344
  13.8 0.0 copy-start.2
  13.8 1.1 %fusion = (bf16[4,32,1024]{2,1,0:T(8,128)(2,1)S(1)}, bf16[4,32,1024]{2,1,0:T(8,128)(2,1)S(1)}) fusion(bf16[8,32,1024]{2,1,0:T(8,128)(2,1)} %own_ref.3), kind=kLoop, calls=%fused_computation | loop fusion | bytes 1048576 | tf_op jit(solution)/shard_map/slice | solution.py:376
  15.0 2.4 %collective-permute-start.1 = (bf16[4,32,1024]{2,1,0:T(8,128)(2,1)S(1)}, bf16[4,32,1024]{2,1,0:T(8,128)(2,1)S(1)}, u32[]{:S(2)}, u32[]{:S(2)}) collective-permute-start(bf16[4,32,1024]{2,1,0:T(8,128)(2,1)S(1)} %get-tuple-element.29), channel_id=1, source_target_pairs={{32,0},{64,32},{96,64},{128,96},{160,128},{192,160},{224,192},{256... | collective-permute-start | bytes 786440 | tf_op jit(solution)/shard_map/ppermute | solution.py:376
  17.4 3.4 %collective-permute-start = (bf16[4,32,1024]{2,1,0:T(8,128)(2,1)S(1)}, bf16[4,32,1024]{2,1,0:T(8,128)(2,1)S(1)}, u32[]{:S(2)}, u32[]{:S(2)}) collective-permute-start(bf16[4,32,1024]{2,1,0:T(8,128)(2,1)S(1)} %get-tuple-element.30), channel_id=1, source_target_pairs={{0,32},{32,64},{64,96},{96,128},{128,160},{160,192},{192,224},{224... | collective-permute-start | bytes 786440 | tf_op jit(solution)/shard_map/ppermute | solution.py:375
  20.8 0.0 copy-done.4
  20.8 0.0 copy-done.5
  20.8 0.0 copy-done.6
  20.8 0.5 shard_map.66
  21.3 10.1 %all-to-all-done = bf16[32,8,1024]{2,1,0:T(8,128)(2,1)S(1)} async-done(((bf16[32,8,1024]{2,1,0:T(8,128)(2,1)}), bf16[32,8,1024]{2,1,0:T(8,128)(2,1)S(1)}, u32[]{:S(2)}, u32[]{:S(2)}) %all-to-all-start) | async-done | bytes 524320 | tf_op jit(solution)/shard_map/all_to_all | solution.py:344
  31.5 1.9 %copy-done = bf16[1024,1536]{1,0:T(8,128)(2,1)S(1)} copy-done((bf16[1024,1536]{1,0:T(8,128)(2,1)S(1)}, bf16[1024,1536]{1,0:T(8,128)(2,1)}, u32[]{:S(2)}) %copy-start) | copy-done | bytes 3145752
  33.4 2.8 %shard_map.69 = bf16[256,512]{1,0:T(8,128)(2,1)} custom-call(bf16[256,1024]{1,0:T(8,128)(2,1)S(1)} %bitcast.8, f32[1,1024]{1,0:T(1,128)S(1)} %get-tuple-element.21.gain_ref, bf16[1024,1536]{1,0:T(8,128)(2,1)S(1)} %copy-done), custom_call_target="tpu_custom_call" | custom-call | flops 1153433600 | bytes 4194304 | tf_op jit(solution)/shard_map/pallas_call | solution.py:389
  36.1 3.9 %all-to-all-start.1 = ((bf16[32,8,512]{2,1,0:T(8,128)(2,1)}), bf16[32,8,512]{2,1,0:T(8,128)(2,1)S(1)}, u32[]{:S(2)}, u32[]{:S(2)}) async-start(bf16[32,8,512]{2,1,0:T(8,128)(2,1)} %bitcast.4), calls=%async_computation.1 | async-start | bytes 524288 | tf_op jit(solution)/shard_map/all_to_all | solution.py:344
  40.0 0.0 copy-start.1
  40.0 0.0 collective-permute-done.1.south_ref
  40.0 0.0 collective-permute-done.north_ref
  40.0 0.0 copy-done.2
  40.0 0.1 shard_map.65
  40.1 0.0 copy-start.3
  40.2 2.3 %collective-permute-start.2 = (bf16[64,1024]{1,0:T(8,128)(2,1)S(1)}, bf16[64,1024]{1,0:T(8,128)(2,1)S(1)}, u32[]{:S(2)}, u32[]{:S(2)}) collective-permute-start(bf16[64,1024]{1,0:T(8,128)(2,1)S(1)} %get-tuple-element.19), channel_id=1, source_target_pairs={{0,1},{1,0},{2,3},{3,2},{4,5},{5,4},{6,7},{7,6},{8,9},{9,8},{10,11... | collective-permute-start | bytes 393224 | tf_op jit(solution)/shard_map/ppermute | solution.py:387
  42.5 5.8 %collective-permute-start.3 = (bf16[64,1024]{1,0:T(8,128)(2,1)S(1)}, bf16[64,1024]{1,0:T(8,128)(2,1)S(1)}, u32[]{:S(2)}, u32[]{:S(2)}) collective-permute-start(bf16[64,1024]{1,0:T(8,128)(2,1)S(1)} %get-tuple-element.20), channel_id=1, source_target_pairs={{0,31},{1,2},{2,1},{3,4},{4,3},{5,6},{6,5},{7,8},{8,7},{9,10},{10,... | collective-permute-start | bytes 393224 | tf_op jit(solution)/shard_map/ppermute | solution.py:386
  48.4 0.0 copy-done.1
  48.4 2.5 %shard_map.67 = (f32[6,32,512]{2,1,0:T(8,128)S(1)}, bf16[2,128,1024]{2,1,0:T(8,128)(2,1)S(1)}) custom-call(bf16[8,32,1024]{2,1,0:T(8,128)(2,1)S(1)} %copy-done.2, bf16[4,32,1024]{2,1,0:T(8,128)(2,1)S(1)} %collective-permute-done.north_ref, bf16[4,32,1024]{2,1,0:T(8,128)(2,1)S(1)} %collective-permute-done.1.south_ref, ...), custom_call_target="tpu_custom_call" | custom-call | flops 1468006400 | bytes 5242880 | tf_op jit(solution)/shard_map/pallas_call | solution.py:407
  50.8 0.0 collective-permute-done.2.near_ref
  50.9 0.7 %collective-permute-done.3.far_ref = bf16[64,1024]{1,0:T(8,128)(2,1)S(1)} collective-permute-done((bf16[64,1024]{1,0:T(8,128)(2,1)S(1)}, bf16[64,1024]{1,0:T(8,128)(2,1)S(1)}, u32[]{:S(2)}, u32[]{:S(2)}) %collective-permute-start.3) | collective-permute-done | bytes 131104 | tf_op jit(solution)/shard_map/ppermute | solution.py:386
  51.6 0.0 copy-done.3
  51.6 2.3 %shard_map.68 = (bf16[256,512]{1,0:T(8,128)(2,1)}, f32[128,512]{1,0:T(8,128)S(1)}, bf16[128,256]{1,0:T(8,128)(2,1)S(1)}) custom-call(bf16[64,1024]{1,0:T(8,128)(2,1)S(1)} %collective-permute-done.2.near_ref, bf16[64,1024]{1,0:T(8,128)(2,1)S(1)} %collective-permute-done.3.far_ref, bf16[2,128,1024]{2,1,0:T(8,128)(2,1)S(1)} %get-tuple-element.23.rims_ref, ...), custom_call_target="tpu_custom_call" | custom-call | flops 943718400 | bytes 5242880 | tf_op jit(solution)/shard_map/pallas_call | solution.py:413
  53.9 0.0 all-to-all-done.1
  53.9 0.9 %shard_map.70 = bf16[256,512]{1,0:T(8,128)(2,1)} custom-call(f32[128,512]{1,0:T(8,128)S(1)} %get-tuple-element.26.win_ref, bf16[256,512]{1,0:T(8,128)(2,1)S(1)} %bitcast.7, bf16[128,256]{1,0:T(8,128)(2,1)S(1)} %get-tuple-element.27.undo_ref, bf16[256,512]{1,0:T(8,128)(2,1)} %get-tuple-element.28.out_in), custom_call_target="tpu_custom_call", output_to_operand_aliasing={{}: (3, {})} | custom-call | flops 33554432 | bytes 524288 | tf_op jit(solution)/shard_map/pallas_call | solution.py:421
  (2 shorter events, 0.0 us)
Async XLA Ops:
  0.0 20.8 %copy-start.4 = (s32[64,64]{1,0:T(8,128)S(1)}, s32[64,64]{1,0:T(8,128)}, u32[]{:S(2)}) copy-start(s32[64,64]{1,0:T(8,128)} %index_ref.1) | copy-start | bytes 49156
  0.0 20.8 %copy-start.5 = (f32[8,225]{1,0:T(8,128)S(1)}, f32[8,225]{1,0:T(8,128)}, u32[]{:S(2)}) copy-start(f32[8,225]{1,0:T(8,128)} %table_ref.1) | copy-start | bytes 21604
  0.0 20.8 %copy-start.6 = (f32[1024]{0:T(1024)S(1)}, f32[1024]{0:T(1024)}, u32[]{:S(2)}) copy-start(f32[1024]{0:T(1024)} %param.7) | copy-start | bytes 12292
  2.1 29.4 %all-to-all-start = ((bf16[32,8,1024]{2,1,0:T(8,128)(2,1)}), bf16[32,8,1024]{2,1,0:T(8,128)(2,1)S(1)}, u32[]{:S(2)}, u32[]{:S(2)}) async-start(bf16[32,8,1024]{2,1,0:T(8,128)(2,1)} %bitcast.10), calls=%async_computation | async-start | bytes 1048576 | tf_op jit(solution)/shard_map/all_to_all | solution.py:344
  13.8 26.2 %copy-start.2 = (bf16[8,32,1024]{2,1,0:T(8,128)(2,1)S(1)}, bf16[8,32,1024]{2,1,0:T(8,128)(2,1)}, u32[]{:S(2)}) copy-start(bf16[8,32,1024]{2,1,0:T(8,128)(2,1)} %own_ref.3) | copy-start | bytes 1572868
  15.0 25.1 %collective-permute-start.1 = (bf16[4,32,1024]{2,1,0:T(8,128)(2,1)S(1)}, bf16[4,32,1024]{2,1,0:T(8,128)(2,1)S(1)}, u32[]{:S(2)}, u32[]{:S(2)}) collective-permute-start(bf16[4,32,1024]{2,1,0:T(8,128)(2,1)S(1)} %get-tuple-element.29), channel_id=1, source_target_pairs={{32,0},{64,32},{96,64},{128,96},{160,128},{192,160},{224,192},{256... | collective-permute-start | bytes 786440 | tf_op jit(solution)/shard_map/ppermute | solution.py:376
  17.4 22.6 %collective-permute-start = (bf16[4,32,1024]{2,1,0:T(8,128)(2,1)S(1)}, bf16[4,32,1024]{2,1,0:T(8,128)(2,1)S(1)}, u32[]{:S(2)}, u32[]{:S(2)}) collective-permute-start(bf16[4,32,1024]{2,1,0:T(8,128)(2,1)S(1)} %get-tuple-element.30), channel_id=1, source_target_pairs={{0,32},{32,64},{64,96},{96,128},{128,160},{160,192},{192,224},{224... | collective-permute-start | bytes 786440 | tf_op jit(solution)/shard_map/ppermute | solution.py:375
  31.5 1.9 %copy-start = (bf16[1024,1536]{1,0:T(8,128)(2,1)S(1)}, bf16[1024,1536]{1,0:T(8,128)(2,1)}, u32[]{:S(2)}) copy-start(bf16[1024,1536]{1,0:T(8,128)(2,1)} %w_ref.5) | copy-start | bytes 9437188
  36.1 17.8 %all-to-all-start.1 = ((bf16[32,8,512]{2,1,0:T(8,128)(2,1)}), bf16[32,8,512]{2,1,0:T(8,128)(2,1)S(1)}, u32[]{:S(2)}, u32[]{:S(2)}) async-start(bf16[32,8,512]{2,1,0:T(8,128)(2,1)} %bitcast.4), calls=%async_computation.1 | async-start | bytes 524288 | tf_op jit(solution)/shard_map/all_to_all | solution.py:344
  40.0 8.4 %copy-start.1 = (bf16[1024,1536]{1,0:T(8,128)(2,1)S(1)}, bf16[1024,1536]{1,0:T(8,128)(2,1)}, u32[]{:S(2)}) copy-start(bf16[1024,1536]{1,0:T(8,128)(2,1)} %w_ref.5) | copy-start | bytes 9437188
  40.1 11.4 %copy-start.3 = (bf16[256,128]{1,0:T(8,128)(2,1)S(1)}, bf16[256,128]{1,0:T(8,128)(2,1)}, u32[]{:S(2)}) copy-start(bf16[256,128]{1,0:T(8,128)(2,1)} %get-tuple-element.25.hot_ref) | copy-start | bytes 196612
  40.2 10.7 %collective-permute-start.2 = (bf16[64,1024]{1,0:T(8,128)(2,1)S(1)}, bf16[64,1024]{1,0:T(8,128)(2,1)S(1)}, u32[]{:S(2)}, u32[]{:S(2)}) collective-permute-start(bf16[64,1024]{1,0:T(8,128)(2,1)S(1)} %get-tuple-element.19), channel_id=1, source_target_pairs={{0,1},{1,0},{2,3},{3,2},{4,5},{5,4},{6,7},{7,6},{8,9},{9,8},{10,11... | collective-permute-start | bytes 393224 | tf_op jit(solution)/shard_map/ppermute | solution.py:387
  42.5 9.1 %collective-permute-start.3 = (bf16[64,1024]{1,0:T(8,128)(2,1)S(1)}, bf16[64,1024]{1,0:T(8,128)(2,1)S(1)}, u32[]{:S(2)}, u32[]{:S(2)}) collective-permute-start(bf16[64,1024]{1,0:T(8,128)(2,1)S(1)} %get-tuple-element.20), channel_id=1, source_target_pairs={{0,31},{1,2},{2,1},{3,4},{4,3},{5,6},{6,5},{7,8},{8,7},{9,10},{10,... | collective-permute-start | bytes 393224 | tf_op jit(solution)/shard_map/ppermute | solution.py:386

commit v10 on v9

--- a/solution.py
+++ b/solution.py
@@ -250,9 +250,15 @@
 
 
 def inner_kernel(
-    own_ref, north_ref, south_ref, gain_ref, bias, w_ref, wout, rims_ref, xs, xq, kv, qs, scores, weights,
+    own_ref, north_ref, south_ref, gain_ref, bias, hot_ref, w_ref, wout, rims_ref, undo_ref, xs, xq, kv, qs, scores, weights,
 ):
     gain = gain_ref[...]
+    lat = lax.axis_index("lat")
+
+    polar = (lat == 0) | (lat == lax.axis_size("lat") - 1)
+    undo = jnp.transpose(hot_ref[...].astype(jnp.float32))
+    undo_ref[...] = jnp.where(polar, undo, 0.0).astype(jnp.bfloat16)
+
     lower = lax.broadcasted_iota(jnp.int32, (8, D), 0) < HALF
     rows = [(north_ref, i) for i in range(HALF)] + [(own_ref, i) for i in range(RH)]
     rows += [(south_ref, i) for i in range(HALF)]
@@ -271,16 +277,11 @@
 
 
 def outer_kernel(
-    near_ref, far_ref, rims_ref, inner_ref, gain_ref, bias, hot_ref, w_ref,
-    out_ref, cap_ref, undo_ref, xs, xq, kv, qs, scores, weights, wout, edges, full,
+    near_ref, far_ref, rims_ref, inner_ref, gain_ref, bias, w_ref,
+    out_ref, cap_ref, xs, xq, kv, qs, scores, weights, wout, edges, full,
 ):
     gain = gain_ref[...]
     lat = lax.axis_index("lat")
-
-    polar = (lat == 0) | (lat == lax.axis_size("lat") - 1)
-    undo = jnp.transpose(hot_ref[...].astype(jnp.float32))
-    undo_ref[...] = jnp.where(polar, undo, 0.0).astype(jnp.bfloat16)
-
     even = lax.rem(lax.axis_index("lon"), 2) == 0
     for i in range(0, 64, 32):
         near = norm_rows(near_ref[i : i + 32].astype(jnp.float32), gain)
@@ -404,20 +405,23 @@
             VMEM((count * 128, 128), bf16),
         ]
 
-    inner, rims = call(
+    inner, rims, undo = call(
         inner_kernel,
-        (sds((2 * INNER, QROWS, HW), f32), sds((2, (RH + WIN) * 8, D), bf16)),
-        [vspec()] * 6, (vspec(), vspec()), scratch(2 * INNER),
+        (
+            sds((2 * INNER, QROWS, HW), f32), sds((2, (RH + WIN) * 8, D), bf16),
+            sds((CAP_TOKENS, SLOT_TOKENS), bf16),
+        ),
+        [vspec()] * 7, (vspec(),) * 3, scratch(2 * INNER),
         SOME_VMEM, 1400 << 20, 5 << 20, 1 << 17,
-    )(tokens, north, south, gain, bias, w_qkv)
-    win_out, cap_rows, undo = call(
+    )(tokens, north, south, gain, bias, hot, w_qkv)
+    win_out, cap_rows = call(
         outer_kernel,
-        (sds((RH * RW, HW), bf16), sds((CAP_TOKENS, HW), f32), sds((CAP_TOKENS, SLOT_TOKENS), bf16)),
-        [vspec()] * 8, (vspec(),) * 3,
+        (sds((RH * RW, HW), bf16), sds((CAP_TOKENS, HW), f32)),
+        [vspec()] * 7, (vspec(),) * 2,
         scratch(2 * OUTER)
         + [VMEM((2 * OUTER, QROWS, HW), f32), VMEM((2, 64, D), f32), VMEM((RH * RW, HW), f32)],
         SOME_VMEM, 900 << 20, 5 << 20, 1 << 17,
-    )(near, far, rims, inner, gain, bias, hot, w_qkv)
+    )(near, far, rims, inner, gain, bias, w_qkv)
     mixed = call(
         join_kernel, sds((RH * RW, HW), bf16),
         [vspec()] * 3 + [aspec()], aspec(),

time: 55.2 us -> 55.2 us (level)
  no operation moved by 1% of the time
where the time goes in v10:
time: 55.2 us; the launch traced here: 54.8 us
  starting transfers between devices  29.6 us (54%)
  Pallas kernels  11.1 us (20%)
  waiting for transfers between devices  10.8 us (20%)
  local copies, waits for them, and re-layouts  3.05 us (6%)
    all_to_all x2, starting transfers between devices, exchange(): return lax.all_to_all(block, 'lon', split_axis=0, concat_axis=0, tiled=True)  15.6 us
    all_to_all x2, waiting for transfers between devices, exchange(): return lax.all_to_all(block, 'lon', split_axis=0, concat_axis=0, tiled=True)  10.1 us
    ppermute x1, starting transfers between devices, layer(): far = lax.ppermute(far, 'lon', across)  5.85 us
    ppermute x1, starting transfers between devices, layer(): north = lax.ppermute(tied[RH - HALF:], 'lat', down)  3.4 us
    pallas_call x1, Pallas kernels, layer(): call(cap_kernel, sds((SLOT_TOKENS, HW), bf16), [vspec()] * 3, vspec(), [V...  2.78 us
    pallas_call x1, Pallas kernels, layer(): call(inner_kernel, (sds((2 * INNER, QROWS, HW), f32), sds((2, (RH + WIN)...  2.52 us
    ppermute x1, starting transfers between devices, layer(): south = lax.ppermute(tied[:HALF], 'lat', up)  2.44 us
    pallas_call x1, Pallas kernels, layer(): call(outer_kernel, (sds((RH * RW, HW), bf16), sds((CAP_TOKENS, HW), f32))...  2.34 us
  transfers between devices with their start and end apart: 6, of which 2 were waited for; matrix products, arithmetic and copies ran while one was open for 2% of the time, Pallas kernels for 15%

profile of v10, /device:TPU:2, one launch (start us, length us, event | category | flops | bytes accessed | tf_op | source)
XLA Modules:
  0.0 54.8 jit_solution(11525762504328896668)
XLA Ops:
  0.0 0.0 copy-start.3
  0.0 0.0 copy-start.4
  0.0 2.1 %shard_map.64 = (bf16[256,1024]{1,0:T(8,128)(2,1)}, bf16[256,128]{1,0:T(8,128)(2,1)}) custom-call(s32[2,4,1,8]{3,2,1,0:T(1,128)} %bitcast.11, bf16[8,32,1024]{2,1,0:T(8,128)(2,1)} %own_ref.3), custom_call_target="tpu_custom_call" | custom-call | flops 4294967296 | bytes 1048576 | tf_op jit(solution)/shard_map/pallas_call | solution.py:355
  2.1 11.7 %all-to-all-start = ((bf16[32,8,1024]{2,1,0:T(8,128)(2,1)}), bf16[32,8,1024]{2,1,0:T(8,128)(2,1)S(1)}, u32[]{:S(2)}, u32[]{:S(2)}) async-start(bf16[32,8,1024]{2,1,0:T(8,128)(2,1)} %bitcast.10), calls=%async_computation | async-start | bytes 1048576 | tf_op jit(solution)/shard_map/all_to_all | solution.py:345
  13.8 0.0 copy-start.2
  13.8 1.1 %fusion = (bf16[4,32,1024]{2,1,0:T(8,128)(2,1)S(1)}, bf16[4,32,1024]{2,1,0:T(8,128)(2,1)S(1)}) fusion(bf16[8,32,1024]{2,1,0:T(8,128)(2,1)} %own_ref.3), kind=kLoop, calls=%fused_computation | loop fusion | bytes 1048576 | tf_op jit(solution)/shard_map/slice | solution.py:377
  15.0 2.4 %collective-permute-start.1 = (bf16[4,32,1024]{2,1,0:T(8,128)(2,1)S(1)}, bf16[4,32,1024]{2,1,0:T(8,128)(2,1)S(1)}, u32[]{:S(2)}, u32[]{:S(2)}) collective-permute-start(bf16[4,32,1024]{2,1,0:T(8,128)(2,1)S(1)} %get-tuple-element.29), channel_id=1, source_target_pairs={{32,0},{64,32},{96,64},{128,96},{160,128},{192,160},{224,192},{256... | collective-permute-start | bytes 786440 | tf_op jit(solution)/shard_map/ppermute | solution.py:377
  17.4 3.4 %collective-permute-start = (bf16[4,32,1024]{2,1,0:T(8,128)(2,1)S(1)}, bf16[4,32,1024]{2,1,0:T(8,128)(2,1)S(1)}, u32[]{:S(2)}, u32[]{:S(2)}) collective-permute-start(bf16[4,32,1024]{2,1,0:T(8,128)(2,1)S(1)} %get-tuple-element.30), channel_id=1, source_target_pairs={{0,32},{32,64},{64,96},{96,128},{128,160},{160,192},{192,224},{224... | collective-permute-start | bytes 786440 | tf_op jit(solution)/shard_map/ppermute | solution.py:376
  20.8 0.0 copy-done.3
  20.8 0.0 copy-done.4
  20.8 0.0 copy-done.5
  20.8 0.5 shard_map.66
  21.3 10.1 %all-to-all-done = bf16[32,8,1024]{2,1,0:T(8,128)(2,1)S(1)} async-done(((bf16[32,8,1024]{2,1,0:T(8,128)(2,1)}), bf16[32,8,1024]{2,1,0:T(8,128)(2,1)S(1)}, u32[]{:S(2)}, u32[]{:S(2)}) %all-to-all-start) | async-done | bytes 524320 | tf_op jit(solution)/shard_map/all_to_all | solution.py:345
  31.5 1.9 %copy-done = bf16[1024,1536]{1,0:T(8,128)(2,1)S(1)} copy-done((bf16[1024,1536]{1,0:T(8,128)(2,1)S(1)}, bf16[1024,1536]{1,0:T(8,128)(2,1)}, u32[]{:S(2)}) %copy-start) | copy-done | bytes 3145752
  33.4 2.8 %shard_map.69 = bf16[256,512]{1,0:T(8,128)(2,1)} custom-call(bf16[256,1024]{1,0:T(8,128)(2,1)S(1)} %bitcast.8, f32[1,1024]{1,0:T(1,128)S(1)} %get-tuple-element.21.gain_ref, bf16[1024,1536]{1,0:T(8,128)(2,1)S(1)} %copy-done), custom_call_target="tpu_custom_call" | custom-call | flops 1153433600 | bytes 4194304 | tf_op jit(solution)/shard_map/pallas_call | solution.py:390
  36.1 3.9 %all-to-all-start.1 = ((bf16[32,8,512]{2,1,0:T(8,128)(2,1)}), bf16[32,8,512]{2,1,0:T(8,128)(2,1)S(1)}, u32[]{:S(2)}, u32[]{:S(2)}) async-start(bf16[32,8,512]{2,1,0:T(8,128)(2,1)} %bitcast.4), calls=%async_computation.1 | async-start | bytes 524288 | tf_op jit(solution)/shard_map/all_to_all | solution.py:345
  40.0 0.0 copy-start.1
  40.0 0.0 copy-start.6
  40.0 0.0 collective-permute-done.1.south_ref
  40.0 0.0 collective-permute-done.north_ref
  40.0 0.0 copy-done.2
  40.1 0.1 shard_map.65
  40.2 2.3 %collective-permute-start.2 = (bf16[64,1024]{1,0:T(8,128)(2,1)S(1)}, bf16[64,1024]{1,0:T(8,128)(2,1)S(1)}, u32[]{:S(2)}, u32[]{:S(2)}) collective-permute-start(bf16[64,1024]{1,0:T(8,128)(2,1)S(1)} %get-tuple-element.19), channel_id=1, source_target_pairs={{0,1},{1,0},{2,3},{3,2},{4,5},{5,4},{6,7},{7,6},{8,9},{9,8},{10,11... | collective-permute-start | bytes 393224 | tf_op jit(solution)/shard_map/ppermute | solution.py:388
  42.5 5.8 %collective-permute-start.3 = (bf16[64,1024]{1,0:T(8,128)(2,1)S(1)}, bf16[64,1024]{1,0:T(8,128)(2,1)S(1)}, u32[]{:S(2)}, u32[]{:S(2)}) collective-permute-start(bf16[64,1024]{1,0:T(8,128)(2,1)S(1)} %get-tuple-element.20), channel_id=1, source_target_pairs={{0,31},{1,2},{2,1},{3,4},{4,3},{5,6},{6,5},{7,8},{8,7},{9,10},{10,... | collective-permute-start | bytes 393224 | tf_op jit(solution)/shard_map/ppermute | solution.py:387
  48.4 0.0 copy-done.1
  48.4 0.0 copy-done.6
  48.4 2.5 %shard_map.67 = (f32[6,32,512]{2,1,0:T(8,128)S(1)}, bf16[2,128,1024]{2,1,0:T(8,128)(2,1)S(1)}, bf16[128,256]{1,0:T(8,128)(2,1)S(1)}) custom-call(bf16[8,32,1024]{2,1,0:T(8,128)(2,1)S(1)} %copy-done.2, bf16[4,32,1024]{2,1,0:T(8,128)(2,1)S(1)} %collective-permute-done.north_ref, bf16[4,32,1024]{2,1,0:T(8,128)(2,1)S(1)} %collective-permute-done.1.south_ref, ...), custom_call_target="tpu_custom_call" | custom-call | flops 1468006400 | bytes 5242880 | tf_op jit(solution)/shard_map/pallas_call | solution.py:408
  50.9 0.0 collective-permute-done.2.near_ref
  50.9 0.7 %collective-permute-done.3.far_ref = bf16[64,1024]{1,0:T(8,128)(2,1)S(1)} collective-permute-done((bf16[64,1024]{1,0:T(8,128)(2,1)S(1)}, bf16[64,1024]{1,0:T(8,128)(2,1)S(1)}, u32[]{:S(2)}, u32[]{:S(2)}) %collective-permute-start.3) | collective-permute-done | bytes 131104 | tf_op jit(solution)/shard_map/ppermute | solution.py:387
  51.6 2.3 %shard_map.68 = (bf16[256,512]{1,0:T(8,128)(2,1)}, f32[128,512]{1,0:T(8,128)S(1)}) custom-call(bf16[64,1024]{1,0:T(8,128)(2,1)S(1)} %collective-permute-done.2.near_ref, bf16[64,1024]{1,0:T(8,128)(2,1)S(1)} %collective-permute-done.3.far_ref, bf16[2,128,1024]{2,1,0:T(8,128)(2,1)S(1)} %get-tuple-element.24.rims_ref, ...), custom_call_target="tpu_custom_call" | custom-call | flops 943718400 | bytes 5242880 | tf_op jit(solution)/shard_map/pallas_call | solution.py:417
  53.9 0.0 all-to-all-done.1
  53.9 0.9 %shard_map.70 = bf16[256,512]{1,0:T(8,128)(2,1)} custom-call(f32[128,512]{1,0:T(8,128)S(1)} %get-tuple-element.26.win_ref, bf16[256,512]{1,0:T(8,128)(2,1)S(1)} %bitcast.7, bf16[128,256]{1,0:T(8,128)(2,1)S(1)} %get-tuple-element.27.undo_ref, bf16[256,512]{1,0:T(8,128)(2,1)} %get-tuple-element.28.out_in), custom_call_target="tpu_custom_call", output_to_operand_aliasing={{}: (3, {})} | custom-call | flops 33554432 | bytes 524288 | tf_op jit(solution)/shard_map/pallas_call | solution.py:425
  (2 shorter events, 0.0 us)
Async XLA Ops:
  0.0 20.8 %copy-start.3 = (s32[64,64]{1,0:T(8,128)S(1)}, s32[64,64]{1,0:T(8,128)}, u32[]{:S(2)}) copy-start(s32[64,64]{1,0:T(8,128)} %index_ref.1) | copy-start | bytes 49156
  0.0 20.8 %copy-start.4 = (f32[8,225]{1,0:T(8,128)S(1)}, f32[8,225]{1,0:T(8,128)}, u32[]{:S(2)}) copy-start(f32[8,225]{1,0:T(8,128)} %table_ref.1) | copy-start | bytes 21604
  0.0 20.8 %copy-start.5 = (f32[1024]{0:T(1024)S(1)}, f32[1024]{0:T(1024)}, u32[]{:S(2)}) copy-start(f32[1024]{0:T(1024)} %param.7) | copy-start | bytes 12292
  2.1 29.4 %all-to-all-start = ((bf16[32,8,1024]{2,1,0:T(8,128)(2,1)}), bf16[32,8,1024]{2,1,0:T(8,128)(2,1)S(1)}, u32[]{:S(2)}, u32[]{:S(2)}) async-start(bf16[32,8,1024]{2,1,0:T(8,128)(2,1)} %bitcast.10), calls=%async_computation | async-start | bytes 1048576 | tf_op jit(solution)/shard_map/all_to_all | solution.py:345
  13.8 26.2 %copy-start.2 = (bf16[8,32,1024]{2,1,0:T(8,128)(2,1)S(1)}, bf16[8,32,1024]{2,1,0:T(8,128)(2,1)}, u32[]{:S(2)}) copy-start(bf16[8,32,1024]{2,1,0:T(8,128)(2,1)} %own_ref.3) | copy-start | bytes 1572868
  15.0 25.1 %collective-permute-start.1 = (bf16[4,32,1024]{2,1,0:T(8,128)(2,1)S(1)}, bf16[4,32,1024]{2,1,0:T(8,128)(2,1)S(1)}, u32[]{:S(2)}, u32[]{:S(2)}) collective-permute-start(bf16[4,32,1024]{2,1,0:T(8,128)(2,1)S(1)} %get-tuple-element.29), channel_id=1, source_target_pairs={{32,0},{64,32},{96,64},{128,96},{160,128},{192,160},{224,192},{256... | collective-permute-start | bytes 786440 | tf_op jit(solution)/shard_map/ppermute | solution.py:377
  17.4 22.6 %collective-permute-start = (bf16[4,32,1024]{2,1,0:T(8,128)(2,1)S(1)}, bf16[4,32,1024]{2,1,0:T(8,128)(2,1)S(1)}, u32[]{:S(2)}, u32[]{:S(2)}) collective-permute-start(bf16[4,32,1024]{2,1,0:T(8,128)(2,1)S(1)} %get-tuple-element.30), channel_id=1, source_target_pairs={{0,32},{32,64},{64,96},{96,128},{128,160},{160,192},{192,224},{224... | collective-permute-start | bytes 786440 | tf_op jit(solution)/shard_map/ppermute | solution.py:376
  31.5 1.9 %copy-start = (bf16[1024,1536]{1,0:T(8,128)(2,1)S(1)}, bf16[1024,1536]{1,0:T(8,128)(2,1)}, u32[]{:S(2)}) copy-start(bf16[1024,1536]{1,0:T(8,128)(2,1)} %w_ref.5) | copy-start | bytes 9437188
  36.1 17.8 %all-to-all-start.1 = ((bf16[32,8,512]{2,1,0:T(8,128)(2,1)}), bf16[32,8,512]{2,1,0:T(8,128)(2,1)S(1)}, u32[]{:S(2)}, u32[]{:S(2)}) async-start(bf16[32,8,512]{2,1,0:T(8,128)(2,1)} %bitcast.4), calls=%async_computation.1 | async-start | bytes 524288 | tf_op jit(solution)/shard_map/all_to_all | solution.py:345
  40.0 8.4 %copy-start.1 = (bf16[1024,1536]{1,0:T(8,128)(2,1)S(1)}, bf16[1024,1536]{1,0:T(8,128)(2,1)}, u32[]{:S(2)}) copy-start(bf16[1024,1536]{1,0:T(8,128)(2,1)} %w_ref.5) | copy-start | bytes 9437188
  40.0 8.4 %copy-start.6 = (bf16[256,128]{1,0:T(8,128)(2,1)S(1)}, bf16[256,128]{1,0:T(8,128)(2,1)}, u32[]{:S(2)}) copy-start(bf16[256,128]{1,0:T(8,128)(2,1)} %get-tuple-element.23.hot_ref) | copy-start | bytes 196612
  40.2 10.7 %collective-permute-start.2 = (bf16[64,1024]{1,0:T(8,128)(2,1)S(1)}, bf16[64,1024]{1,0:T(8,128)(2,1)S(1)}, u32[]{:S(2)}, u32[]{:S(2)}) collective-permute-start(bf16[64,1024]{1,0:T(8,128)(2,1)S(1)} %get-tuple-element.19), channel_id=1, source_target_pairs={{0,1},{1,0},{2,3},{3,2},{4,5},{5,4},{6,7},{7,6},{8,9},{9,8},{10,11... | collective-permute-start | bytes 393224 | tf_op jit(solution)/shard_map/ppermute | solution.py:388
  42.5 9.1 %collective-permute-start.3 = (bf16[64,1024]{1,0:T(8,128)(2,1)S(1)}, bf16[64,1024]{1,0:T(8,128)(2,1)S(1)}, u32[]{:S(2)}, u32[]{:S(2)}) collective-permute-start(bf16[64,1024]{1,0:T(8,128)(2,1)S(1)} %get-tuple-element.20), channel_id=1, source_target_pairs={{0,31},{1,2},{2,1},{3,4},{4,3},{5,6},{6,5},{7,8},{8,7},{9,10},{10,... | collective-permute-start | bytes 393224 | tf_op jit(solution)/shard_map/ppermute | solution.py:387
